TPU v7x, 128 devices: a whole 4x4x4 slice. The times are simulated.
128 devices in a mesh: sy: 16 (over x_lo, y, core), sx: 8 (over x_hi, z).
Axes of the slice: x: 4 (x_hi: 2, x_lo: 2; x = x_hi * 2 + x_lo), y: 4, z: 4, core: 2. Of those that a mesh axis runs over, the one named last changes fastest.
Arguments:
- spectrum: bfloat16 [2, 18432, 18432], P(None, 'sy', 'sx'), may hold values from -6 to 6
- pupils: bfloat16 [2, 4096, 4096], P(None, 'sy', 'sx'), may hold values from -6 to 6
- amplitudes: float32 [16, 16, 4, 256, 256], P('sy', 'sx'), may hold values from 0.2 to 2
- crop_starts: int32 [16, 16, 4, 2], P('sy', 'sx'), may hold values from 0 to 896
- led_counts: int32 [16, 16], P('sy', 'sx'), may hold values from 1 to 4, as said below
Outputs:
- spectrum_grad: bfloat16 [2, 18432, 18432], P(None, 'sy', 'sx')
- pupil_grad: float32 [2, 4096, 4096], P(None, 'sy', 'sx')
Inputs may be any that keep to these rules, and one draw needn't show every extreme that they name: `led_counts`: slots at or past a segment's count are ignored.
All inputs are finite; a program needn't handle non-finite values.
Results may differ from a plain program's by a relative error of at most 0.001.
Values may be sent and summed in bfloat16 or wider, within the bound.
No kernel may reach another device: no remote copies, remote signals or barrier semaphores. Data moves between devices by JAX's collectives and lax.ppermute only.
A program may use at most 256 MiB of HBM per device.

v0:
```python
import functools
import math

import jax
import jax.numpy as jnp
import ml_dtypes
import numpy as np
from jax import lax
from jax.experimental import pallas as pl
from jax.experimental.pallas import tpu as pltpu
from jax.sharding import PartitionSpec as P

H = 64
MAXL = 4
W = 256
HALF = 128
FLOOR_SQUARE = 0.0625
BAND = 2 * H
BF = jnp.bfloat16
F32 = jnp.float32


def halves(table):
    high = table.astype(ml_dtypes.bfloat16)
    low = (table - high.astype(np.float64)).astype(ml_dtypes.bfloat16)
    return high, low


def tables():
    m = np.arange(HALF)[:, None]
    j = np.arange(HALF)[None, :]
    out = []
    for parity in (0, 1):
        phase = ((2 * m + parity) * j % W) * (2.0 * math.pi / W)
        re = np.cos(phase) / math.sqrt(W)
        im = np.sin(phase) / math.sqrt(W)
        left = np.block([[re, -im], [im, re]])
        out.append(left)
        out.append(left.T)
    packed = np.stack([np.stack(halves(t)) for t in out])
    spread = np.zeros((W, W))
    for p in (0, 1):
        for q in range(HALF):
            spread[2 * q + p, p * HALF + q] = 1.0
    return packed, spread.astype(ml_dtypes.bfloat16)


def split(value):
    high = value.astype(BF)
    low = (value - high.astype(F32)).astype(BF)
    return high, low


def dot(a, b):
    return jnp.dot(a, b, preferred_element_type=F32)


def compute_kernel(
    starts, counts, weights, spec_hbm, pup_hbm, amp_hbm, tab_hbm, spread_hbm,
    out_hbm, prow_hbm, pcol_hbm, ppup_hbm,
    spec, pupb, pup, amp, tab, spread, acc, pacc, inner,
    win, prs, xh, xl, ya, yb, ampq, sem_in, sem_out,
):
    edge = spec.shape[2]
    tiles = edge // 128
    low_row, high_row = BAND, edge - BAND
    mid = high_row - low_row
    copies = []
    for g in range(2):
        copies.append(pltpu.make_async_copy(spec_hbm.at[:, :, pl.ds(g * edge, edge)], spec.at[g], sem_in.at[g]))
    copies.append(pltpu.make_async_copy(pup_hbm, pupb, sem_in.at[2]))
    copies.append(pltpu.make_async_copy(tab_hbm, tab, sem_in.at[3]))
    copies.append(pltpu.make_async_copy(spread_hbm, spread, sem_in.at[4]))
    for h in range(2):
        copies.append(pltpu.make_async_copy(amp_hbm.at[0, :, :, :, pl.ds(h * 128, 128)], amp.at[:, :, h], sem_in.at[5 + h]))
    for c in copies:
        c.start()

    zero = jnp.zeros((128, 128), F32)

    def clear(i, carry):
        for g in range(2):
            for c in range(2):
                for k in range(tiles):
                    acc[g, c, k, pl.ds(pl.multiple_of(i * 32, 32), 32), :] = zero[:32]
        return carry

    lax.fori_loop(0, edge // 32, clear, 0)
    for c in copies[2:]:
        c.wait()
    for g in range(2):
        for c in range(2):
            pup[g, c] = pupb[c, :, pl.ds(g * W, W)].astype(F32)
            pacc[g, c] = jnp.zeros((W, W), F32)
    copies[0].wait()
    copies[1].wait()
    lane = lax.broadcasted_iota(jnp.int32, (16, 128), 1)

    def slot_step(g, slot):
        a = starts[(g * MAXL + slot) * 2]
        b = starts[(g * MAXL + slot) * 2 + 1]
        a0 = pl.multiple_of(jnp.minimum(a // 16 * 16, edge - W - 16), 16)
        off = a - a0
        k0 = jnp.minimum(b // 128, tiles - 3)
        s = b - k0 * 128
        sr = lax.rem(s, 128)
        back_shift = lax.rem(128 - sr, 128)
        from_first = lane >= s
        keep_low = lane < 128 - s
        col0 = pl.multiple_of(k0 * 128, 128)
        for c in range(2):
            for r in range(0, W + 16, 16):
                block = spec[g, c, pl.ds(a0 + r, 16), pl.ds(col0, 384)].astype(F32)
                for i in range(3):
                    win[c, i, pl.ds(r, 16), :] = block[:, i * 128 : (i + 1) * 128]
        for c in range(2):
            for r in range(0, W, 16):
                r0 = pltpu.roll(pup[g, c, pl.ds(r, 16), pl.ds(0, 128)], sr, 1)
                r1 = pltpu.roll(pup[g, c, pl.ds(r, 16), pl.ds(128, 128)], sr, 1)
                prs[c, 0, pl.ds(r, 16), :] = jnp.where(from_first, r0, r1)
                prs[c, 1, pl.ds(r, 16), :] = jnp.where(from_first, r1, r0)

        def crop(c, h, r):
            if h == 1:
                return win[c, 1, pl.ds(off + r, 16), :]
            return jnp.where(from_first, win[c, 0, pl.ds(off + r, 16), :], win[c, 2, pl.ds(off + r, 16), :])

        for p in range(2):
            for h in range(2):
                rows = amp[g, slot, h, pl.ds(p, 128, stride=2), :]
                hi, lo = split(rows)
                xh[0, pl.ds(p * 128, 128), pl.ds(h * 128, 128)] = hi
                xl[0, pl.ds(p * 128, 128), pl.ds(h * 128, 128)] = lo
        ampq[...] = dot(xh[0], spread[...]) + dot(xl[0], spread[...])

        for r in range(0, HALF, 16):
            for h in range(2):
                parts = []
                for rr in (r, r + HALF):
                    cr = crop(0, h, rr)
                    ci = crop(1, h, rr)
                    pr = prs[0, h, pl.ds(rr, 16), :]
                    pi = prs[1, h, pl.ds(rr, 16), :]
                    parts.append((pr * cr - pi * ci, pr * ci + pi * cr))
                for c in range(2):
                    for q in range(2):
                        v = parts[0][c] + parts[1][c] if q == 0 else parts[0][c] - parts[1][c]
                        hi, lo = split(v)
                        xh[q, pl.ds(c * HALF + r, 16), pl.ds(h * 128, 128)] = hi
                        xl[q, pl.ds(c * HALF + r, 16), pl.ds(h * 128, 128)] = lo
        for q in range(2):
            th, tl = tab[2 * q, 0], tab[2 * q, 1]
            ya[q] = dot(th, xh[q]) + dot(th, xl[q]) + dot(tl, xh[q])
        for q in range(2):
            for r in range(0, HALF, 16):
                for c in range(2):
                    y0 = ya[q, pl.ds(c * HALF + r, 16), pl.ds(0, 128)]
                    y1 = ya[q, pl.ds(c * HALF + r, 16), pl.ds(128, 128)]
                    for u in range(2):
                        hi, lo = split(y0 + y1 if u == 0 else y0 - y1)
                        xh[u, pl.ds(q * HALF + r, 16), pl.ds(c * 128, 128)] = hi
                        xl[u, pl.ds(q * HALF + r, 16), pl.ds(c * 128, 128)] = lo
        for u in range(2):
            th, tl = tab[2 * u + 1, 0], tab[2 * u + 1, 1]
            yb[u] = dot(xh[u], th) + dot(xl[u], th) + dot(xh[u], tl)
        for u in range(2):
            for r in range(0, W, 16):
                re = yb[u, pl.ds(r, 16), pl.ds(0, 128)]
                im = yb[u, pl.ds(r, 16), pl.ds(128, 128)]
                power = jnp.maximum(re * re + im * im, FLOOR_SQUARE)
                keeper = 1.0 - ampq[pl.ds(r, 16), pl.ds(u * 128, 128)] * lax.rsqrt(power)
                for c, v in enumerate((re, im)):
                    hi, lo = split(v * keeper)
                    xh[u, pl.ds(r, 16), pl.ds(c * 128, 128)] = hi
                    xl[u, pl.ds(r, 16), pl.ds(c * 128, 128)] = lo
        for u in range(2):
            th, tl = tab[2 * u, 0], tab[2 * u, 1]
            ya[u] = dot(xh[u], th) + dot(xl[u], th) + dot(xh[u], tl)
        for q in range(2):
            for r in range(0, HALF, 16):
                for c in range(2):
                    e = ya[0, pl.ds(q * HALF + r, 16), pl.ds(c * 128, 128)]
                    o = ya[1, pl.ds(q * HALF + r, 16), pl.ds(c * 128, 128)]
                    for h in range(2):
                        hi, lo = split(e + o if h == 0 else e - o)
                        xh[q, pl.ds(c * HALF + r, 16), pl.ds(h * 128, 128)] = hi
                        xl[q, pl.ds(c * HALF + r, 16), pl.ds(h * 128, 128)] = lo
        for q in range(2):
            th, tl = tab[2 * q + 1, 0], tab[2 * q + 1, 1]
            yb[q] = dot(th, xh[q]) + dot(th, xl[q]) + dot(tl, xh[q])
        for r in range(0, HALF, 16):
            for rr in (r, r + HALF):
                back = []
                for c in range(2):
                    row = []
                    for h in range(2):
                        e = yb[0, pl.ds(c * HALF + r, 16), pl.ds(h * 128, 128)]
                        o = yb[1, pl.ds(c * HALF + r, 16), pl.ds(h * 128, 128)]
                        row.append(e + o if rr == r else e - o)
                    back.append(row)
                terms = []
                for h in range(2):
                    br, bi = back[0][h], back[1][h]
                    pr = prs[0, h, pl.ds(rr, 16), :]
                    pi = prs[1, h, pl.ds(rr, 16), :]
                    cr = crop(0, h, rr)
                    ci = crop(1, h, rr)
                    drop = (pr * br + pi * bi, pr * bi - pi * br)
                    terms.append((cr * br + ci * bi, cr * bi - ci * br))
                    rows = pl.ds(a + rr, 16)
                    for c in range(2):
                        if h == 1:
                            acc[g, c, k0 + 1, rows, :] += drop[c]
                        else:
                            acc[g, c, k0, rows, :] += jnp.where(from_first, drop[c], 0.0)
                            acc[g, c, k0 + 2, rows, :] += jnp.where(from_first, 0.0, drop[c])
                for c in range(2):
                    t0 = pltpu.roll(terms[0][c], back_shift, 1)
                    t1 = pltpu.roll(terms[1][c], back_shift, 1)
                    pacc[g, c, pl.ds(rr, 16), pl.ds(0, 128)] += jnp.where(keep_low, t0, t1)
                    pacc[g, c, pl.ds(rr, 16), pl.ds(128, 128)] += jnp.where(keep_low, t1, t0)

    up, down, left_out, right_out = weights[0], weights[1], weights[2], weights[3]
    pending = []

    def put(src, dst):
        copy = pltpu.make_async_copy(src, dst, sem_out.at[len(pending)])
        copy.start()
        pending.append(copy)

    for g in range(2):

        def step(slot, carry, g=g):
            slot_step(g, slot)
            return carry

        lax.fori_loop(0, counts[g], step, 0)
        left = left_out if g == 0 else F32(1.0)
        right = right_out if g == 1 else F32(1.0)
        neighbours = up + down + left + right
        for c in range(2):
            pacc[g, c] = pacc[g, c] + 0.5 * (neighbours * pup[g, c] - pup[1 - g, c])
            put(pacc.at[g, c], ppup_hbm.at[c, :, pl.ds(g * W, W)])
        for c in range(2):
            for k in range(tiles):
                side = left if k == 0 else right if k == tiles - 1 else None
                local = (k == 0 and g == 1) or (k == tiles - 1 and g == 0)
                for t, (first, vert) in enumerate(((0, up), (high_row, down))):
                    factor = vert if side is None else (1.0 + vert) * (1.0 + side) - 1.0
                    own = spec[g, c, pl.ds(first, BAND), pl.ds(k * 128, 128)].astype(F32)
                    add = (0.5 * factor) * own
                    if local:
                        other = spec[1 - g, c, pl.ds(first, BAND), pl.ds((tiles - 1 - k) * 128, 128)].astype(F32)
                        add = add - 0.5 * other
                    acc[g, c, k, pl.ds(first, BAND), :] += add
            for t, first in enumerate((0, high_row)):
                put(acc.at[g, c, :, pl.ds(first, BAND), :], prow_hbm.at[t, c, pl.ds(g * tiles, tiles)])
        k_out = 0 if g == 0 else tiles - 1
        w_out = left_out if g == 0 else right_out
        for c in range(2):

            def outer(i, carry, c=c):
                rows = pl.ds(pl.multiple_of(low_row + i * 128, 128), 128)
                acc[g, c, k_out, rows, :] += (0.5 * w_out) * spec[g, c, rows, pl.ds(k_out * 128, 128)].astype(F32)
                return carry

            lax.fori_loop(0, mid // 128, outer, 0)
            put(acc.at[g, c, k_out, pl.ds(low_row, mid), :], pcol_hbm.at[g, c])
        k_in = tiles - 1 if g == 0 else 0
        first_tile = 1 if g == 0 else 0
        for c in range(2):

            def finish(i, carry, c=c):
                rows = pl.ds(pl.multiple_of(low_row + i * 64, 64), 64)
                dst = pl.ds(pl.multiple_of(i * 64, 64), 64)
                for k in range(first_tile, first_tile + tiles - 1):
                    v = acc[g, c, k, rows, :]
                    if k == k_in:
                        own = spec[g, c, rows, pl.ds(k * 128, 128)].astype(F32)
                        other = spec[1 - g, c, rows, pl.ds((tiles - 1 - k) * 128, 128)].astype(F32)
                        v = v + 0.5 * (own - other)
                    inner[g, c, dst, pl.ds((k - first_tile) * 128, 128)] = v.astype(BF)
                return carry

            lax.fori_loop(0, mid // 64, finish, 0)
            put(
                inner.at[g, c],
                out_hbm.at[c, pl.ds(low_row, mid), pl.ds((g * tiles + first_tile) * 128, (tiles - 1) * 128)],
            )
    for copy in pending:
        copy.wait()


def compute(spectrum, pupils, amplitudes, starts, counts, weights):
    edge = spectrum.shape[1]
    tiles = edge // 128
    mid = edge - 2 * BAND
    packed, spread = tables()
    hbm = pl.BlockSpec(memory_space=pl.ANY)
    smem = pl.BlockSpec(memory_space=pltpu.SMEM)
    return pl.pallas_call(
        compute_kernel,
        out_shape=(
            jax.ShapeDtypeStruct(spectrum.shape, BF),
            jax.ShapeDtypeStruct((2, 2, 2 * tiles, BAND, 128), F32),
            jax.ShapeDtypeStruct((2, 2, mid, 128), F32),
            jax.ShapeDtypeStruct(pupils.shape, F32),
        ),
        in_specs=[smem, smem, smem, hbm, hbm, hbm, hbm, hbm],
        out_specs=(hbm, hbm, hbm, hbm),
        scratch_shapes=[
            pltpu.VMEM((2, 2, edge, edge), BF),
            pltpu.VMEM((2, W, 2 * W), BF),
            pltpu.VMEM((2, 2, W, W), F32),
            pltpu.VMEM((2, MAXL, 2, W, 128), F32),
            pltpu.VMEM((4, 2, W, W), BF),
            pltpu.VMEM((W, W), BF),
            pltpu.VMEM((2, 2, tiles, edge, 128), F32),
            pltpu.VMEM((2, 2, W, W), F32),
            pltpu.VMEM((2, 2, mid, (tiles - 1) * 128), BF),
            pltpu.VMEM((2, 3, W + 16, 128), F32),
            pltpu.VMEM((2, 2, W, 128), F32),
            pltpu.VMEM((2, W, W), BF),
            pltpu.VMEM((2, W, W), BF),
            pltpu.VMEM((2, W, W), F32),
            pltpu.VMEM((2, W, W), F32),
            pltpu.VMEM((W, W), F32),
            pltpu.SemaphoreType.DMA((7,)),
            pltpu.SemaphoreType.DMA((20,)),
        ],
        compiler_params=pltpu.CompilerParams(vmem_limit_bytes=52 * 1024 * 1024),
        cost_estimate=pl.CostEstimate(flops=20_000_000_000, bytes_accessed=30_000_000, transcendentals=0),
        name="data_terms",
    )(starts, counts, weights, spectrum, pupils, amplitudes, jnp.asarray(packed), jnp.asarray(spread))


def finish_kernel(
    out_in, prow_hbm, pcol_hbm, ppup_hbm, up_hbm, down_hbm, left_hbm, right_hbm, ul_hbm, ur_hbm, dl_hbm, dr_hbm,
    out_hbm, pup_hbm,
    prow, pcol, ppup, vert, side, diag, rows_out, cols_out, pup_out, sem_in, sem_out,
):
    edge = out_in.shape[1]
    tiles = edge // 128
    mid = edge - 2 * BAND
    high_row = edge - BAND
    last = 2 * tiles - 1
    ins = {}

    def get(name, src, dst):
        copy = pltpu.make_async_copy(src, dst, sem_in.at[len(ins)])
        copy.start()
        ins[name] = copy

    verts = (up_hbm, down_hbm)
    sides = (left_hbm, right_hbm)
    diags = ((ul_hbm, ur_hbm), (dl_hbm, dr_hbm))
    for d in range(2):
        get(("side", d), sides[d], side.at[d])
    for t in range(2):
        get(("vert", t), verts[t], vert.at[t])
        for d in range(2):
            get(("diag", t, d), diags[t][d], diag.at[t, d])
        get(("prow", t), prow_hbm.at[t], prow.at[t])
    for d in range(2):
        get(("pcol", d), pcol_hbm.at[d], pcol.at[d])
    get("ppup", ppup_hbm, ppup)
    outs = []

    def put(src, dst):
        copy = pltpu.make_async_copy(src, dst, sem_out.at[len(outs)])
        copy.start()
        outs.append(copy)

    ins["side", 0].wait()
    ins["side", 1].wait()
    for t in range(2):
        ins["vert", t].wait()
        ins["diag", t, 0].wait()
        ins["diag", t, 1].wait()
        ins["prow", t].wait()
        first = t * high_row
        for c in range(2):
            for k in range(2 * tiles):
                sub = vert[t, c, :, pl.ds(k * 128, 128)].astype(F32)
                if k == tiles - 1 or k == tiles:
                    sub = sub + vert[t, c, :, pl.ds((2 * tiles - 1 - k) * 128, 128)].astype(F32)
                if k == 0 or k == last:
                    d = 0 if k == 0 else 1
                    sub = sub + (diag[t, d, c].astype(F32) + side[d, c, pl.ds(first, BAND), :].astype(F32))
                rows_out[t, c, :, pl.ds(k * 128, 128)] = (prow[t, c, k] - 0.5 * sub).astype(BF)
            put(rows_out.at[t, c], out_hbm.at[c, pl.ds(first, BAND), :])
    for d in range(2):
        ins["pcol", d].wait()
        for c in range(2):
            sub = side[d, c, pl.ds(BAND, mid), :].astype(F32)
            cols_out[d, c] = (pcol[d, c] - 0.5 * sub).astype(BF)
            put(cols_out.at[d, c], out_hbm.at[c, pl.ds(BAND, mid), pl.ds(d * last * 128, 128)])
    ins["ppup"].wait()
    for c in range(2):
        for half in range(2):
            rows = pl.ds(half * 128, 128)
            for q in range(4):
                cols = pl.ds(q * 128, 128)
                d = q // 2
                sub = side[d, c, pl.ds(edge + (q % 2) * W + half * 128, 128), :].astype(F32)
                for t in range(2):
                    sub = sub + vert[t, c, :, pl.ds(2 * edge + half * 512 + q * 128, 128)].astype(F32)
                pup_out[c, rows, cols] = ppup[c, rows, cols] - 0.5 * sub
    put(pup_out, pup_hbm)
    for copy in outs:
        copy.wait()


def finish(out, prow, pcol, ppup, ups, sides, diags):
    edge = out.shape[1]
    tiles = edge // 128
    mid = edge - 2 * BAND
    hbm = pl.BlockSpec(memory_space=pl.ANY)
    return pl.pallas_call(
        finish_kernel,
        out_shape=(
            jax.ShapeDtypeStruct(out.shape, BF),
            jax.ShapeDtypeStruct(ppup.shape, F32),
        ),
        in_specs=[hbm] * 12,
        out_specs=(hbm, hbm),
        input_output_aliases={0: 0},
        scratch_shapes=[
            pltpu.VMEM(prow.shape, F32),
            pltpu.VMEM(pcol.shape, F32),
            pltpu.VMEM(ppup.shape, F32),
            pltpu.VMEM((2,) + ups[0].shape, BF),
            pltpu.VMEM((2,) + sides[0].shape, BF),
            pltpu.VMEM((2, 2) + diags[0].shape, BF),
            pltpu.VMEM((2, 2, BAND, 2 * edge), BF),
            pltpu.VMEM((2, 2, mid, 128), BF),
            pltpu.VMEM(ppup.shape, F32),
            pltpu.SemaphoreType.DMA((16,)),
            pltpu.SemaphoreType.DMA((9,)),
        ],
        compiler_params=pltpu.CompilerParams(vmem_limit_bytes=32 * 1024 * 1024),
        cost_estimate=pl.CostEstimate(flops=10_000_000, bytes_accessed=17_000_000, transcendentals=0),
        name="shared_bands",
    )(out, prow, pcol, ppup, *ups, *sides, *diags)


def local(spectrum, pupils, amplitudes, crop_starts, led_counts):
    edge = spectrum.shape[1]
    wide = spectrum.shape[2]
    rows = lax.axis_size("sy")
    cols = lax.axis_size("sx")
    row = lax.axis_index("sy")
    col = lax.axis_index("sx")

    def chain(count, step):
        return [(i, i + step) for i in range(count) if 0 <= i + step < count]

    def corner(dy, dx):
        return [
            (y * cols + x, (y + dy) * cols + x + dx)
            for y in range(rows)
            for x in range(cols)
            if 0 <= y + dy < rows and 0 <= x + dx < cols
        ]

    def side_pack(first, half):
        band = spectrum[:, :, first : first + BAND]
        tile = pupils[:, :, half * W : (half + 1) * W]
        return jnp.concatenate([band, tile[:, :, :128], tile[:, :, 128:]], axis=1)

    def vert_pack(first):
        band = spectrum[:, first : first + BAND, :]
        return jnp.concatenate([band, pupils[:, :128, :], pupils[:, 128:, :]], axis=2)

    from_left = lax.ppermute(side_pack(wide - BAND, 1), "sx", chain(cols, 1))
    from_right = lax.ppermute(side_pack(0, 0), "sx", chain(cols, -1))
    from_up = lax.ppermute(vert_pack(edge - BAND), "sy", chain(rows, 1))
    from_down = lax.ppermute(vert_pack(0), "sy", chain(rows, -1))
    diags = []
    for dy in (-1, 1):
        for dx in (-1, 1):
            y0 = edge - BAND if dy < 0 else 0
            x0 = wide - BAND if dx < 0 else 0
            piece = spectrum[:, y0 : y0 + BAND, x0 : x0 + BAND]
            diags.append(lax.ppermute(piece, ("sy", "sx"), corner(-dy, -dx)))
    weights = jnp.stack([row > 0, row < rows - 1, col > 0, col < cols - 1]).astype(F32)
    out, prow, pcol, ppup = compute(
        spectrum, pupils, amplitudes, crop_starts.reshape(-1), led_counts.reshape(-1), weights
    )
    return finish(out, prow, pcol, ppup, (from_up, from_down), (from_left, from_right), diags)


def solution(mesh):
    placed = (
        P(None, "sy", "sx"),
        P(None, "sy", "sx"),
        P("sy", "sx", None, None, None),
        P("sy", "sx", None, None),
        P("sy", "sx"),
    )
    return jax.shard_map(
        local,
        mesh=mesh,
        in_specs=placed,
        out_specs=(P(None, "sy", "sx"), P(None, "sy", "sx")),
        check_vma=False,
    )
```

profile of v0, /device:TPU:6, one launch (start us, length us, event | category | flops | bytes accessed | tf_op | source)
XLA Modules:
  0.0 86.9 jit_solution(11701048520877284263)
XLA Ops:
  0.6 1.7 %fusion = (bf16[2,128,128]{2,1,0:T(8,128)(2,1)}, bf16[2,128,128]{2,1,0:T(8,128)(2,1)}, bf16[2,128,128]{2,1,0:T(8,128)(2,1)}, bf16[2,128,128]{2,1,0:T(8,128)(2,1)}) fusion(bf16[2,1152,2304]{2,1,0:T(8,128)(2,1)} %spec_hbm.1), kind=kLoop, calls=%fused_computation.7 | loop fusion | bytes 524288 | tf_op jit(solution)/shard_map/slice | solution.py:484
  2.4 7.7 %collective-permute-start.7 = (bf16[2,128,128]{2,1,0:T(8,128)(2,1)}, bf16[2,128,128]{2,1,0:T(8,128)(2,1)S(1)}, u32[]{:S(2)}, u32[]{:S(2)}) collective-permute-start(bf16[2,128,128]{2,1,0:T(8,128)(2,1)} %get-tuple-element.10), channel_id=1, source_target_pairs={{9,0},{10,1},{11,2},{12,3},{13,4},{14,5},{15,6},{17,8},{18,9},{19,... | collective-permute-start | bytes 196616 | tf_op jit(solution)/shard_map/ppermute | solution.py:485
  10.1 1.9 %collective-permute-start.5 = (bf16[2,128,128]{2,1,0:T(8,128)(2,1)}, bf16[2,128,128]{2,1,0:T(8,128)(2,1)S(1)}, u32[]{:S(2)}, u32[]{:S(2)}) collective-permute-start(bf16[2,128,128]{2,1,0:T(8,128)(2,1)} %get-tuple-element.11), channel_id=1, source_target_pairs={{1,8},{2,9},{3,10},{4,11},{5,12},{6,13},{7,14},{9,16},{10,17},{11,... | collective-permute-start | bytes 196616 | tf_op jit(solution)/shard_map/ppermute | solution.py:485
  12.0 3.0 %collective-permute-start.4 = (bf16[2,128,128]{2,1,0:T(8,128)(2,1)}, bf16[2,128,128]{2,1,0:T(8,128)(2,1)S(1)}, u32[]{:S(2)}, u32[]{:S(2)}) collective-permute-start(bf16[2,128,128]{2,1,0:T(8,128)(2,1)} %get-tuple-element.12), channel_id=1, source_target_pairs={{0,9},{1,10},{2,11},{3,12},{4,13},{5,14},{6,15},{8,17},{9,18},{10,... | collective-permute-start | bytes 196616 | tf_op jit(solution)/shard_map/ppermute | solution.py:485
  15.1 5.6 %collective-permute-start.6 = (bf16[2,128,128]{2,1,0:T(8,128)(2,1)}, bf16[2,128,128]{2,1,0:T(8,128)(2,1)S(1)}, u32[]{:S(2)}, u32[]{:S(2)}) collective-permute-start(bf16[2,128,128]{2,1,0:T(8,128)(2,1)} %get-tuple-element.13), channel_id=1, source_target_pairs={{8,1},{9,2},{10,3},{11,4},{12,5},{13,6},{14,7},{16,9},{17,10},{18,... | collective-permute-start | bytes 196616 | tf_op jit(solution)/shard_map/ppermute | solution.py:485
  20.6 1.3 %fusion.1 = (bf16[2,1152,128]{2,1,0:T(8,128)(2,1)S(1)}, bf16[2,1152,128]{2,1,0:T(8,128)(2,1)S(1)}) fusion(bf16[2,1152,2304]{2,1,0:T(8,128)(2,1)} %spec_hbm.1), kind=kLoop, calls=%fused_computation.8 | loop fusion | bytes 2359296 | tf_op jit(solution)/shard_map/slice | solution.py:467
  22.0 0.8 fusion.3
  22.7 1.0 %pad_maximum_fusion.4 = bf16[2,1664,128]{2,1,0:T(8,128)(2,1)} fusion(bf16[2,256,128]{2,1,0:T(8,128)(2,1)S(1)} %get-tuple-element.19, bf16[2,256,128]{2,1,0:T(8,128)(2,1)S(1)} %get-tuple-element.20, bf16[2,1152,128]{2,1,0:T(8,128)(2,1)S(1)} %get-tuple-element.15), kind=kLoop, calls=%fused_computation.4 | loop fusion | flops 2555904 | bytes 1703936 | tf_op jit(solution)/shard_map/concatenate | solution.py:469
  23.7 1.9 %collective-permute-start.2 = (bf16[2,1664,128]{2,1,0:T(8,128)(2,1)}, bf16[2,1664,128]{2,1,0:T(8,128)(2,1)S(1)}, u32[]{:S(2)}, u32[]{:S(2)}) collective-permute-start(bf16[2,1664,128]{2,1,0:T(8,128)(2,1)} %pad_maximum_fusion.4), channel_id=1, source_target_pairs={{0,1},{1,2},{2,3},{3,4},{4,5},{5,6},{6,7},{8,9},{9,10},{10,11},{11... | collective-permute-start | bytes 2555912 | tf_op jit(solution)/shard_map/ppermute | solution.py:475
  25.6 0.8 fusion.4
  26.4 2.8 %fusion.2 = (bf16[2,128,2304]{2,1,0:T(8,128)(2,1)S(1)}, bf16[2,128,2304]{2,1,0:T(8,128)(2,1)}) fusion(bf16[2,1152,2304]{2,1,0:T(8,128)(2,1)} %spec_hbm.1), kind=kLoop, calls=%fused_computation.9 | loop fusion | bytes 4718592 | tf_op jit(solution)/shard_map/slice | solution.py:472
  29.3 0.1 copy.11
  29.3 0.1 reshape.10.starts
  29.5 2.1 %pad_maximum_fusion.5 = bf16[2,1664,128]{2,1,0:T(8,128)(2,1)} fusion(bf16[2,256,128]{2,1,0:T(8,128)(2,1)} %get-tuple-element.21, bf16[2,256,128]{2,1,0:T(8,128)(2,1)S(1)} %get-tuple-element.18, bf16[2,1152,128]{2,1,0:T(8,128)(2,1)S(1)} %get-tuple-element.14), kind=kLoop, calls=%fused_computation.5 | loop fusion | flops 2555904 | bytes 1703936 | tf_op jit(solution)/shard_map/concatenate | solution.py:469
  31.6 1.5 %pad_maximum_fusion = (bf16[2,128,3328]{2,1,0:T(8,128)(2,1)}, bf16[2,128,3328]{2,1,0:T(8,128)(2,1)S(1)}) fusion(bf16[2,128,512]{2,1,0:T(8,128)(2,1)S(1)} %copy-done.7, bf16[2,128,512]{2,1,0:T(8,128)(2,1)S(1)} %copy-done.6, bf16[2,128,2304]{2,1,0:T(8,128)(2,1)S(1)} %get-tuple-element.16, bf16[2,128,2304]{2,1,0:T(8,128)(2,1)S(1)} %copy-done.5), kind=kLoop, calls=%fused_computation | loop fusion | flops 8519680 | bytes 6291456 | tf_op jit(solution)/shard_map/concatenate | solution.py:473
  33.1 7.5 %collective-permute-start.3 = (bf16[2,1664,128]{2,1,0:T(8,128)(2,1)}, bf16[2,1664,128]{2,1,0:T(8,128)(2,1)S(1)}, u32[]{:S(2)}, u32[]{:S(2)}) collective-permute-start(bf16[2,1664,128]{2,1,0:T(8,128)(2,1)} %pad_maximum_fusion.5), channel_id=1, source_target_pairs={{1,0},{2,1},{3,2},{4,3},{5,4},{6,5},{7,6},{9,8},{10,9},{11,10},{12... | collective-permute-start | bytes 2555912 | tf_op jit(solution)/shard_map/ppermute | solution.py:476
  40.7 1.9 %collective-permute-start.1 = (bf16[2,128,3328]{2,1,0:T(8,128)(2,1)}, bf16[2,128,3328]{2,1,0:T(8,128)(2,1)S(1)}, u32[]{:S(2)}, u32[]{:S(2)}) collective-permute-start(bf16[2,128,3328]{2,1,0:T(8,128)(2,1)} %get-tuple-element.22), channel_id=1, source_target_pairs={{8,0},{16,8},{24,16},{32,24},{40,32},{48,40},{56,48},{64,56},{72,6... | collective-permute-start | bytes 5111816 | tf_op jit(solution)/shard_map/ppermute | solution.py:478
  42.6 2.4 %collective-permute-start = (bf16[2,128,3328]{2,1,0:T(8,128)(2,1)S(1)}, bf16[2,128,3328]{2,1,0:T(8,128)(2,1)S(1)}, u32[]{:S(2)}, u32[]{:S(2)}) collective-permute-start(bf16[2,128,3328]{2,1,0:T(8,128)(2,1)S(1)} %get-tuple-element.23), channel_id=1, source_target_pairs={{0,8},{8,16},{16,24},{24,32},{32,40},{40,48},{48,56},{56,64},{64,7... | collective-permute-start | bytes 5111816 | tf_op jit(solution)/shard_map/ppermute | solution.py:477
  45.0 14.9 %data_terms.1 = (bf16[2,1152,2304]{2,1,0:T(8,128)(2,1)}, f32[2,2,18,128,128]{4,3,2,1,0:T(8,128)}, f32[2,2,896,128]{3,2,1,0:T(8,128)}, f32[2,256,512]{2,1,0:T(8,128)S(1)}) custom-call(s32[16]{0:T(128)S(1)} %reshape.10.starts, s32[2]{0:T(128)S(1)} %bitcast.5, f32[4]{0:T(128)S(1)} %add_convert_fusion.weights, bf16[2,1152,2304]{2,1,0:T(8,128)(2,1)} %spec_hbm.1, ...), custom_call_target="tpu_custom_call" | custom-call | flops 20000000000 | bytes 30000000 | tf_op jit(solution)/shard_map/data_terms/pallas_call | solution.py:301
  60.0 14.5 %collective-permute-done.1.down_hbm = bf16[2,128,3328]{2,1,0:T(8,128)(2,1)S(1)} collective-permute-done((bf16[2,128,3328]{2,1,0:T(8,128)(2,1)}, bf16[2,128,3328]{2,1,0:T(8,128)(2,1)S(1)}, u32[]{:S(2)}, u32[]{:S(2)}) %collective-permute-start.1) | collective-permute-done | bytes 1703968 | tf_op jit(solution)/shard_map/ppermute | solution.py:478
  74.5 4.2 %collective-permute-done.up_hbm = bf16[2,128,3328]{2,1,0:T(8,128)(2,1)S(1)} collective-permute-done((bf16[2,128,3328]{2,1,0:T(8,128)(2,1)S(1)}, bf16[2,128,3328]{2,1,0:T(8,128)(2,1)S(1)}, u32[]{:S(2)}, u32[]{:S(2)}) %collective-permute-start) | collective-permute-done | bytes 1703968 | tf_op jit(solution)/shard_map/ppermute | solution.py:477
  78.6 2.3 %copy-done = f32[2,2,18,128,128]{4,3,2,1,0:T(8,128)S(1)} copy-done((f32[2,2,18,128,128]{4,3,2,1,0:T(8,128)S(1)}, f32[2,2,18,128,128]{4,3,2,1,0:T(8,128)}, u32[]{:S(2)}) %copy-start) | copy-done | bytes 4718616
  81.0 1.5 %copy-done.2 = f32[2,2,896,128]{3,2,1,0:T(8,128)S(1)} copy-done((f32[2,2,896,128]{3,2,1,0:T(8,128)S(1)}, f32[2,2,896,128]{3,2,1,0:T(8,128)}, u32[]{:S(2)}) %copy-start.2) | copy-done | bytes 1835032
  82.4 4.4 %shared_bands.1 = (bf16[2,1152,2304]{2,1,0:T(8,128)(2,1)}, f32[2,256,512]{2,1,0:T(8,128)}) custom-call(bf16[2,1152,2304]{2,1,0:T(8,128)(2,1)} %get-tuple-element.6.out_in, f32[2,2,18,128,128]{4,3,2,1,0:T(8,128)S(1)} %copy-done, f32[2,2,896,128]{3,2,1,0:T(8,128)S(1)} %copy-done.2, ...), custom_call_target="tpu_custom_call", output_to_operand_aliasing={{0}: (0, {})} | custom-call | flops 10000000 | bytes 17000000 | tf_op jit(solution)/shard_map/shared_bands/pallas_call | solution.py:419
  (23 shorter events, 0.1 us)
Async XLA Ops:
  0.6 21.3 %copy-start.1 = (bf16[2,256,512]{2,1,0:T(8,128)(2,1)S(1)}, bf16[2,256,512]{2,1,0:T(8,128)(2,1)}, u32[]{:S(2)}) copy-start(bf16[2,256,512]{2,1,0:T(8,128)(2,1)} %pup_hbm.1) | copy-start | bytes 1572868
  2.4 30.8 %collective-permute-start.7 = (bf16[2,128,128]{2,1,0:T(8,128)(2,1)}, bf16[2,128,128]{2,1,0:T(8,128)(2,1)S(1)}, u32[]{:S(2)}, u32[]{:S(2)}) collective-permute-start(bf16[2,128,128]{2,1,0:T(8,128)(2,1)} %get-tuple-element.10), channel_id=1, source_target_pairs={{9,0},{10,1},{11,2},{12,3},{13,4},{14,5},{15,6},{17,8},{18,9},{19,... | collective-permute-start | bytes 196616 | tf_op jit(solution)/shard_map/ppermute | solution.py:485
  10.1 30.6 %collective-permute-start.5 = (bf16[2,128,128]{2,1,0:T(8,128)(2,1)}, bf16[2,128,128]{2,1,0:T(8,128)(2,1)S(1)}, u32[]{:S(2)}, u32[]{:S(2)}) collective-permute-start(bf16[2,128,128]{2,1,0:T(8,128)(2,1)} %get-tuple-element.11), channel_id=1, source_target_pairs={{1,8},{2,9},{3,10},{4,11},{5,12},{6,13},{7,14},{9,16},{10,17},{11,... | collective-permute-start | bytes 196616 | tf_op jit(solution)/shard_map/ppermute | solution.py:485
  12.0 30.6 %collective-permute-start.4 = (bf16[2,128,128]{2,1,0:T(8,128)(2,1)}, bf16[2,128,128]{2,1,0:T(8,128)(2,1)S(1)}, u32[]{:S(2)}, u32[]{:S(2)}) collective-permute-start(bf16[2,128,128]{2,1,0:T(8,128)(2,1)} %get-tuple-element.12), channel_id=1, source_target_pairs={{0,9},{1,10},{2,11},{3,12},{4,13},{5,14},{6,15},{8,17},{9,18},{10,... | collective-permute-start | bytes 196616 | tf_op jit(solution)/shard_map/ppermute | solution.py:485
  15.1 44.9 %collective-permute-start.6 = (bf16[2,128,128]{2,1,0:T(8,128)(2,1)}, bf16[2,128,128]{2,1,0:T(8,128)(2,1)S(1)}, u32[]{:S(2)}, u32[]{:S(2)}) collective-permute-start(bf16[2,128,128]{2,1,0:T(8,128)(2,1)} %get-tuple-element.13), channel_id=1, source_target_pairs={{8,1},{9,2},{10,3},{11,4},{12,5},{13,6},{14,7},{16,9},{17,10},{18,... | collective-permute-start | bytes 196616 | tf_op jit(solution)/shard_map/ppermute | solution.py:485
  23.7 36.3 %collective-permute-start.2 = (bf16[2,1664,128]{2,1,0:T(8,128)(2,1)}, bf16[2,1664,128]{2,1,0:T(8,128)(2,1)S(1)}, u32[]{:S(2)}, u32[]{:S(2)}) collective-permute-start(bf16[2,1664,128]{2,1,0:T(8,128)(2,1)} %pad_maximum_fusion.4), channel_id=1, source_target_pairs={{0,1},{1,2},{2,3},{3,4},{4,5},{5,6},{6,7},{8,9},{9,10},{10,11},{11... | collective-permute-start | bytes 2555912 | tf_op jit(solution)/shard_map/ppermute | solution.py:475
  26.4 2.8 %copy-start.8 = (s32[1,2,4,2]{2,3,1,0:T(2,128)S(1)}, s32[1,2,4,2]{2,3,1,0:T(2,128)}, u32[]{:S(2)}) copy-start(s32[1,2,4,2]{2,3,1,0:T(2,128)} %param.10) | copy-start | bytes 196
  29.4 2.1 %copy-start.5 = (bf16[2,128,2304]{2,1,0:T(8,128)(2,1)S(1)}, bf16[2,128,2304]{2,1,0:T(8,128)(2,1)}, u32[]{:S(2)}) copy-start(bf16[2,128,2304]{2,1,0:T(8,128)(2,1)} %get-tuple-element.17) | copy-start | bytes 3538948
  29.4 2.1 %copy-start.6 = (bf16[2,128,512]{2,1,0:T(8,128)(2,1)S(1)}, bf16[2,128,512]{2,1,0:T(8,128)(2,1)}, u32[]{:S(2)}) copy-start(bf16[2,128,512]{2,1,0:T(8,128)(2,1)} %get-tuple-element.24) | copy-start | bytes 786436
  29.4 2.1 %copy-start.7 = (bf16[2,128,512]{2,1,0:T(8,128)(2,1)S(1)}, bf16[2,128,512]{2,1,0:T(8,128)(2,1)}, u32[]{:S(2)}) copy-start(bf16[2,128,512]{2,1,0:T(8,128)(2,1)} %get-tuple-element.25) | copy-start | bytes 786436
  31.5 13.5 %copy-start.3 = (s32[1,2]{1,0:T(1,128)S(1)}, s32[1,2]{1,0:T(1,128)}, u32[]{:S(2)}) copy-start(s32[1,2]{1,0:T(1,128)} %param.11) | copy-start | bytes 28
  31.6 13.5 %copy-start.4 = (bf16[256,256]{1,0:T(8,128)(2,1)S(1)}, bf16[256,256]{1,0:T(8,128)(2,1)}, u32[]{:S(2)}) copy-start(bf16[256,256]{1,0:T(8,128)(2,1)} %constant.20.clone.spread_hbm) | copy-start | bytes 393220
  33.1 26.8 %collective-permute-start.3 = (bf16[2,1664,128]{2,1,0:T(8,128)(2,1)}, bf16[2,1664,128]{2,1,0:T(8,128)(2,1)S(1)}, u32[]{:S(2)}, u32[]{:S(2)}) collective-permute-start(bf16[2,1664,128]{2,1,0:T(8,128)(2,1)} %pad_maximum_fusion.5), channel_id=1, source_target_pairs={{1,0},{2,1},{3,2},{4,3},{5,4},{6,5},{7,6},{9,8},{10,9},{11,10},{12... | collective-permute-start | bytes 2555912 | tf_op jit(solution)/shard_map/ppermute | solution.py:476
  40.7 33.8 %collective-permute-start.1 = (bf16[2,128,3328]{2,1,0:T(8,128)(2,1)}, bf16[2,128,3328]{2,1,0:T(8,128)(2,1)S(1)}, u32[]{:S(2)}, u32[]{:S(2)}) collective-permute-start(bf16[2,128,3328]{2,1,0:T(8,128)(2,1)} %get-tuple-element.22), channel_id=1, source_target_pairs={{8,0},{16,8},{24,16},{32,24},{40,32},{48,40},{56,48},{64,56},{72,6... | collective-permute-start | bytes 5111816 | tf_op jit(solution)/shard_map/ppermute | solution.py:478
  42.6 36.0 %collective-permute-start = (bf16[2,128,3328]{2,1,0:T(8,128)(2,1)S(1)}, bf16[2,128,3328]{2,1,0:T(8,128)(2,1)S(1)}, u32[]{:S(2)}, u32[]{:S(2)}) collective-permute-start(bf16[2,128,3328]{2,1,0:T(8,128)(2,1)S(1)} %get-tuple-element.23), channel_id=1, source_target_pairs={{0,8},{8,16},{16,24},{24,32},{32,40},{40,48},{48,56},{56,64},{64,7... | collective-permute-start | bytes 5111816 | tf_op jit(solution)/shard_map/ppermute | solution.py:477
  78.6 2.3 %copy-start = (f32[2,2,18,128,128]{4,3,2,1,0:T(8,128)S(1)}, f32[2,2,18,128,128]{4,3,2,1,0:T(8,128)}, u32[]{:S(2)}) copy-start(f32[2,2,18,128,128]{4,3,2,1,0:T(8,128)} %get-tuple-element.7.prow_hbm) | copy-start | bytes 14155780
  80.9 1.5 %copy-start.2 = (f32[2,2,896,128]{3,2,1,0:T(8,128)S(1)}, f32[2,2,896,128]{3,2,1,0:T(8,128)}, u32[]{:S(2)}) copy-start(f32[2,2,896,128]{3,2,1,0:T(8,128)} %get-tuple-element.8.pcol_hbm) | copy-start | bytes 5505028
where the time goes:
time: 87.3 us; the launch traced here: 86.9 us
  starting transfers between devices  32 us (37%)
  Pallas kernels  19.3 us (22%)
  waiting for transfers between devices  18.7 us (21%)
  local copies, waits for them, and re-layouts  11.5 us (13%)
  other arithmetic  4.59 us (5%)
    ppermute x4, starting transfers between devices, local(): diags.append(lax.ppermute(piece, ('sy', 'sx'), corner(-dy, -dx)))  18.2 us
    pallas_call x1, Pallas kernels, compute(): pl.pallas_call(compute_kernel, out_shape=(jax.ShapeDtypeStruct(spectrum.s...  14.9 us
    ppermute x1, waiting for transfers between devices, local(): from_down = lax.ppermute(vert_pack(0), 'sy', chain(rows, -1))  14.5 us
    ppermute x1, starting transfers between devices, local(): from_right = lax.ppermute(side_pack(0, 0), 'sx', chain(cols, -1))  7.53 us
    pallas_call x1, Pallas kernels, finish(): pl.pallas_call(finish_kernel, out_shape=(jax.ShapeDtypeStruct(out.shape,...  4.44 us
    ppermute x1, waiting for transfers between devices, local(): from_up = lax.ppermute(vert_pack(edge - BAND), 'sy', chain(rows, 1))  4.15 us
    unnamed x19, local copies, waits for them, and re-layouts  3.97 us
    concatenate x2, other arithmetic, side_pack(): return jnp.concatenate([band, tile[:, :, :128], tile[:, :, 128:]], axis=1)  3.03 us
  transfers between devices with their start and end apart: 8, of which 2 were waited for; matrix products, arithmetic and copies ran while one was open for 12% of the time, Pallas kernels for 17%

commit v1 on v0

--- a/solution.py
+++ b/solution.py
@@ -15,6 +15,9 @@
 W = 256
 HALF = 128
 FLOOR_SQUARE = 0.0625
+PACK_VMEM = 60 * 1024 * 1024
+CORNER_VMEM = 8 * 1024 * 1024
+FINISH_VMEM = 66500000
 BAND = 2 * H
 BF = jnp.bfloat16
 F32 = jnp.float32
@@ -37,12 +40,13 @@
         left = np.block([[re, -im], [im, re]])
         out.append(left)
         out.append(left.T)
-    packed = np.stack([np.stack(halves(t)) for t in out])
+    packed = np.stack([np.stack([halves(t)[part] for t in out]) for part in (0, 1)])
     spread = np.zeros((W, W))
     for p in (0, 1):
         for q in range(HALF):
             spread[2 * q + p, p * HALF + q] = 1.0
-    return packed, spread.astype(ml_dtypes.bfloat16)
+    spread = np.concatenate([spread, spread]).astype(ml_dtypes.bfloat16)
+    return packed, spread
 
 
 def split(value):
@@ -55,26 +59,46 @@
     return jnp.dot(a, b, preferred_element_type=F32)
 
 
+def put_rows(ref, index, rows, cols, value):
+    high, low = split(value)
+    ref[index, pl.ds(rows, 16), cols] = high
+    ref[index, pl.ds(W + rows, 16), cols] = low
+    ref[index, pl.ds(2 * W + rows, 16), cols] = high
+
+
+def put_cols(ref, index, rows, cols, value):
+    high, low = split(value)
+    ref[index, rows, pl.ds(cols, 128)] = high
+    ref[index, rows, pl.ds(W + cols, 128)] = low
+    ref[index, rows, pl.ds(2 * W + cols, 128)] = high
+
+
 def compute_kernel(
     starts, counts, weights, spec_hbm, pup_hbm, amp_hbm, tab_hbm, spread_hbm,
     out_hbm, prow_hbm, pcol_hbm, ppup_hbm,
-    spec, pupb, pup, amp, tab, spread, acc, pacc, inner,
-    win, prs, xh, xl, ya, yb, ampq, sem_in, sem_out,
+    spec, pupb, pup, amp, tab_l, tab_r, spread, acc, pacc, inner,
+    win, prs, xr, xc, xa, ya, yb, ampq, sem_in, sem_out,
 ):
     edge = spec.shape[2]
     tiles = edge // 128
     low_row, high_row = BAND, edge - BAND
     mid = high_row - low_row
     copies = []
+
+    def get(src, dst):
+        copy = pltpu.make_async_copy(src, dst, sem_in.at[len(copies)])
+        copy.start()
+        copies.append(copy)
+
+    get(pup_hbm, pupb)
+    for h in range(2):
+        get(amp_hbm.at[0, :, :, :, pl.ds(h * 128, 128)], amp.at[:, :, h])
+    for i, part in enumerate((0, 0, 1)):
+        get(tab_hbm.at[part], tab_l.at[:, :, pl.ds(i * W, W)])
+        get(tab_hbm.at[part], tab_r.at[:, pl.ds(i * W, W), :])
+    get(spread_hbm, spread)
     for g in range(2):
-        copies.append(pltpu.make_async_copy(spec_hbm.at[:, :, pl.ds(g * edge, edge)], spec.at[g], sem_in.at[g]))
-    copies.append(pltpu.make_async_copy(pup_hbm, pupb, sem_in.at[2]))
-    copies.append(pltpu.make_async_copy(tab_hbm, tab, sem_in.at[3]))
-    copies.append(pltpu.make_async_copy(spread_hbm, spread, sem_in.at[4]))
-    for h in range(2):
-        copies.append(pltpu.make_async_copy(amp_hbm.at[0, :, :, :, pl.ds(h * 128, 128)], amp.at[:, :, h], sem_in.at[5 + h]))
-    for c in copies:
-        c.start()
+        get(spec_hbm.at[:, :, pl.ds(g * edge, edge)], spec.at[g])
 
     zero = jnp.zeros((128, 128), F32)
 
@@ -86,14 +110,13 @@
         return carry
 
     lax.fori_loop(0, edge // 32, clear, 0)
-    for c in copies[2:]:
+    for c in copies[:-2]:
         c.wait()
     for g in range(2):
         for c in range(2):
             pup[g, c] = pupb[c, :, pl.ds(g * W, W)].astype(F32)
             pacc[g, c] = jnp.zeros((W, W), F32)
-    copies[0].wait()
-    copies[1].wait()
+    copies[-2].wait()
     lane = lax.broadcasted_iota(jnp.int32, (16, 128), 1)
 
     def slot_step(g, slot):
@@ -129,9 +152,9 @@
             for h in range(2):
                 rows = amp[g, slot, h, pl.ds(p, 128, stride=2), :]
                 hi, lo = split(rows)
-                xh[0, pl.ds(p * 128, 128), pl.ds(h * 128, 128)] = hi
-                xl[0, pl.ds(p * 128, 128), pl.ds(h * 128, 128)] = lo
-        ampq[...] = dot(xh[0], spread[...]) + dot(xl[0], spread[...])
+                xa[pl.ds(p * 128, 128), pl.ds(h * 128, 128)] = hi
+                xa[pl.ds(p * 128, 128), pl.ds(W + h * 128, 128)] = lo
+        ampq[...] = dot(xa[...], spread[...])
 
         for r in range(0, HALF, 16):
             for h in range(2):
@@ -143,77 +166,64 @@
                     pi = prs[1, h, pl.ds(rr, 16), :]
                     parts.append((pr * cr - pi * ci, pr * ci + pi * cr))
                 for c in range(2):
-                    for q in range(2):
-                        v = parts[0][c] + parts[1][c] if q == 0 else parts[0][c] - parts[1][c]
-                        hi, lo = split(v)
-                        xh[q, pl.ds(c * HALF + r, 16), pl.ds(h * 128, 128)] = hi
-                        xl[q, pl.ds(c * HALF + r, 16), pl.ds(h * 128, 128)] = lo
+                    cols = pl.ds(h * 128, 128)
+                    put_rows(xr, 0, c * HALF + r, cols, parts[0][c] + parts[1][c])
+                    put_rows(xr, 1, c * HALF + r, cols, parts[0][c] - parts[1][c])
         for q in range(2):
-            th, tl = tab[2 * q, 0], tab[2 * q, 1]
-            ya[q] = dot(th, xh[q]) + dot(th, xl[q]) + dot(tl, xh[q])
+            ya[q] = dot(tab_l[2 * q], xr[q])
         for q in range(2):
             for r in range(0, HALF, 16):
+                rows = pl.ds(q * HALF + r, 16)
                 for c in range(2):
                     y0 = ya[q, pl.ds(c * HALF + r, 16), pl.ds(0, 128)]
                     y1 = ya[q, pl.ds(c * HALF + r, 16), pl.ds(128, 128)]
-                    for u in range(2):
-                        hi, lo = split(y0 + y1 if u == 0 else y0 - y1)
-                        xh[u, pl.ds(q * HALF + r, 16), pl.ds(c * 128, 128)] = hi
-                        xl[u, pl.ds(q * HALF + r, 16), pl.ds(c * 128, 128)] = lo
+                    put_cols(xc, 0, rows, c * 128, y0 + y1)
+                    put_cols(xc, 1, rows, c * 128, y0 - y1)
         for u in range(2):
-            th, tl = tab[2 * u + 1, 0], tab[2 * u + 1, 1]
-            yb[u] = dot(xh[u], th) + dot(xl[u], th) + dot(xh[u], tl)
+            yb[u] = dot(xc[u], tab_r[2 * u + 1])
         for u in range(2):
             for r in range(0, W, 16):
-                re = yb[u, pl.ds(r, 16), pl.ds(0, 128)]
-                im = yb[u, pl.ds(r, 16), pl.ds(128, 128)]
+                rows = pl.ds(r, 16)
+                re = yb[u, rows, pl.ds(0, 128)]
+                im = yb[u, rows, pl.ds(128, 128)]
                 power = jnp.maximum(re * re + im * im, FLOOR_SQUARE)
-                keeper = 1.0 - ampq[pl.ds(r, 16), pl.ds(u * 128, 128)] * lax.rsqrt(power)
-                for c, v in enumerate((re, im)):
-                    hi, lo = split(v * keeper)
-                    xh[u, pl.ds(r, 16), pl.ds(c * 128, 128)] = hi
-                    xl[u, pl.ds(r, 16), pl.ds(c * 128, 128)] = lo
+                keeper = 1.0 - ampq[rows, pl.ds(u * 128, 128)] * lax.rsqrt(power)
+                put_cols(xc, u, rows, 0, re * keeper)
+                put_cols(xc, u, rows, 128, im * keeper)
         for u in range(2):
-            th, tl = tab[2 * u, 0], tab[2 * u, 1]
-            ya[u] = dot(xh[u], th) + dot(xl[u], th) + dot(xh[u], tl)
+            ya[u] = dot(xc[u], tab_r[2 * u])
         for q in range(2):
             for r in range(0, HALF, 16):
+                rows = pl.ds(q * HALF + r, 16)
                 for c in range(2):
-                    e = ya[0, pl.ds(q * HALF + r, 16), pl.ds(c * 128, 128)]
-                    o = ya[1, pl.ds(q * HALF + r, 16), pl.ds(c * 128, 128)]
-                    for h in range(2):
-                        hi, lo = split(e + o if h == 0 else e - o)
-                        xh[q, pl.ds(c * HALF + r, 16), pl.ds(h * 128, 128)] = hi
-                        xl[q, pl.ds(c * HALF + r, 16), pl.ds(h * 128, 128)] = lo
+                    e = ya[0, rows, pl.ds(c * 128, 128)]
+                    o = ya[1, rows, pl.ds(c * 128, 128)]
+                    put_rows(xr, q, c * HALF + r, pl.ds(0, 128), e + o)
+                    put_rows(xr, q, c * HALF + r, pl.ds(128, 128), e - o)
         for q in range(2):
-            th, tl = tab[2 * q + 1, 0], tab[2 * q + 1, 1]
-            yb[q] = dot(th, xh[q]) + dot(th, xl[q]) + dot(tl, xh[q])
+            yb[q] = dot(tab_l[2 * q + 1], xr[q])
         for r in range(0, HALF, 16):
             for rr in (r, r + HALF):
-                back = []
-                for c in range(2):
-                    row = []
-                    for h in range(2):
+                rows = pl.ds(a + rr, 16)
+                old = [[acc[g, c, k0 + i, rows, :] for i in range(3)] for c in range(2)]
+                drop, terms = [], []
+                for h in range(2):
+                    back = []
+                    for c in range(2):
                         e = yb[0, pl.ds(c * HALF + r, 16), pl.ds(h * 128, 128)]
                         o = yb[1, pl.ds(c * HALF + r, 16), pl.ds(h * 128, 128)]
-                        row.append(e + o if rr == r else e - o)
-                    back.append(row)
-                terms = []
-                for h in range(2):
-                    br, bi = back[0][h], back[1][h]
+                        back.append(e + o if rr == r else e - o)
+                    br, bi = back
                     pr = prs[0, h, pl.ds(rr, 16), :]
                     pi = prs[1, h, pl.ds(rr, 16), :]
                     cr = crop(0, h, rr)
                     ci = crop(1, h, rr)
-                    drop = (pr * br + pi * bi, pr * bi - pi * br)
+                    drop.append((pr * br + pi * bi, pr * bi - pi * br))
                     terms.append((cr * br + ci * bi, cr * bi - ci * br))
-                    rows = pl.ds(a + rr, 16)
-                    for c in range(2):
-                        if h == 1:
-                            acc[g, c, k0 + 1, rows, :] += drop[c]
-                        else:
-                            acc[g, c, k0, rows, :] += jnp.where(from_first, drop[c], 0.0)
-                            acc[g, c, k0 + 2, rows, :] += jnp.where(from_first, 0.0, drop[c])
+                for c in range(2):
+                    acc[g, c, k0, rows, :] = old[c][0] + jnp.where(from_first, drop[0][c], 0.0)
+                    acc[g, c, k0 + 1, rows, :] = old[c][1] + drop[1][c]
+                    acc[g, c, k0 + 2, rows, :] = old[c][2] + jnp.where(from_first, 0.0, drop[0][c])
                 for c in range(2):
                     t0 = pltpu.roll(terms[0][c], back_shift, 1)
                     t1 = pltpu.roll(terms[1][c], back_shift, 1)
@@ -235,6 +245,8 @@
             return carry
 
         lax.fori_loop(0, counts[g], step, 0)
+        if g == 0:
+            copies[-1].wait()
         left = left_out if g == 0 else F32(1.0)
         right = right_out if g == 1 else F32(1.0)
         neighbours = up + down + left + right
@@ -306,38 +318,40 @@
             jax.ShapeDtypeStruct((2, 2, mid, 128), F32),
             jax.ShapeDtypeStruct(pupils.shape, F32),
         ),
-        in_specs=[smem, smem, smem, hbm, hbm, hbm, hbm, hbm],
+        in_specs=[smem, smem, smem] + [hbm] * 5,
         out_specs=(hbm, hbm, hbm, hbm),
         scratch_shapes=[
             pltpu.VMEM((2, 2, edge, edge), BF),
             pltpu.VMEM((2, W, 2 * W), BF),
             pltpu.VMEM((2, 2, W, W), F32),
             pltpu.VMEM((2, MAXL, 2, W, 128), F32),
-            pltpu.VMEM((4, 2, W, W), BF),
-            pltpu.VMEM((W, W), BF),
+            pltpu.VMEM((4, W, 3 * W), BF),
+            pltpu.VMEM((4, 3 * W, W), BF),
+            pltpu.VMEM((2 * W, W), BF),
             pltpu.VMEM((2, 2, tiles, edge, 128), F32),
             pltpu.VMEM((2, 2, W, W), F32),
             pltpu.VMEM((2, 2, mid, (tiles - 1) * 128), BF),
             pltpu.VMEM((2, 3, W + 16, 128), F32),
             pltpu.VMEM((2, 2, W, 128), F32),
-            pltpu.VMEM((2, W, W), BF),
-            pltpu.VMEM((2, W, W), BF),
+            pltpu.VMEM((2, 3 * W, W), BF),
+            pltpu.VMEM((2, W, 3 * W), BF),
+            pltpu.VMEM((W, 2 * W), BF),
             pltpu.VMEM((2, W, W), F32),
             pltpu.VMEM((2, W, W), F32),
             pltpu.VMEM((W, W), F32),
-            pltpu.SemaphoreType.DMA((7,)),
+            pltpu.SemaphoreType.DMA((12,)),
             pltpu.SemaphoreType.DMA((20,)),
         ],
-        compiler_params=pltpu.CompilerParams(vmem_limit_bytes=52 * 1024 * 1024),
+        compiler_params=pltpu.CompilerParams(vmem_limit_bytes=66500000),
         cost_estimate=pl.CostEstimate(flops=20_000_000_000, bytes_accessed=30_000_000, transcendentals=0),
         name="data_terms",
     )(starts, counts, weights, spectrum, pupils, amplitudes, jnp.asarray(packed), jnp.asarray(spread))
 
 
 def finish_kernel(
-    out_in, prow_hbm, pcol_hbm, ppup_hbm, up_hbm, down_hbm, left_hbm, right_hbm, ul_hbm, ur_hbm, dl_hbm, dr_hbm,
+    out_in, prow_hbm, pcol_hbm, ppup_hbm, up_hbm, down_hbm, left_hbm, right_hbm, endl_hbm, endr_hbm,
     out_hbm, pup_hbm,
-    prow, pcol, ppup, vert, side, diag, rows_out, cols_out, pup_out, sem_in, sem_out,
+    prow, pcol, ppup, vert, side, ends, rows_out, cols_out, pup_out, sem_in, sem_out,
 ):
     edge = out_in.shape[1]
     tiles = edge // 128
@@ -353,13 +367,11 @@
 
     verts = (up_hbm, down_hbm)
     sides = (left_hbm, right_hbm)
-    diags = ((ul_hbm, ur_hbm), (dl_hbm, dr_hbm))
     for d in range(2):
         get(("side", d), sides[d], side.at[d])
+        get(("ends", d), (endl_hbm, endr_hbm)[d], ends.at[d])
     for t in range(2):
         get(("vert", t), verts[t], vert.at[t])
-        for d in range(2):
-            get(("diag", t, d), diags[t][d], diag.at[t, d])
         get(("prow", t), prow_hbm.at[t], prow.at[t])
     for d in range(2):
         get(("pcol", d), pcol_hbm.at[d], pcol.at[d])
@@ -371,12 +383,10 @@
         copy.start()
         outs.append(copy)
 
-    ins["side", 0].wait()
-    ins["side", 1].wait()
+    ins["ends", 0].wait()
+    ins["ends", 1].wait()
     for t in range(2):
         ins["vert", t].wait()
-        ins["diag", t, 0].wait()
-        ins["diag", t, 1].wait()
         ins["prow", t].wait()
         first = t * high_row
         for c in range(2):
@@ -386,13 +396,15 @@
                     sub = sub + vert[t, c, :, pl.ds((2 * tiles - 1 - k) * 128, 128)].astype(F32)
                 if k == 0 or k == last:
                     d = 0 if k == 0 else 1
-                    sub = sub + (diag[t, d, c].astype(F32) + side[d, c, pl.ds(first, BAND), :].astype(F32))
+                    far = vert[t, c, :, pl.ds(2 * edge + 4 * W + d * BAND, BAND)].astype(F32)
+                    sub = sub + (far + ends[d, c, pl.ds(t * BAND, BAND), :].astype(F32))
                 rows_out[t, c, :, pl.ds(k * 128, 128)] = (prow[t, c, k] - 0.5 * sub).astype(BF)
             put(rows_out.at[t, c], out_hbm.at[c, pl.ds(first, BAND), :])
     for d in range(2):
+        ins["side", d].wait()
         ins["pcol", d].wait()
         for c in range(2):
-            sub = side[d, c, pl.ds(BAND, mid), :].astype(F32)
+            sub = side[d, c, pl.ds(0, mid), :].astype(F32)
             cols_out[d, c] = (pcol[d, c] - 0.5 * sub).astype(BF)
             put(cols_out.at[d, c], out_hbm.at[c, pl.ds(BAND, mid), pl.ds(d * last * 128, 128)])
     ins["ppup"].wait()
@@ -402,7 +414,7 @@
             for q in range(4):
                 cols = pl.ds(q * 128, 128)
                 d = q // 2
-                sub = side[d, c, pl.ds(edge + (q % 2) * W + half * 128, 128), :].astype(F32)
+                sub = side[d, c, pl.ds(mid + (q % 2) * W + half * 128, 128), :].astype(F32)
                 for t in range(2):
                     sub = sub + vert[t, c, :, pl.ds(2 * edge + half * 512 + q * 128, 128)].astype(F32)
                 pup_out[c, rows, cols] = ppup[c, rows, cols] - 0.5 * sub
@@ -411,7 +423,7 @@
         copy.wait()
 
 
-def finish(out, prow, pcol, ppup, ups, sides, diags):
+def finish(out, prow, pcol, ppup, ups, sides, ends):
     edge = out.shape[1]
     tiles = edge // 128
     mid = edge - 2 * BAND
@@ -422,7 +434,7 @@
             jax.ShapeDtypeStruct(out.shape, BF),
             jax.ShapeDtypeStruct(ppup.shape, F32),
         ),
-        in_specs=[hbm] * 12,
+        in_specs=[hbm] * 10,
         out_specs=(hbm, hbm),
         input_output_aliases={0: 0},
         scratch_shapes=[
@@ -431,22 +443,93 @@
             pltpu.VMEM(ppup.shape, F32),
             pltpu.VMEM((2,) + ups[0].shape, BF),
             pltpu.VMEM((2,) + sides[0].shape, BF),
-            pltpu.VMEM((2, 2) + diags[0].shape, BF),
+            pltpu.VMEM((2,) + ends[0].shape, BF),
             pltpu.VMEM((2, 2, BAND, 2 * edge), BF),
             pltpu.VMEM((2, 2, mid, 128), BF),
             pltpu.VMEM(ppup.shape, F32),
             pltpu.SemaphoreType.DMA((16,)),
             pltpu.SemaphoreType.DMA((9,)),
         ],
-        compiler_params=pltpu.CompilerParams(vmem_limit_bytes=32 * 1024 * 1024),
+        compiler_params=pltpu.CompilerParams(vmem_limit_bytes=FINISH_VMEM),
         cost_estimate=pl.CostEstimate(flops=10_000_000, bytes_accessed=17_000_000, transcendentals=0),
         name="shared_bands",
-    )(out, prow, pcol, ppup, *ups, *sides, *diags)
+    )(out, prow, pcol, ppup, *ups, *sides, *ends)
+
+
+def pack_kernel(spec_hbm, pup_hbm, left_c, right_c, left, right, top, bottom, sem):
+    edge, wide = spec_hbm.shape[1], spec_hbm.shape[2]
+    mid = edge - 2 * BAND
+    copies = []
+
+    def put(src, dst):
+        copy = pltpu.make_async_copy(src, dst, sem.at[len(copies)])
+        copy.start()
+        copies.append(copy)
+
+    for ends, msg, first, half in ((left_c, left, 0, 0), (right_c, right, wide - BAND, 1)):
+        cols = pl.ds(first, BAND)
+        put(spec_hbm.at[:, pl.ds(0, BAND), cols], ends.at[:, pl.ds(0, BAND), :])
+        put(spec_hbm.at[:, pl.ds(edge - BAND, BAND), cols], ends.at[:, pl.ds(BAND, BAND), :])
+        put(spec_hbm.at[:, pl.ds(BAND, mid), cols], msg.at[:, pl.ds(0, mid), :])
+        for q in range(2):
+            put(pup_hbm.at[:, :, pl.ds(half * W + q * 128, 128)], msg.at[:, pl.ds(mid + q * W, W), :])
+    for msg, first in ((top, 0), (bottom, edge - BAND)):
+        put(spec_hbm.at[:, pl.ds(first, BAND), :], msg.at[:, :, pl.ds(0, wide)])
+        for q in range(2):
+            put(pup_hbm.at[:, pl.ds(q * 128, 128), :], msg.at[:, :, pl.ds(wide + q * 2 * W, 2 * W)])
+    for copy in copies:
+        copy.wait()
+
+
+def pack(spectrum, pupils):
+    edge, wide = spectrum.shape[1], spectrum.shape[2]
+    hbm = pl.BlockSpec(memory_space=pl.ANY)
+    ends = jax.ShapeDtypeStruct((2, 2 * BAND, BAND), BF)
+    side = jax.ShapeDtypeStruct((2, edge - 2 * BAND + 2 * W, BAND), BF)
+    vert = jax.ShapeDtypeStruct((2, BAND, wide + 4 * W + 2 * BAND), BF)
+    return pl.pallas_call(
+        pack_kernel,
+        out_shape=(ends, ends, side, side, vert, vert),
+        in_specs=[hbm, hbm],
+        out_specs=(hbm,) * 6,
+        scratch_shapes=[pltpu.SemaphoreType.DMA((16,))],
+        compiler_params=pltpu.CompilerParams(vmem_limit_bytes=PACK_VMEM),
+        cost_estimate=pl.CostEstimate(flops=1, bytes_accessed=11_000_000, transcendentals=0),
+        name="pack",
+    )(spectrum, pupils)
+
+
+def corners_kernel(top_in, bottom_in, left, right, top, bottom, sem):
+    start = top.shape[2] - 2 * BAND
+    copies = []
+    for t, msg in enumerate((top, bottom)):
+        for d, src in enumerate((left, right)):
+            copy = pltpu.make_async_copy(
+                src.at[:, pl.ds(t * BAND, BAND), :], msg.at[:, :, pl.ds(start + d * BAND, BAND)], sem.at[2 * t + d]
+            )
+            copy.start()
+            copies.append(copy)
+    for copy in copies:
+        copy.wait()
+
+
+def add_corners(top, bottom, left, right):
+    hbm = pl.BlockSpec(memory_space=pl.ANY)
+    vert = jax.ShapeDtypeStruct(top.shape, BF)
+    return pl.pallas_call(
+        corners_kernel,
+        out_shape=(vert, vert),
+        in_specs=[hbm] * 4,
+        out_specs=(hbm, hbm),
+        input_output_aliases={0: 0, 1: 1},
+        scratch_shapes=[pltpu.SemaphoreType.DMA((4,))],
+        compiler_params=pltpu.CompilerParams(vmem_limit_bytes=CORNER_VMEM),
+        cost_estimate=pl.CostEstimate(flops=1, bytes_accessed=1_000_000, transcendentals=0),
+        name="add_corners",
+    )(top, bottom, left, right)
 
 
 def local(spectrum, pupils, amplitudes, crop_starts, led_counts):
-    edge = spectrum.shape[1]
-    wide = spectrum.shape[2]
     rows = lax.axis_size("sy")
     cols = lax.axis_size("sx")
     row = lax.axis_index("sy")
@@ -455,39 +538,19 @@
     def chain(count, step):
         return [(i, i + step) for i in range(count) if 0 <= i + step < count]
 
-    def corner(dy, dx):
-        return [
-            (y * cols + x, (y + dy) * cols + x + dx)
-            for y in range(rows)
-            for x in range(cols)
-            if 0 <= y + dy < rows and 0 <= x + dx < cols
-        ]
-
-    def side_pack(first, half):
-        band = spectrum[:, :, first : first + BAND]
-        tile = pupils[:, :, half * W : (half + 1) * W]
-        return jnp.concatenate([band, tile[:, :, :128], tile[:, :, 128:]], axis=1)
-
-    def vert_pack(first):
-        band = spectrum[:, first : first + BAND, :]
-        return jnp.concatenate([band, pupils[:, :128, :], pupils[:, 128:, :]], axis=2)
-
-    from_left = lax.ppermute(side_pack(wide - BAND, 1), "sx", chain(cols, 1))
-    from_right = lax.ppermute(side_pack(0, 0), "sx", chain(cols, -1))
-    from_up = lax.ppermute(vert_pack(edge - BAND), "sy", chain(rows, 1))
-    from_down = lax.ppermute(vert_pack(0), "sy", chain(rows, -1))
-    diags = []
-    for dy in (-1, 1):
-        for dx in (-1, 1):
-            y0 = edge - BAND if dy < 0 else 0
-            x0 = wide - BAND if dx < 0 else 0
-            piece = spectrum[:, y0 : y0 + BAND, x0 : x0 + BAND]
-            diags.append(lax.ppermute(piece, ("sy", "sx"), corner(-dy, -dx)))
+    left_c, right_c, left, right, top, bottom = pack(spectrum, pupils)
+    ends_left = lax.ppermute(right_c, "sx", chain(cols, 1))
+    ends_right = lax.ppermute(left_c, "sx", chain(cols, -1))
+    from_left = lax.ppermute(right, "sx", chain(cols, 1))
+    from_right = lax.ppermute(left, "sx", chain(cols, -1))
+    top, bottom = add_corners(top, bottom, ends_left, ends_right)
+    from_up = lax.ppermute(bottom, "sy", chain(rows, 1))
+    from_down = lax.ppermute(top, "sy", chain(rows, -1))
     weights = jnp.stack([row > 0, row < rows - 1, col > 0, col < cols - 1]).astype(F32)
     out, prow, pcol, ppup = compute(
         spectrum, pupils, amplitudes, crop_starts.reshape(-1), led_counts.reshape(-1), weights
     )
-    return finish(out, prow, pcol, ppup, (from_up, from_down), (from_left, from_right), diags)
+    return finish(out, prow, pcol, ppup, (from_up, from_down), (from_left, from_right), (ends_left, ends_right))
 
 
 def solution(mesh):

time: 87.3 us -> 221 us (2.53)
  Pallas kernels: 19.3 us -> 178 us
  local copies, waits for them, and re-layouts: 11.5 us -> 0.68 us
  starting transfers between devices: 32 us -> 26.6 us
  waiting for transfers between devices: 18.7 us -> 13.7 us
  other arithmetic: 4.59 us -> 0.65 us
    pallas_call x0 -> x2, Pallas kernels: none -> 157 us  [the longest x1 156 us: pack(): pl.pallas_call(pack_kernel, out_shape=(ends, ends, side, side, vert, vert...]
    slice x5 -> x0, local copies, waits for them, and re-layouts: 7.45 us -> none  [the longest x1 2.8 us: vert_pack(): band = spectrum[:, first:first + BAND, :]]
    ppermute x8 -> x6, starting transfers between devices: 32 us -> 26.6 us  [the longest x1 7.54 us: local(): from_right = lax.ppermute(left, 'sx', chain(cols, -1))]
    ppermute x8 -> x6, waiting for transfers between devices: 18.7 us -> 13.7 us  [the longest x1 13.7 us: local(): from_up = lax.ppermute(bottom, 'sy', chain(rows, 1))]
    concatenate x3 -> x0, other arithmetic: 4.51 us -> none  [the longest x2 3.03 us: side_pack(): return jnp.concatenate([band, tile[:, :, :128], tile[:, :, 128:]], axis=1)]
    unnamed x19 -> x7, local copies, waits for them, and re-layouts: 3.97 us -> 0.11 us
  transfers between devices with their start and end apart: 8 -> 6, of which waited for: 2 -> 1; matrix products, arithmetic and copies ran while one was open for 12% -> 1% of each run, Pallas kernels for 17% -> 7%
where the time goes in v1:
time: 221 us
  Pallas kernels  178 us (81%)
  starting transfers between devices  26.6 us (12%)
  waiting for transfers between devices  13.7 us (6%)
    pallas_call x1, Pallas kernels, pack(): pl.pallas_call(pack_kernel, out_shape=(ends, ends, side, side, vert, vert...  156 us
    pallas_call x1, Pallas kernels, compute(): pl.pallas_call(compute_kernel, out_shape=(jax.ShapeDtypeStruct(spectrum.s...  14.7 us
    ppermute x1, waiting for transfers between devices, local(): from_up = lax.ppermute(bottom, 'sy', chain(rows, 1))  13.7 us
    ppermute x1, starting transfers between devices, local(): from_right = lax.ppermute(left, 'sx', chain(cols, -1))  7.54 us
    pallas_call x1, Pallas kernels, finish(): pl.pallas_call(finish_kernel, out_shape=(jax.ShapeDtypeStruct(out.shape,...  6.58 us
    ppermute x1, starting transfers between devices, local(): from_down = lax.ppermute(top, 'sy', chain(rows, -1))  5.75 us
    ppermute x1, starting transfers between devices, local(): ends_right = lax.ppermute(left_c, 'sx', chain(cols, -1))  5.63 us
  transfers between devices with their start and end apart: 6, of which 1 were waited for; matrix products, arithmetic and copies ran while one was open for 1% of the time, Pallas kernels for 7%

profile of v1, /device:TPU:6, one launch (start us, length us, event | category | flops | bytes accessed | tf_op | source)
XLA Modules:
  0.0 220.5 jit_solution(11694413037768541622)
XLA Ops:
  0.6 0.0 copy-start.2
  0.6 156.1 %pack.1 = (bf16[2,256,128]{2,1,0:T(8,128)(2,1)}, bf16[2,256,128]{2,1,0:T(8,128)(2,1)}, bf16[2,1408,128]{2,1,0:T(8,128)(2,1)}, bf16[2,1408,128]{2,1,0:T(8,128)(2,...) custom-call(bf16[2,1152,2304]{2,1,0:T(8,128)(2,1)} %spec_hbm.3, bf16[2,256,512]{2,1,0:T(8,128)(2,1)} %pup_hbm.3), custom_call_target="tpu_custom_call" | custom-call | flops 1 | bytes 11000000 | tf_op jit(solution)/shard_map/pack/pallas_call | solution.py:490
  156.7 3.8 %collective-permute-start = (bf16[2,256,128]{2,1,0:T(8,128)(2,1)}, bf16[2,256,128]{2,1,0:T(8,128)(2,1)S(1)}, u32[]{:S(2)}, u32[]{:S(2)}) collective-permute-start(bf16[2,256,128]{2,1,0:T(8,128)(2,1)} %get-tuple-element.20), channel_id=1, source_target_pairs={{0,1},{1,2},{2,3},{3,4},{4,5},{5,6},{6,7},{8,9},{9,10},{10,11},{11... | collective-permute-start | bytes 393224 | tf_op jit(solution)/shard_map/ppermute | solution.py:542
  160.6 5.6 %collective-permute-start.1 = (bf16[2,256,128]{2,1,0:T(8,128)(2,1)}, bf16[2,256,128]{2,1,0:T(8,128)(2,1)S(1)}, u32[]{:S(2)}, u32[]{:S(2)}) collective-permute-start(bf16[2,256,128]{2,1,0:T(8,128)(2,1)} %get-tuple-element.21), channel_id=1, source_target_pairs={{1,0},{2,1},{3,2},{4,3},{5,4},{6,5},{7,6},{9,8},{10,9},{11,10},{12... | collective-permute-start | bytes 393224 | tf_op jit(solution)/shard_map/ppermute | solution.py:543
  166.2 1.9 collective-permute-start.4
  168.1 7.5 %collective-permute-start.5 = (bf16[2,1408,128]{2,1,0:T(8,128)(2,1)}, bf16[2,1408,128]{2,1,0:T(8,128)(2,1)}, u32[]{:S(2)}, u32[]{:S(2)}) collective-permute-start(bf16[2,1408,128]{2,1,0:T(8,128)(2,1)} %get-tuple-element.25), channel_id=1, source_target_pairs={{1,0},{2,1},{3,2},{4,3},{5,4},{6,5},{7,6},{9,8},{10,9},{11,10},{12... | collective-permute-start | bytes 2162696 | tf_op jit(solution)/shard_map/ppermute | solution.py:545
  175.7 0.0 copy-done.2
  175.7 0.1 copy.13
  175.8 0.6 reshape.10.starts
  176.4 0.7 add_convert_fusion.weights
  177.0 0.0 collective-permute-done.left.endl_hbm
  177.0 0.0 collective-permute-done.1.right.endr_hbm
  177.1 0.0 copy-start.1
  177.1 0.8 add_corners.1
  177.9 0.0 copy-done
  177.9 0.0 copy-done.1
  177.9 1.9 collective-permute-start.2
  179.8 5.8 %collective-permute-start.3 = (bf16[2,128,3584]{2,1,0:T(8,128)(2,1)}, bf16[2,128,3584]{2,1,0:T(8,128)(2,1)}, u32[]{:S(2)}, u32[]{:S(2)}) collective-permute-start(bf16[2,128,3584]{2,1,0:T(8,128)(2,1)} %get-tuple-element.23), channel_id=1, source_target_pairs={{8,0},{16,8},{24,16},{32,24},{40,32},{48,40},{56,48},{64,56},{72,6... | collective-permute-start | bytes 5505032 | tf_op jit(solution)/shard_map/ppermute | solution.py:548
  185.6 14.7 %data_terms.1 = (bf16[2,1152,2304]{2,1,0:T(8,128)(2,1)}, f32[2,2,18,128,128]{4,3,2,1,0:T(8,128)}, f32[2,2,896,128]{3,2,1,0:T(8,128)}, f32[2,256,512]{2,1,0:T(8,128)}) custom-call(s32[16]{0:T(128)} %reshape.10.starts, s32[2]{0:T(128)} %bitcast.5, f32[4]{0:T(128)} %add_convert_fusion.weights, bf16[2,1152,2304]{2,1,0:T(8,128)(2,1)} %spec_hbm.3, ...), custom_call_target="tpu_custom_call" | custom-call | flops 20000000000 | bytes 30000000 | tf_op jit(solution)/shard_map/data_terms/pallas_call | solution.py:313
  200.2 0.0 collective-permute-done.4.left_hbm
  200.2 0.0 collective-permute-done.5.right_hbm
  200.3 13.7 %collective-permute-done.2.up_hbm = bf16[2,128,3584]{2,1,0:T(8,128)(2,1)} collective-permute-done((bf16[2,128,3584]{2,1,0:T(8,128)(2,1)}, bf16[2,128,3584]{2,1,0:T(8,128)(2,1)}, u32[]{:S(2)}, u32[]{:S(2)}) %collective-permute-start.2) | collective-permute-done | bytes 1835040 | tf_op jit(solution)/shard_map/ppermute | solution.py:547
  213.9 0.0 collective-permute-done.3.down_hbm
  213.9 6.6 %shared_bands.1 = (bf16[2,1152,2304]{2,1,0:T(8,128)(2,1)}, f32[2,256,512]{2,1,0:T(8,128)}) custom-call(bf16[2,1152,2304]{2,1,0:T(8,128)(2,1)} %get-tuple-element.14.out_in, f32[2,2,18,128,128]{4,3,2,1,0:T(8,128)} %get-tuple-element.15.prow_hbm, f32[2,2,896,128]{3,2,1,0:T(8,128)} %get-tuple-element.16.pcol_hbm, ...), custom_call_target="tpu_custom_call", output_to_operand_aliasing={{0}: (0, {})} | custom-call | flops 10000000 | bytes 17000000 | tf_op jit(solution)/shard_map/shared_bands/pallas_call | solution.py:431
  (1 shorter events, 0.0 us)
Async XLA Ops:
  0.6 175.1 %copy-start.2 = (s32[1,2,4,2]{2,3,1,0:T(2,128)S(1)}, s32[1,2,4,2]{2,3,1,0:T(2,128)}, u32[]{:S(2)}) copy-start(s32[1,2,4,2]{2,3,1,0:T(2,128)} %param.10) | copy-start | bytes 196
  156.7 20.3 %collective-permute-start = (bf16[2,256,128]{2,1,0:T(8,128)(2,1)}, bf16[2,256,128]{2,1,0:T(8,128)(2,1)S(1)}, u32[]{:S(2)}, u32[]{:S(2)}) collective-permute-start(bf16[2,256,128]{2,1,0:T(8,128)(2,1)} %get-tuple-element.20), channel_id=1, source_target_pairs={{0,1},{1,2},{2,3},{3,4},{4,5},{5,6},{6,7},{8,9},{9,10},{10,11},{11... | collective-permute-start | bytes 393224 | tf_op jit(solution)/shard_map/ppermute | solution.py:542
  160.6 16.5 %collective-permute-start.1 = (bf16[2,256,128]{2,1,0:T(8,128)(2,1)}, bf16[2,256,128]{2,1,0:T(8,128)(2,1)S(1)}, u32[]{:S(2)}, u32[]{:S(2)}) collective-permute-start(bf16[2,256,128]{2,1,0:T(8,128)(2,1)} %get-tuple-element.21), channel_id=1, source_target_pairs={{1,0},{2,1},{3,2},{4,3},{5,4},{6,5},{7,6},{9,8},{10,9},{11,10},{12... | collective-permute-start | bytes 393224 | tf_op jit(solution)/shard_map/ppermute | solution.py:543
  166.2 34.0 %collective-permute-start.4 = (bf16[2,1408,128]{2,1,0:T(8,128)(2,1)}, bf16[2,1408,128]{2,1,0:T(8,128)(2,1)}, u32[]{:S(2)}, u32[]{:S(2)}) collective-permute-start(bf16[2,1408,128]{2,1,0:T(8,128)(2,1)} %get-tuple-element.24), channel_id=1, source_target_pairs={{0,1},{1,2},{2,3},{3,4},{4,5},{5,6},{6,7},{8,9},{9,10},{10,11},{11... | collective-permute-start | bytes 2162696 | tf_op jit(solution)/shard_map/ppermute | solution.py:544
  168.1 32.1 %collective-permute-start.5 = (bf16[2,1408,128]{2,1,0:T(8,128)(2,1)}, bf16[2,1408,128]{2,1,0:T(8,128)(2,1)}, u32[]{:S(2)}, u32[]{:S(2)}) collective-permute-start(bf16[2,1408,128]{2,1,0:T(8,128)(2,1)} %get-tuple-element.25), channel_id=1, source_target_pairs={{1,0},{2,1},{3,2},{4,3},{5,4},{6,5},{7,6},{9,8},{10,9},{11,10},{12... | collective-permute-start | bytes 2162696 | tf_op jit(solution)/shard_map/ppermute | solution.py:545
  177.0 0.8 copy-start
  177.1 0.8 copy-start.1
  177.9 36.1 %collective-permute-start.2 = (bf16[2,128,3584]{2,1,0:T(8,128)(2,1)}, bf16[2,128,3584]{2,1,0:T(8,128)(2,1)}, u32[]{:S(2)}, u32[]{:S(2)}) collective-permute-start(bf16[2,128,3584]{2,1,0:T(8,128)(2,1)} %get-tuple-element.22), channel_id=1, source_target_pairs={{0,8},{8,16},{16,24},{24,32},{32,40},{40,48},{48,56},{56,64},{64,7... | collective-permute-start | bytes 5505032 | tf_op jit(solution)/shard_map/ppermute | solution.py:547
  179.8 34.1 %collective-permute-start.3 = (bf16[2,128,3584]{2,1,0:T(8,128)(2,1)}, bf16[2,128,3584]{2,1,0:T(8,128)(2,1)}, u32[]{:S(2)}, u32[]{:S(2)}) collective-permute-start(bf16[2,128,3584]{2,1,0:T(8,128)(2,1)} %get-tuple-element.23), channel_id=1, source_target_pairs={{8,0},{16,8},{24,16},{32,24},{40,32},{48,40},{56,48},{64,56},{72,6... | collective-permute-start | bytes 5505032 | tf_op jit(solution)/shard_map/ppermute | solution.py:548

commit v2 on v1

--- a/solution.py
+++ b/solution.py
@@ -117,9 +117,10 @@
             pup[g, c] = pupb[c, :, pl.ds(g * W, W)].astype(F32)
             pacc[g, c] = jnp.zeros((W, W), F32)
     copies[-2].wait()
+    copies[-1].wait()
     lane = lax.broadcasted_iota(jnp.int32, (16, 128), 1)
 
-    def slot_step(g, slot):
+    def slot_stages(g, slot):
         a = starts[(g * MAXL + slot) * 2]
         b = starts[(g * MAXL + slot) * 2 + 1]
         a0 = pl.multiple_of(jnp.minimum(a // 16 * 16, edge - W - 16), 16)
@@ -135,26 +136,27 @@
             for r in range(0, W + 16, 16):
                 block = spec[g, c, pl.ds(a0 + r, 16), pl.ds(col0, 384)].astype(F32)
                 for i in range(3):
-                    win[c, i, pl.ds(r, 16), :] = block[:, i * 128 : (i + 1) * 128]
+                    win[g, c, i, pl.ds(r, 16), :] = block[:, i * 128 : (i + 1) * 128]
         for c in range(2):
             for r in range(0, W, 16):
                 r0 = pltpu.roll(pup[g, c, pl.ds(r, 16), pl.ds(0, 128)], sr, 1)
                 r1 = pltpu.roll(pup[g, c, pl.ds(r, 16), pl.ds(128, 128)], sr, 1)
-                prs[c, 0, pl.ds(r, 16), :] = jnp.where(from_first, r0, r1)
-                prs[c, 1, pl.ds(r, 16), :] = jnp.where(from_first, r1, r0)
+                prs[g, c, 0, pl.ds(r, 16), :] = jnp.where(from_first, r0, r1)
+                prs[g, c, 1, pl.ds(r, 16), :] = jnp.where(from_first, r1, r0)
 
         def crop(c, h, r):
             if h == 1:
-                return win[c, 1, pl.ds(off + r, 16), :]
-            return jnp.where(from_first, win[c, 0, pl.ds(off + r, 16), :], win[c, 2, pl.ds(off + r, 16), :])
+                return win[g, c, 1, pl.ds(off + r, 16), :]
+            return jnp.where(from_first, win[g, c, 0, pl.ds(off + r, 16), :], win[g, c, 2, pl.ds(off + r, 16), :])
 
         for p in range(2):
             for h in range(2):
                 rows = amp[g, slot, h, pl.ds(p, 128, stride=2), :]
                 hi, lo = split(rows)
-                xa[pl.ds(p * 128, 128), pl.ds(h * 128, 128)] = hi
-                xa[pl.ds(p * 128, 128), pl.ds(W + h * 128, 128)] = lo
-        ampq[...] = dot(xa[...], spread[...])
+                xa[g, pl.ds(p * 128, 128), pl.ds(h * 128, 128)] = hi
+                xa[g, pl.ds(p * 128, 128), pl.ds(W + h * 128, 128)] = lo
+        ampq[g] = dot(xa[g], spread[...])
+        yield
 
         for r in range(0, HALF, 16):
             for h in range(2):
@@ -162,46 +164,50 @@
                 for rr in (r, r + HALF):
                     cr = crop(0, h, rr)
                     ci = crop(1, h, rr)
-                    pr = prs[0, h, pl.ds(rr, 16), :]
-                    pi = prs[1, h, pl.ds(rr, 16), :]
+                    pr = prs[g, 0, h, pl.ds(rr, 16), :]
+                    pi = prs[g, 1, h, pl.ds(rr, 16), :]
                     parts.append((pr * cr - pi * ci, pr * ci + pi * cr))
                 for c in range(2):
                     cols = pl.ds(h * 128, 128)
-                    put_rows(xr, 0, c * HALF + r, cols, parts[0][c] + parts[1][c])
-                    put_rows(xr, 1, c * HALF + r, cols, parts[0][c] - parts[1][c])
+                    put_rows(xr.at[g], 0, c * HALF + r, cols, parts[0][c] + parts[1][c])
+                    put_rows(xr.at[g], 1, c * HALF + r, cols, parts[0][c] - parts[1][c])
         for q in range(2):
-            ya[q] = dot(tab_l[2 * q], xr[q])
+            ya[g, q] = dot(tab_l[2 * q], xr[g, q])
+        yield
         for q in range(2):
             for r in range(0, HALF, 16):
                 rows = pl.ds(q * HALF + r, 16)
                 for c in range(2):
-                    y0 = ya[q, pl.ds(c * HALF + r, 16), pl.ds(0, 128)]
-                    y1 = ya[q, pl.ds(c * HALF + r, 16), pl.ds(128, 128)]
-                    put_cols(xc, 0, rows, c * 128, y0 + y1)
-                    put_cols(xc, 1, rows, c * 128, y0 - y1)
+                    y0 = ya[g, q, pl.ds(c * HALF + r, 16), pl.ds(0, 128)]
+                    y1 = ya[g, q, pl.ds(c * HALF + r, 16), pl.ds(128, 128)]
+                    put_cols(xc.at[g], 0, rows, c * 128, y0 + y1)
+                    put_cols(xc.at[g], 1, rows, c * 128, y0 - y1)
         for u in range(2):
-            yb[u] = dot(xc[u], tab_r[2 * u + 1])
+            yb[g, u] = dot(xc[g, u], tab_r[2 * u + 1])
+        yield
         for u in range(2):
             for r in range(0, W, 16):
                 rows = pl.ds(r, 16)
-                re = yb[u, rows, pl.ds(0, 128)]
-                im = yb[u, rows, pl.ds(128, 128)]
+                re = yb[g, u, rows, pl.ds(0, 128)]
+                im = yb[g, u, rows, pl.ds(128, 128)]
                 power = jnp.maximum(re * re + im * im, FLOOR_SQUARE)
-                keeper = 1.0 - ampq[rows, pl.ds(u * 128, 128)] * lax.rsqrt(power)
-                put_cols(xc, u, rows, 0, re * keeper)
-                put_cols(xc, u, rows, 128, im * keeper)
+                keeper = 1.0 - ampq[g, rows, pl.ds(u * 128, 128)] * lax.rsqrt(power)
+                put_cols(xc.at[g], u, rows, 0, re * keeper)
+                put_cols(xc.at[g], u, rows, 128, im * keeper)
         for u in range(2):
-            ya[u] = dot(xc[u], tab_r[2 * u])
+            ya[g, u] = dot(xc[g, u], tab_r[2 * u])
+        yield
         for q in range(2):
             for r in range(0, HALF, 16):
                 rows = pl.ds(q * HALF + r, 16)
                 for c in range(2):
-                    e = ya[0, rows, pl.ds(c * 128, 128)]
-                    o = ya[1, rows, pl.ds(c * 128, 128)]
-                    put_rows(xr, q, c * HALF + r, pl.ds(0, 128), e + o)
-                    put_rows(xr, q, c * HALF + r, pl.ds(128, 128), e - o)
+                    e = ya[g, 0, rows, pl.ds(c * 128, 128)]
+                    o = ya[g, 1, rows, pl.ds(c * 128, 128)]
+                    put_rows(xr.at[g], q, c * HALF + r, pl.ds(0, 128), e + o)
+                    put_rows(xr.at[g], q, c * HALF + r, pl.ds(128, 128), e - o)
         for q in range(2):
-            yb[q] = dot(tab_l[2 * q + 1], xr[q])
+            yb[g, q] = dot(tab_l[2 * q + 1], xr[g, q])
+        yield
         for r in range(0, HALF, 16):
             for rr in (r, r + HALF):
                 rows = pl.ds(a + rr, 16)
@@ -210,12 +216,12 @@
                 for h in range(2):
                     back = []
                     for c in range(2):
-                        e = yb[0, pl.ds(c * HALF + r, 16), pl.ds(h * 128, 128)]
-                        o = yb[1, pl.ds(c * HALF + r, 16), pl.ds(h * 128, 128)]
+                        e = yb[g, 0, pl.ds(c * HALF + r, 16), pl.ds(h * 128, 128)]
+                        o = yb[g, 1, pl.ds(c * HALF + r, 16), pl.ds(h * 128, 128)]
                         back.append(e + o if rr == r else e - o)
                     br, bi = back
-                    pr = prs[0, h, pl.ds(rr, 16), :]
-                    pi = prs[1, h, pl.ds(rr, 16), :]
+                    pr = prs[g, 0, h, pl.ds(rr, 16), :]
+                    pi = prs[g, 1, h, pl.ds(rr, 16), :]
                     cr = crop(0, h, rr)
                     ci = crop(1, h, rr)
                     drop.append((pr * br + pi * bi, pr * bi - pi * br))
@@ -238,15 +244,20 @@
         copy.start()
         pending.append(copy)
 
+    def run(segments):
+        def step(slot, carry):
+            stages = [slot_stages(g, slot) for g in segments]
+            while stages:
+                stages = [stage for stage in stages if next(stage, stage) is not stage]
+            return carry
+
+        return step
+
+    both = jnp.minimum(counts[0], counts[1])
+    lax.fori_loop(0, both, run((0, 1)), 0)
     for g in range(2):
-
-        def step(slot, carry, g=g):
-            slot_step(g, slot)
-            return carry
-
-        lax.fori_loop(0, counts[g], step, 0)
-        if g == 0:
-            copies[-1].wait()
+        lax.fori_loop(both, counts[g], run((g,)), 0)
+    for g in range(2):
         left = left_out if g == 0 else F32(1.0)
         right = right_out if g == 1 else F32(1.0)
         neighbours = up + down + left + right
@@ -331,14 +342,14 @@
             pltpu.VMEM((2, 2, tiles, edge, 128), F32),
             pltpu.VMEM((2, 2, W, W), F32),
             pltpu.VMEM((2, 2, mid, (tiles - 1) * 128), BF),
-            pltpu.VMEM((2, 3, W + 16, 128), F32),
-            pltpu.VMEM((2, 2, W, 128), F32),
-            pltpu.VMEM((2, 3 * W, W), BF),
-            pltpu.VMEM((2, W, 3 * W), BF),
-            pltpu.VMEM((W, 2 * W), BF),
+            pltpu.VMEM((2, 2, 3, W + 16, 128), F32),
+            pltpu.VMEM((2, 2, 2, W, 128), F32),
+            pltpu.VMEM((2, 2, 3 * W, W), BF),
+            pltpu.VMEM((2, 2, W, 3 * W), BF),
+            pltpu.VMEM((2, W, 2 * W), BF),
+            pltpu.VMEM((2, 2, W, W), F32),
+            pltpu.VMEM((2, 2, W, W), F32),
             pltpu.VMEM((2, W, W), F32),
-            pltpu.VMEM((2, W, W), F32),
-            pltpu.VMEM((W, W), F32),
             pltpu.SemaphoreType.DMA((12,)),
             pltpu.SemaphoreType.DMA((20,)),
         ],
@@ -349,7 +360,7 @@
 
 
 def finish_kernel(
-    out_in, prow_hbm, pcol_hbm, ppup_hbm, up_hbm, down_hbm, left_hbm, right_hbm, endl_hbm, endr_hbm,
+    par, out_in, prow_hbm, pcol_hbm, ppup_hbm, verte_hbm, verto_hbm, sidee_hbm, sideo_hbm, endse_hbm, endso_hbm,
     out_hbm, pup_hbm,
     prow, pcol, ppup, vert, side, ends, rows_out, cols_out, pup_out, sem_in, sem_out,
 ):
@@ -365,13 +376,16 @@
         copy.start()
         ins[name] = copy
 
-    verts = (up_hbm, down_hbm)
-    sides = (left_hbm, right_hbm)
+    verts = (verte_hbm, verto_hbm)
+    sides = (sidee_hbm, sideo_hbm)
+    v_at = (1 - par[0], par[0])
+    s_at = (1 - par[1], par[1])
     for d in range(2):
         get(("side", d), sides[d], side.at[d])
-        get(("ends", d), (endl_hbm, endr_hbm)[d], ends.at[d])
+        get(("ends", d), (endse_hbm, endso_hbm)[d], ends.at[d])
     for t in range(2):
         get(("vert", t), verts[t], vert.at[t])
+    for t in range(2):
         get(("prow", t), prow_hbm.at[t], prow.at[t])
     for d in range(2):
         get(("pcol", d), pcol_hbm.at[d], pcol.at[d])
@@ -383,28 +397,28 @@
         copy.start()
         outs.append(copy)
 
-    ins["ends", 0].wait()
-    ins["ends", 1].wait()
+    for d in range(2):
+        ins["ends", d].wait()
+        ins["side", d].wait()
+        ins["vert", d].wait()
     for t in range(2):
-        ins["vert", t].wait()
         ins["prow", t].wait()
         first = t * high_row
         for c in range(2):
             for k in range(2 * tiles):
-                sub = vert[t, c, :, pl.ds(k * 128, 128)].astype(F32)
+                sub = vert[v_at[t], c, :, pl.ds(k * 128, 128)].astype(F32)
                 if k == tiles - 1 or k == tiles:
-                    sub = sub + vert[t, c, :, pl.ds((2 * tiles - 1 - k) * 128, 128)].astype(F32)
+                    sub = sub + vert[v_at[t], c, :, pl.ds((2 * tiles - 1 - k) * 128, 128)].astype(F32)
                 if k == 0 or k == last:
                     d = 0 if k == 0 else 1
-                    far = vert[t, c, :, pl.ds(2 * edge + 4 * W + d * BAND, BAND)].astype(F32)
-                    sub = sub + (far + ends[d, c, pl.ds(t * BAND, BAND), :].astype(F32))
+                    far = vert[v_at[t], c, :, pl.ds(2 * edge + 4 * W + d * BAND, BAND)].astype(F32)
+                    sub = sub + (far + ends[s_at[d], c, pl.ds(t * BAND, BAND), :].astype(F32))
                 rows_out[t, c, :, pl.ds(k * 128, 128)] = (prow[t, c, k] - 0.5 * sub).astype(BF)
             put(rows_out.at[t, c], out_hbm.at[c, pl.ds(first, BAND), :])
     for d in range(2):
-        ins["side", d].wait()
         ins["pcol", d].wait()
         for c in range(2):
-            sub = side[d, c, pl.ds(0, mid), :].astype(F32)
+            sub = side[s_at[d], c, pl.ds(0, mid), :].astype(F32)
             cols_out[d, c] = (pcol[d, c] - 0.5 * sub).astype(BF)
             put(cols_out.at[d, c], out_hbm.at[c, pl.ds(BAND, mid), pl.ds(d * last * 128, 128)])
     ins["ppup"].wait()
@@ -414,16 +428,16 @@
             for q in range(4):
                 cols = pl.ds(q * 128, 128)
                 d = q // 2
-                sub = side[d, c, pl.ds(mid + (q % 2) * W + half * 128, 128), :].astype(F32)
+                sub = side[s_at[d], c, pl.ds(mid + (q % 2) * W + half * 128, 128), :].astype(F32)
                 for t in range(2):
-                    sub = sub + vert[t, c, :, pl.ds(2 * edge + half * 512 + q * 128, 128)].astype(F32)
+                    sub = sub + vert[v_at[t], c, :, pl.ds(2 * edge + half * 512 + q * 128, 128)].astype(F32)
                 pup_out[c, rows, cols] = ppup[c, rows, cols] - 0.5 * sub
     put(pup_out, pup_hbm)
     for copy in outs:
         copy.wait()
 
 
-def finish(out, prow, pcol, ppup, ups, sides, ends):
+def finish(parity, out, prow, pcol, ppup, ups, sides, ends):
     edge = out.shape[1]
     tiles = edge // 128
     mid = edge - 2 * BAND
@@ -434,9 +448,9 @@
             jax.ShapeDtypeStruct(out.shape, BF),
             jax.ShapeDtypeStruct(ppup.shape, F32),
         ),
-        in_specs=[hbm] * 10,
+        in_specs=[pl.BlockSpec(memory_space=pltpu.SMEM)] + [hbm] * 10,
         out_specs=(hbm, hbm),
-        input_output_aliases={0: 0},
+        input_output_aliases={1: 0},
         scratch_shapes=[
             pltpu.VMEM(prow.shape, F32),
             pltpu.VMEM(pcol.shape, F32),
@@ -453,80 +467,120 @@
         compiler_params=pltpu.CompilerParams(vmem_limit_bytes=FINISH_VMEM),
         cost_estimate=pl.CostEstimate(flops=10_000_000, bytes_accessed=17_000_000, transcendentals=0),
         name="shared_bands",
-    )(out, prow, pcol, ppup, *ups, *sides, *ends)
-
-
-def pack_kernel(spec_hbm, pup_hbm, left_c, right_c, left, right, top, bottom, sem):
+    )(parity, out, prow, pcol, ppup, *ups, *sides, *ends)
+
+
+def pack_kernel(
+    par, spec_hbm, pup_hbm,
+    ends_e, ends_o, side_e, side_o, vert_e, vert_o,
+    ends_v, side_v, vert_v, sem_in, sem_out,
+):
     edge, wide = spec_hbm.shape[1], spec_hbm.shape[2]
     mid = edge - 2 * BAND
-    copies = []
-
-    def put(src, dst):
-        copy = pltpu.make_async_copy(src, dst, sem.at[len(copies)])
+    ins, outs = [], []
+
+    def get(src, dst):
+        copy = pltpu.make_async_copy(src, dst, sem_in.at[len(ins)])
         copy.start()
-        copies.append(copy)
-
-    for ends, msg, first, half in ((left_c, left, 0, 0), (right_c, right, wide - BAND, 1)):
-        cols = pl.ds(first, BAND)
-        put(spec_hbm.at[:, pl.ds(0, BAND), cols], ends.at[:, pl.ds(0, BAND), :])
-        put(spec_hbm.at[:, pl.ds(edge - BAND, BAND), cols], ends.at[:, pl.ds(BAND, BAND), :])
-        put(spec_hbm.at[:, pl.ds(BAND, mid), cols], msg.at[:, pl.ds(0, mid), :])
+        ins.append(copy)
+
+    def right(i):
+        return 1 - par[1] if i == 0 else par[1]
+
+    def low(i):
+        return 1 - par[0] if i == 0 else par[0]
+
+    for i in range(2):
+        cols = pl.ds(pl.multiple_of(right(i) * (wide - BAND), 128), BAND)
+        get(spec_hbm.at[:, pl.ds(0, BAND), cols], ends_v.at[i, :, pl.ds(0, BAND), :])
+        get(spec_hbm.at[:, pl.ds(edge - BAND, BAND), cols], ends_v.at[i, :, pl.ds(BAND, BAND), :])
+    for i in range(2):
+        cols = pl.ds(pl.multiple_of(right(i) * (wide - BAND), 128), BAND)
+        get(spec_hbm.at[:, pl.ds(BAND, mid), cols], side_v.at[i, :, pl.ds(0, mid), :])
         for q in range(2):
-            put(pup_hbm.at[:, :, pl.ds(half * W + q * 128, 128)], msg.at[:, pl.ds(mid + q * W, W), :])
-    for msg, first in ((top, 0), (bottom, edge - BAND)):
-        put(spec_hbm.at[:, pl.ds(first, BAND), :], msg.at[:, :, pl.ds(0, wide)])
+            half = pl.ds(pl.multiple_of(right(i) * W + q * 128, 128), 128)
+            get(pup_hbm.at[:, :, half], side_v.at[i, :, pl.ds(mid + q * W, W), :])
+    for i in range(2):
+        rows = pl.ds(pl.multiple_of(low(i) * (edge - BAND), 128), BAND)
+        get(spec_hbm.at[:, rows, :], vert_v.at[i, :, :, pl.ds(0, wide)])
         for q in range(2):
-            put(pup_hbm.at[:, pl.ds(q * 128, 128), :], msg.at[:, :, pl.ds(wide + q * 2 * W, 2 * W)])
-    for copy in copies:
+            get(pup_hbm.at[:, pl.ds(q * 128, 128), :], vert_v.at[i, :, :, pl.ds(wide + q * 2 * W, 2 * W)])
+    body = wide + 4 * W
+    done = 0
+    for ready, src, dst in (
+        (4, ends_v.at[0], ends_e),
+        (4, ends_v.at[1], ends_o),
+        (7, side_v.at[0], side_e),
+        (10, side_v.at[1], side_o),
+        (13, vert_v.at[0], vert_e.at[:, :, pl.ds(0, body)]),
+        (16, vert_v.at[1], vert_o.at[:, :, pl.ds(0, body)]),
+    ):
+        while done < ready:
+            ins[done].wait()
+            done += 1
+        copy = pltpu.make_async_copy(src, dst, sem_out.at[len(outs)])
+        copy.start()
+        outs.append(copy)
+    for copy in outs:
         copy.wait()
 
 
-def pack(spectrum, pupils):
+def pack(parity, spectrum, pupils):
     edge, wide = spectrum.shape[1], spectrum.shape[2]
     hbm = pl.BlockSpec(memory_space=pl.ANY)
-    ends = jax.ShapeDtypeStruct((2, 2 * BAND, BAND), BF)
-    side = jax.ShapeDtypeStruct((2, edge - 2 * BAND + 2 * W, BAND), BF)
-    vert = jax.ShapeDtypeStruct((2, BAND, wide + 4 * W + 2 * BAND), BF)
+    smem = pl.BlockSpec(memory_space=pltpu.SMEM)
+    ends = (2, 2 * BAND, BAND)
+    side = (2, edge - 2 * BAND + 2 * W, BAND)
+    vert = (2, BAND, wide + 4 * W + 2 * BAND)
     return pl.pallas_call(
         pack_kernel,
-        out_shape=(ends, ends, side, side, vert, vert),
-        in_specs=[hbm, hbm],
+        out_shape=tuple(jax.ShapeDtypeStruct(shape, BF) for shape in (ends, ends, side, side, vert, vert)),
+        in_specs=[smem, hbm, hbm],
         out_specs=(hbm,) * 6,
-        scratch_shapes=[pltpu.SemaphoreType.DMA((16,))],
+        scratch_shapes=[
+            pltpu.VMEM((2,) + ends, BF),
+            pltpu.VMEM((2,) + side, BF),
+            pltpu.VMEM((2, 2, BAND, wide + 4 * W), BF),
+            pltpu.SemaphoreType.DMA((16,)),
+            pltpu.SemaphoreType.DMA((6,)),
+        ],
         compiler_params=pltpu.CompilerParams(vmem_limit_bytes=PACK_VMEM),
         cost_estimate=pl.CostEstimate(flops=1, bytes_accessed=11_000_000, transcendentals=0),
         name="pack",
-    )(spectrum, pupils)
-
-
-def corners_kernel(top_in, bottom_in, left, right, top, bottom, sem):
-    start = top.shape[2] - 2 * BAND
+    )(parity, spectrum, pupils)
+
+
+def corners_kernel(par, e_in, o_in, ends_e, ends_o, vert_e, vert_o, sem):
+    body = vert_e.shape[2] - 2 * BAND
     copies = []
-    for t, msg in enumerate((top, bottom)):
-        for d, src in enumerate((left, right)):
-            copy = pltpu.make_async_copy(
-                src.at[:, pl.ds(t * BAND, BAND), :], msg.at[:, :, pl.ds(start + d * BAND, BAND)], sem.at[2 * t + d]
-            )
+    for i, msg in enumerate((vert_e, vert_o)):
+        low = 1 - par[0] if i == 0 else par[0]
+        rows = pl.ds(pl.multiple_of(low * BAND, 128), BAND)
+        for j, src in enumerate((ends_e, ends_o)):
+            right = 1 - par[1] if j == 0 else par[1]
+            cols = pl.ds(pl.multiple_of(body + right * BAND, 128), BAND)
+            copy = pltpu.make_async_copy(src.at[:, rows, :], msg.at[:, :, cols], sem.at[2 * i + j])
             copy.start()
             copies.append(copy)
     for copy in copies:
         copy.wait()
 
 
-def add_corners(top, bottom, left, right):
+def add_corners(parity, vert_e, vert_o, ends_e, ends_o):
     hbm = pl.BlockSpec(memory_space=pl.ANY)
-    vert = jax.ShapeDtypeStruct(top.shape, BF)
+    smem = pl.BlockSpec(memory_space=pltpu.SMEM)
+    vert = jax.ShapeDtypeStruct(vert_e.shape, BF)
     return pl.pallas_call(
         corners_kernel,
         out_shape=(vert, vert),
-        in_specs=[hbm] * 4,
+        in_specs=[smem] + [hbm] * 4,
         out_specs=(hbm, hbm),
-        input_output_aliases={0: 0, 1: 1},
+        input_output_aliases={1: 0, 2: 1},
         scratch_shapes=[pltpu.SemaphoreType.DMA((4,))],
         compiler_params=pltpu.CompilerParams(vmem_limit_bytes=CORNER_VMEM),
         cost_estimate=pl.CostEstimate(flops=1, bytes_accessed=1_000_000, transcendentals=0),
         name="add_corners",
-    )(top, bottom, left, right)
+    )(parity, vert_e, vert_o, ends_e, ends_o)
 
 
 def local(spectrum, pupils, amplitudes, crop_starts, led_counts):
@@ -535,22 +589,24 @@
     row = lax.axis_index("sy")
     col = lax.axis_index("sx")
 
-    def chain(count, step):
-        return [(i, i + step) for i in range(count) if 0 <= i + step < count]
-
-    left_c, right_c, left, right, top, bottom = pack(spectrum, pupils)
-    ends_left = lax.ppermute(right_c, "sx", chain(cols, 1))
-    ends_right = lax.ppermute(left_c, "sx", chain(cols, -1))
-    from_left = lax.ppermute(right, "sx", chain(cols, 1))
-    from_right = lax.ppermute(left, "sx", chain(cols, -1))
-    top, bottom = add_corners(top, bottom, ends_left, ends_right)
-    from_up = lax.ppermute(bottom, "sy", chain(rows, 1))
-    from_down = lax.ppermute(top, "sy", chain(rows, -1))
+    def swap(value, axis, count, first):
+        pairs = [(i, i + 1) for i in range(first, count - 1, 2)]
+        return lax.ppermute(value, axis, pairs + [(j, i) for i, j in pairs])
+
+    parity = jnp.stack([row % 2, col % 2]).astype(jnp.int32)
+    ends_e, ends_o, side_e, side_o, vert_e, vert_o = pack(parity, spectrum, pupils)
+    ends_e = swap(ends_e, "sx", cols, 0)
+    ends_o = swap(ends_o, "sx", cols, 1)
+    side_e = swap(side_e, "sx", cols, 0)
+    side_o = swap(side_o, "sx", cols, 1)
+    vert_e, vert_o = add_corners(parity, vert_e, vert_o, ends_e, ends_o)
+    vert_o = swap(vert_o, "sy", rows, 1)
+    vert_e = swap(vert_e, "sy", rows, 0)
     weights = jnp.stack([row > 0, row < rows - 1, col > 0, col < cols - 1]).astype(F32)
     out, prow, pcol, ppup = compute(
         spectrum, pupils, amplitudes, crop_starts.reshape(-1), led_counts.reshape(-1), weights
     )
-    return finish(out, prow, pcol, ppup, (from_up, from_down), (from_left, from_right), (ends_left, ends_right))
+    return finish(parity, out, prow, pcol, ppup, (vert_e, vert_o), (side_e, side_o), (ends_e, ends_o))
 
 
 def solution(mesh):

time: 221 us -> 64.6 us (0.29)
  Pallas kernels: 178 us -> 32.9 us
  starting transfers between devices: 26.6 us -> 16.9 us
    pallas_call x2, Pallas kernels: 157 us -> 6.96 us  [the longest x1 5.65 us: pack(): pl.pallas_call(pack_kernel, out_shape=tuple((jax.ShapeDtypeStruct(shape,...]
    ppermute x6, starting transfers between devices: 26.6 us -> 16.9 us  [swap(): return lax.ppermute(value, axis, pairs + [(j, i) for i, j in pairs])]
    pallas_call x1, Pallas kernels: 14.7 us -> 18.6 us  [compute(): pl.pallas_call(compute_kernel, out_shape=(jax.ShapeDtypeStruct(spectrum.s...]
  transfers between devices with their start and end apart: 6 -> 6, of which waited for: 1 -> 1; matrix products, arithmetic and copies ran while one was open for 1% -> 2% of each run, Pallas kernels for 7% -> 31%
where the time goes in v2:
time: 64.6 us; the launch traced here: 64.4 us
  Pallas kernels  32.9 us (51%)
  starting transfers between devices  16.9 us (26%)
  waiting for transfers between devices  11.7 us (18%)
  other arithmetic  1.26 us (2%)
  between operations  0.79 us (1%)
  local copies, waits for them, and re-layouts  0.78 us (1%)
    pallas_call x1, Pallas kernels, compute(): pl.pallas_call(compute_kernel, out_shape=(jax.ShapeDtypeStruct(spectrum.s...  18.6 us
    ppermute x6, starting transfers between devices, swap(): return lax.ppermute(value, axis, pairs + [(j, i) for i, j in pairs])  16.9 us
    ppermute x6, waiting for transfers between devices, swap(): return lax.ppermute(value, axis, pairs + [(j, i) for i, j in pairs])  11.7 us
    pallas_call x1, Pallas kernels, finish(): pl.pallas_call(finish_kernel, out_shape=(jax.ShapeDtypeStruct(out.shape,...  7.32 us
    pallas_call x1, Pallas kernels, pack(): pl.pallas_call(pack_kernel, out_shape=tuple((jax.ShapeDtypeStruct(shape,...  5.65 us
    pallas_call x1, Pallas kernels, add_corners(): pl.pallas_call(corners_kernel, out_shape=(vert, vert), in_specs=[smem] +...  1.3 us
  transfers between devices with their start and end apart: 6, of which 1 were waited for; matrix products, arithmetic and copies ran while one was open for 2% of the time, Pallas kernels for 31%

profile of v2, /device:TPU:6, one launch (start us, length us, event | category | flops | bytes accessed | tf_op | source)
XLA Modules:
  0.0 64.4 jit_solution(11517978513801362496)
XLA Ops:
  0.6 0.7 %pad_add_fusion.par = s32[2]{0:T(128)} fusion(s32[1]{0:T(128)} %bitcast.1, s32[1]{0:T(128)} %bitcast), kind=kLoop, calls=%fused_computation.1 | loop fusion | flops 2 | bytes 16 | tf_op jit(solution)/shard_map/stack | solution.py:596
  1.3 5.7 %pack.1 = (bf16[2,256,128]{2,1,0:T(8,128)(2,1)}, bf16[2,256,128]{2,1,0:T(8,128)(2,1)}, bf16[2,1408,128]{2,1,0:T(8,128)(2,1)}, bf16[2,1408,128]{2,1,0:T(8,128)(2,...) custom-call(s32[2]{0:T(128)} %pad_add_fusion.par, bf16[2,1152,2304]{2,1,0:T(8,128)(2,1)} %spec_hbm.3, ...), custom_call_target="tpu_custom_call" | custom-call | flops 1 | bytes 11000000 | tf_op jit(solution)/shard_map/pack/pallas_call | solution.py:535
  7.0 2.0 %collective-permute-start = (bf16[2,256,128]{2,1,0:T(8,128)(2,1)}, bf16[2,256,128]{2,1,0:T(8,128)(2,1)S(1)}, u32[]{:S(2)}, u32[]{:S(2)}) collective-permute-start(bf16[2,256,128]{2,1,0:T(8,128)(2,1)} %get-tuple-element.20), channel_id=1, source_target_pairs={{0,1},{2,3},{4,5},{6,7},{1,0},{3,2},{5,4},{7,6},{8,9},{10,11},{12,... | collective-permute-start | bytes 393224 | tf_op jit(solution)/shard_map/ppermute | solution.py:594
  9.0 5.3 %collective-permute-start.1 = (bf16[2,256,128]{2,1,0:T(8,128)(2,1)}, bf16[2,256,128]{2,1,0:T(8,128)(2,1)S(1)}, u32[]{:S(2)}, u32[]{:S(2)}) collective-permute-start(bf16[2,256,128]{2,1,0:T(8,128)(2,1)} %get-tuple-element.21), channel_id=1, source_target_pairs={{1,2},{3,4},{5,6},{2,1},{4,3},{6,5},{9,10},{11,12},{13,14},{10,9},... | collective-permute-start | bytes 393224 | tf_op jit(solution)/shard_map/ppermute | solution.py:594
  14.2 0.3 collective-permute-start.4
  14.5 4.0 %collective-permute-start.5 = (bf16[2,1408,128]{2,1,0:T(8,128)(2,1)}, bf16[2,1408,128]{2,1,0:T(8,128)(2,1)}, u32[]{:S(2)}, u32[]{:S(2)}) collective-permute-start(bf16[2,1408,128]{2,1,0:T(8,128)(2,1)} %get-tuple-element.25), channel_id=1, source_target_pairs={{1,2},{3,4},{5,6},{2,1},{4,3},{6,5},{9,10},{11,12},{13,14},{10,9},... | collective-permute-start | bytes 2162696 | tf_op jit(solution)/shard_map/ppermute | solution.py:594
  18.5 0.0 copy-done.3
  18.5 0.1 copy.13
  18.6 0.7 %reshape.10.starts = s32[16]{0:T(128)} reshape(s32[1,2,4,2]{3,2,1,0:T(4,128)S(1)} %copy.13) | data formatting | bytes 128 | tf_op jit(solution)/shard_map/reshape | solution.py:607
  19.3 0.6 add_convert_fusion.weights
  19.9 0.0 collective-permute-done.ends_e.endse_hbm
  19.9 0.0 collective-permute-done.1.ends_o.endso_hbm
  19.9 0.0 copy-start.1
  19.9 0.0 copy-done.2
  19.9 1.3 %add_corners.1 = (bf16[2,128,3584]{2,1,0:T(8,128)(2,1)}, bf16[2,128,3584]{2,1,0:T(8,128)(2,1)}) custom-call(s32[2]{0:T(128)S(1)} %copy-done.2, bf16[2,128,3584]{2,1,0:T(8,128)(2,1)} %get-tuple-element.18.e_in, bf16[2,128,3584]{2,1,0:T(8,128)(2,1)} %get-tuple-element.19.o_in, ...), custom_call_target="tpu_custom_call", output_to_operand_aliasing={{0}: (1, {}), {1}: (2, {})} | custom-call | flops 1 | bytes 1000000 | tf_op jit(solution)/shard_map/add_corners/pallas_call | solution.py:573
  21.3 0.0 copy-done
  21.3 0.1 collective-permute-start.2
  21.4 5.3 %collective-permute-start.3 = (bf16[2,128,3584]{2,1,0:T(8,128)(2,1)}, bf16[2,128,3584]{2,1,0:T(8,128)(2,1)}, u32[]{:S(2)}, u32[]{:S(2)}) collective-permute-start(bf16[2,128,3584]{2,1,0:T(8,128)(2,1)} %get-tuple-element.23), channel_id=1, source_target_pairs={{8,16},{24,32},{40,48},{56,64},{72,80},{88,96},{104,112},{16,8},{3... | collective-permute-start | bytes 5505032 | tf_op jit(solution)/shard_map/ppermute | solution.py:594
  26.7 18.6 %data_terms.1 = (bf16[2,1152,2304]{2,1,0:T(8,128)(2,1)}, f32[2,2,18,128,128]{4,3,2,1,0:T(8,128)}, f32[2,2,896,128]{3,2,1,0:T(8,128)}, f32[2,256,512]{2,1,0:T(8,128)}) custom-call(s32[16]{0:T(128)} %reshape.10.starts, s32[2]{0:T(128)} %bitcast.7, f32[4]{0:T(128)} %add_convert_fusion.weights, bf16[2,1152,2304]{2,1,0:T(8,128)(2,1)} %spec_hbm.3, ...), custom_call_target="tpu_custom_call" | custom-call | flops 20000000000 | bytes 30000000 | tf_op jit(solution)/shard_map/data_terms/pallas_call | solution.py:324
  45.3 0.0 collective-permute-done.4.sidee_hbm
  45.3 0.0 collective-permute-done.5.sideo_hbm
  45.3 0.0 collective-permute-done.2.verte_hbm
  45.3 11.7 %collective-permute-done.3.verto_hbm = bf16[2,128,3584]{2,1,0:T(8,128)(2,1)} collective-permute-done((bf16[2,128,3584]{2,1,0:T(8,128)(2,1)}, bf16[2,128,3584]{2,1,0:T(8,128)(2,1)}, u32[]{:S(2)}, u32[]{:S(2)}) %collective-permute-start.3) | collective-permute-done | bytes 1835040 | tf_op jit(solution)/shard_map/ppermute | solution.py:594
  57.0 7.3 %shared_bands.1 = (bf16[2,1152,2304]{2,1,0:T(8,128)(2,1)}, f32[2,256,512]{2,1,0:T(8,128)}) custom-call(s32[2]{0:T(128)} %pad_add_fusion.par, bf16[2,1152,2304]{2,1,0:T(8,128)(2,1)} %get-tuple-element.14.out_in, f32[2,2,18,128,128]{4,3,2,1,0:T(8,128)} %get-tuple-element.15.prow_hbm, ...), custom_call_target="tpu_custom_call", output_to_operand_aliasing={{0}: (1, {})} | custom-call | flops 10000000 | bytes 17000000 | tf_op jit(solution)/shard_map/shared_bands/pallas_call | solution.py:445
  (4 shorter events, 0.0 us)
Async XLA Ops:
  1.3 17.2 %copy-start.3 = (s32[1,2,4,2]{2,3,1,0:T(2,128)S(1)}, s32[1,2,4,2]{2,3,1,0:T(2,128)}, u32[]{:S(2)}) copy-start(s32[1,2,4,2]{2,3,1,0:T(2,128)} %param.10) | copy-start | bytes 196
  1.3 18.6 %copy-start.2 = (s32[2]{0:T(128)S(1)}, s32[2]{0:T(128)}, u32[]{:S(2)}) copy-start(s32[2]{0:T(128)} %pad_add_fusion.par) | copy-start | bytes 28
  7.0 13.0 %collective-permute-start = (bf16[2,256,128]{2,1,0:T(8,128)(2,1)}, bf16[2,256,128]{2,1,0:T(8,128)(2,1)S(1)}, u32[]{:S(2)}, u32[]{:S(2)}) collective-permute-start(bf16[2,256,128]{2,1,0:T(8,128)(2,1)} %get-tuple-element.20), channel_id=1, source_target_pairs={{0,1},{2,3},{4,5},{6,7},{1,0},{3,2},{5,4},{7,6},{8,9},{10,11},{12,... | collective-permute-start | bytes 393224 | tf_op jit(solution)/shard_map/ppermute | solution.py:594
  9.0 11.0 %collective-permute-start.1 = (bf16[2,256,128]{2,1,0:T(8,128)(2,1)}, bf16[2,256,128]{2,1,0:T(8,128)(2,1)S(1)}, u32[]{:S(2)}, u32[]{:S(2)}) collective-permute-start(bf16[2,256,128]{2,1,0:T(8,128)(2,1)} %get-tuple-element.21), channel_id=1, source_target_pairs={{1,2},{3,4},{5,6},{2,1},{4,3},{6,5},{9,10},{11,12},{13,14},{10,9},... | collective-permute-start | bytes 393224 | tf_op jit(solution)/shard_map/ppermute | solution.py:594
  14.2 31.1 %collective-permute-start.4 = (bf16[2,1408,128]{2,1,0:T(8,128)(2,1)}, bf16[2,1408,128]{2,1,0:T(8,128)(2,1)}, u32[]{:S(2)}, u32[]{:S(2)}) collective-permute-start(bf16[2,1408,128]{2,1,0:T(8,128)(2,1)} %get-tuple-element.24), channel_id=1, source_target_pairs={{0,1},{2,3},{4,5},{6,7},{1,0},{3,2},{5,4},{7,6},{8,9},{10,11},{12,... | collective-permute-start | bytes 2162696 | tf_op jit(solution)/shard_map/ppermute | solution.py:594
  14.5 30.8 %collective-permute-start.5 = (bf16[2,1408,128]{2,1,0:T(8,128)(2,1)}, bf16[2,1408,128]{2,1,0:T(8,128)(2,1)}, u32[]{:S(2)}, u32[]{:S(2)}) collective-permute-start(bf16[2,1408,128]{2,1,0:T(8,128)(2,1)} %get-tuple-element.25), channel_id=1, source_target_pairs={{1,2},{3,4},{5,6},{2,1},{4,3},{6,5},{9,10},{11,12},{13,14},{10,9},... | collective-permute-start | bytes 2162696 | tf_op jit(solution)/shard_map/ppermute | solution.py:594
  19.9 1.3 %copy-start = (bf16[2,256,128]{2,1,0:T(8,128)(2,1)}, bf16[2,256,128]{2,1,0:T(8,128)(2,1)S(1)}, u32[]{:S(2)}) copy-start(bf16[2,256,128]{2,1,0:T(8,128)(2,1)S(1)} %collective-permute-done.ends_e.endse_hbm) | copy-start | bytes 393220
  19.9 1.3 %copy-start.1 = (bf16[2,256,128]{2,1,0:T(8,128)(2,1)}, bf16[2,256,128]{2,1,0:T(8,128)(2,1)S(1)}, u32[]{:S(2)}) copy-start(bf16[2,256,128]{2,1,0:T(8,128)(2,1)S(1)} %collective-permute-done.1.ends_o.endso_hbm) | copy-start | bytes 393220
  21.3 24.1 %collective-permute-start.2 = (bf16[2,128,3584]{2,1,0:T(8,128)(2,1)}, bf16[2,128,3584]{2,1,0:T(8,128)(2,1)}, u32[]{:S(2)}, u32[]{:S(2)}) collective-permute-start(bf16[2,128,3584]{2,1,0:T(8,128)(2,1)} %get-tuple-element.22), channel_id=1, source_target_pairs={{0,8},{16,24},{32,40},{48,56},{64,72},{80,88},{96,104},{112,120},{... | collective-permute-start | bytes 5505032 | tf_op jit(solution)/shard_map/ppermute | solution.py:594
  21.4 35.7 %collective-permute-start.3 = (bf16[2,128,3584]{2,1,0:T(8,128)(2,1)}, bf16[2,128,3584]{2,1,0:T(8,128)(2,1)}, u32[]{:S(2)}, u32[]{:S(2)}) collective-permute-start(bf16[2,128,3584]{2,1,0:T(8,128)(2,1)} %get-tuple-element.23), channel_id=1, source_target_pairs={{8,16},{24,32},{40,48},{56,64},{72,80},{88,96},{104,112},{16,8},{3... | collective-permute-start | bytes 5505032 | tf_op jit(solution)/shard_map/ppermute | solution.py:594

commit v3 on v2

--- a/solution.py
+++ b/solution.py
@@ -15,8 +15,9 @@
 W = 256
 HALF = 128
 FLOOR_SQUARE = 0.0625
+COST_FLOPS = 1000
+COST_BYTES = 1000
 PACK_VMEM = 60 * 1024 * 1024
-CORNER_VMEM = 8 * 1024 * 1024
 FINISH_VMEM = 66500000
 BAND = 2 * H
 BF = jnp.bfloat16
@@ -74,7 +75,7 @@
 
 
 def compute_kernel(
-    starts, counts, weights, spec_hbm, pup_hbm, amp_hbm, tab_hbm, spread_hbm,
+    starts, counts, spec_hbm, pup_hbm, amp_hbm, tab_hbm, spread_hbm,
     out_hbm, prow_hbm, pcol_hbm, ppup_hbm,
     spec, pupb, pup, amp, tab_l, tab_r, spread, acc, pacc, inner,
     win, prs, xr, xc, xa, ya, yb, ampq, sem_in, sem_out,
@@ -236,7 +237,12 @@
                     pacc[g, c, pl.ds(rr, 16), pl.ds(0, 128)] += jnp.where(keep_low, t0, t1)
                     pacc[g, c, pl.ds(rr, 16), pl.ds(128, 128)] += jnp.where(keep_low, t1, t0)
 
-    up, down, left_out, right_out = weights[0], weights[1], weights[2], weights[3]
+    def weight(inside):
+        return jnp.where(inside, F32(1.0), F32(0.0))
+
+    row, col = lax.axis_index("sy"), lax.axis_index("sx")
+    up, down = weight(row > 0), weight(row < lax.axis_size("sy") - 1)
+    left_out, right_out = weight(col > 0), weight(col < lax.axis_size("sx") - 1)
     pending = []
 
     def put(src, dst):
@@ -314,7 +320,7 @@
         copy.wait()
 
 
-def compute(spectrum, pupils, amplitudes, starts, counts, weights):
+def compute(spectrum, pupils, amplitudes, starts, counts):
     edge = spectrum.shape[1]
     tiles = edge // 128
     mid = edge - 2 * BAND
@@ -329,7 +335,7 @@
             jax.ShapeDtypeStruct((2, 2, mid, 128), F32),
             jax.ShapeDtypeStruct(pupils.shape, F32),
         ),
-        in_specs=[smem, smem, smem] + [hbm] * 5,
+        in_specs=[smem, smem] + [hbm] * 5,
         out_specs=(hbm, hbm, hbm, hbm),
         scratch_shapes=[
             pltpu.VMEM((2, 2, edge, edge), BF),
@@ -354,15 +360,16 @@
             pltpu.SemaphoreType.DMA((20,)),
         ],
         compiler_params=pltpu.CompilerParams(vmem_limit_bytes=66500000),
-        cost_estimate=pl.CostEstimate(flops=20_000_000_000, bytes_accessed=30_000_000, transcendentals=0),
+        cost_estimate=pl.CostEstimate(flops=COST_FLOPS, bytes_accessed=COST_BYTES, transcendentals=0),
         name="data_terms",
-    )(starts, counts, weights, spectrum, pupils, amplitudes, jnp.asarray(packed), jnp.asarray(spread))
+    )(starts, counts, spectrum, pupils, amplitudes, jnp.asarray(packed), jnp.asarray(spread))
 
 
 def finish_kernel(
-    par, out_in, prow_hbm, pcol_hbm, ppup_hbm, verte_hbm, verto_hbm, sidee_hbm, sideo_hbm, endse_hbm, endso_hbm,
+    out_in, prow_hbm, pcol_hbm, ppup_hbm, verto_hbm, sidee_hbm, sideo_hbm,
+    maino_hbm, antio_hbm, maine_hbm, antie_hbm, verte_hbm,
     out_hbm, pup_hbm,
-    prow, pcol, ppup, vert, side, ends, rows_out, cols_out, pup_out, sem_in, sem_out,
+    prow, pcol, ppup, vert, side, diag, rows_out, cols_out, pup_out, sem_in, sem_out,
 ):
     edge = out_in.shape[1]
     tiles = edge // 128
@@ -378,15 +385,21 @@
 
     verts = (verte_hbm, verto_hbm)
     sides = (sidee_hbm, sideo_hbm)
-    v_at = (1 - par[0], par[0])
-    s_at = (1 - par[1], par[1])
-    for d in range(2):
-        get(("side", d), sides[d], side.at[d])
-        get(("ends", d), (endse_hbm, endso_hbm)[d], ends.at[d])
-    for t in range(2):
-        get(("vert", t), verts[t], vert.at[t])
-    for t in range(2):
-        get(("prow", t), prow_hbm.at[t], prow.at[t])
+    diags = ((maine_hbm, maino_hbm), (antie_hbm, antio_hbm))
+    odd_row, odd_col = parity_of("sy"), parity_of("sx")
+    v_at = (1 - odd_row, odd_row)
+    s_at = (1 - odd_col, odd_col)
+    for i in range(2):
+        get(("vert", i), verts[i], vert.at[i])
+    for c in range(2):
+        get(("prow", 0, c), prow_hbm.at[0, c], prow.at[0, c])
+    for i in range(2):
+        get(("side", i), sides[i], side.at[i])
+    for j in range(2):
+        for i in range(2):
+            get(("diag", j, i), diags[j][i], diag.at[j, i])
+    for c in range(2):
+        get(("prow", 1, c), prow_hbm.at[1, c], prow.at[1, c])
     for d in range(2):
         get(("pcol", d), pcol_hbm.at[d], pcol.at[d])
     get("ppup", ppup_hbm, ppup)
@@ -397,28 +410,36 @@
         copy.start()
         outs.append(copy)
 
-    for d in range(2):
-        ins["ends", d].wait()
-        ins["side", d].wait()
-        ins["vert", d].wait()
+    def band(t, c, k):
+        sub = vert[v_at[t], c, :, pl.ds(k * 128, 128)].astype(F32)
+        if k == tiles - 1 or k == tiles:
+            sub = sub + vert[v_at[t], c, :, pl.ds((2 * tiles - 1 - k) * 128, 128)].astype(F32)
+        if k == 0 or k == last:
+            d = 0 if k == 0 else 1
+            far = diag[0 if t == d else 1, v_at[t], c].astype(F32)
+            sub = sub + (far + side[s_at[d], c, pl.ds(t * high_row, BAND), :].astype(F32))
+        rows_out[t, c, :, pl.ds(k * 128, 128)] = (prow[t, c, k] - 0.5 * sub).astype(BF)
+
+    for i in range(2):
+        ins["vert", i].wait()
     for t in range(2):
-        ins["prow", t].wait()
-        first = t * high_row
-        for c in range(2):
-            for k in range(2 * tiles):
-                sub = vert[v_at[t], c, :, pl.ds(k * 128, 128)].astype(F32)
-                if k == tiles - 1 or k == tiles:
-                    sub = sub + vert[v_at[t], c, :, pl.ds((2 * tiles - 1 - k) * 128, 128)].astype(F32)
-                if k == 0 or k == last:
-                    d = 0 if k == 0 else 1
-                    far = vert[v_at[t], c, :, pl.ds(2 * edge + 4 * W + d * BAND, BAND)].astype(F32)
-                    sub = sub + (far + ends[s_at[d], c, pl.ds(t * BAND, BAND), :].astype(F32))
-                rows_out[t, c, :, pl.ds(k * 128, 128)] = (prow[t, c, k] - 0.5 * sub).astype(BF)
-            put(rows_out.at[t, c], out_hbm.at[c, pl.ds(first, BAND), :])
+        for c in range(2):
+            ins["prow", t, c].wait()
+            for k in range(1, last):
+                band(t, c, k)
+        if t == 0:
+            for i in range(2):
+                ins["side", i].wait()
+                for j in range(2):
+                    ins["diag", j, i].wait()
+        for c in range(2):
+            band(t, c, 0)
+            band(t, c, last)
+            put(rows_out.at[t, c], out_hbm.at[c, pl.ds(t * high_row, BAND), :])
     for d in range(2):
         ins["pcol", d].wait()
         for c in range(2):
-            sub = side[s_at[d], c, pl.ds(0, mid), :].astype(F32)
+            sub = side[s_at[d], c, pl.ds(BAND, mid), :].astype(F32)
             cols_out[d, c] = (pcol[d, c] - 0.5 * sub).astype(BF)
             put(cols_out.at[d, c], out_hbm.at[c, pl.ds(BAND, mid), pl.ds(d * last * 128, 128)])
     ins["ppup"].wait()
@@ -428,16 +449,16 @@
             for q in range(4):
                 cols = pl.ds(q * 128, 128)
                 d = q // 2
-                sub = side[s_at[d], c, pl.ds(mid + (q % 2) * W + half * 128, 128), :].astype(F32)
+                sub = side[s_at[d], c, pl.ds(edge + (q % 2) * W + half * 128, 128), :].astype(F32)
                 for t in range(2):
                     sub = sub + vert[v_at[t], c, :, pl.ds(2 * edge + half * 512 + q * 128, 128)].astype(F32)
                 pup_out[c, rows, cols] = ppup[c, rows, cols] - 0.5 * sub
-    put(pup_out, pup_hbm)
+        put(pup_out.at[c], pup_hbm.at[c])
     for copy in outs:
         copy.wait()
 
 
-def finish(parity, out, prow, pcol, ppup, ups, sides, ends):
+def finish(out, prow, pcol, ppup, verts, sides, diags):
     edge = out.shape[1]
     tiles = edge // 128
     mid = edge - 2 * BAND
@@ -448,165 +469,138 @@
             jax.ShapeDtypeStruct(out.shape, BF),
             jax.ShapeDtypeStruct(ppup.shape, F32),
         ),
-        in_specs=[pl.BlockSpec(memory_space=pltpu.SMEM)] + [hbm] * 10,
+        in_specs=[hbm] * 12,
         out_specs=(hbm, hbm),
-        input_output_aliases={1: 0},
+        input_output_aliases={0: 0},
         scratch_shapes=[
             pltpu.VMEM(prow.shape, F32),
             pltpu.VMEM(pcol.shape, F32),
             pltpu.VMEM(ppup.shape, F32),
-            pltpu.VMEM((2,) + ups[0].shape, BF),
+            pltpu.VMEM((2,) + verts[0].shape, BF),
             pltpu.VMEM((2,) + sides[0].shape, BF),
-            pltpu.VMEM((2,) + ends[0].shape, BF),
+            pltpu.VMEM((2, 2) + diags[0].shape, BF),
             pltpu.VMEM((2, 2, BAND, 2 * edge), BF),
             pltpu.VMEM((2, 2, mid, 128), BF),
             pltpu.VMEM(ppup.shape, F32),
             pltpu.SemaphoreType.DMA((16,)),
-            pltpu.SemaphoreType.DMA((9,)),
+            pltpu.SemaphoreType.DMA((10,)),
         ],
         compiler_params=pltpu.CompilerParams(vmem_limit_bytes=FINISH_VMEM),
         cost_estimate=pl.CostEstimate(flops=10_000_000, bytes_accessed=17_000_000, transcendentals=0),
         name="shared_bands",
-    )(parity, out, prow, pcol, ppup, *ups, *sides, *ends)
+    )(out, prow, pcol, ppup, verts[1], *sides, diags[1], diags[3], diags[0], diags[2], verts[0])
+
+
+def parity_of(axis):
+    return lax.rem(lax.axis_index(axis), 2)
 
 
 def pack_kernel(
-    par, spec_hbm, pup_hbm,
-    ends_e, ends_o, side_e, side_o, vert_e, vert_o,
-    ends_v, side_v, vert_v, sem_in, sem_out,
+    spec_hbm, pup_hbm,
+    vert_o, side_e, side_o, main_o, anti_o, main_e, anti_e, vert_e,
+    vert_v, side_v, diag_v, sem_in, sem_out,
 ):
     edge, wide = spec_hbm.shape[1], spec_hbm.shape[2]
-    mid = edge - 2 * BAND
+    odd_row, odd_col = parity_of("sy"), parity_of("sx")
+    low = (1 - odd_row, odd_row)
+    right = (1 - odd_col, odd_col)
     ins, outs = [], []
 
     def get(src, dst):
-        copy = pltpu.make_async_copy(src, dst, sem_in.at[len(ins)])
-        copy.start()
-        ins.append(copy)
-
-    def right(i):
-        return 1 - par[1] if i == 0 else par[1]
-
-    def low(i):
-        return 1 - par[0] if i == 0 else par[0]
-
-    for i in range(2):
-        cols = pl.ds(pl.multiple_of(right(i) * (wide - BAND), 128), BAND)
-        get(spec_hbm.at[:, pl.ds(0, BAND), cols], ends_v.at[i, :, pl.ds(0, BAND), :])
-        get(spec_hbm.at[:, pl.ds(edge - BAND, BAND), cols], ends_v.at[i, :, pl.ds(BAND, BAND), :])
-    for i in range(2):
-        cols = pl.ds(pl.multiple_of(right(i) * (wide - BAND), 128), BAND)
-        get(spec_hbm.at[:, pl.ds(BAND, mid), cols], side_v.at[i, :, pl.ds(0, mid), :])
-        for q in range(2):
-            half = pl.ds(pl.multiple_of(right(i) * W + q * 128, 128), 128)
-            get(pup_hbm.at[:, :, half], side_v.at[i, :, pl.ds(mid + q * W, W), :])
-    for i in range(2):
-        rows = pl.ds(pl.multiple_of(low(i) * (edge - BAND), 128), BAND)
-        get(spec_hbm.at[:, rows, :], vert_v.at[i, :, :, pl.ds(0, wide)])
+        for c in range(2):
+            copy = pltpu.make_async_copy(src.at[c], dst.at[c], sem_in.at[len(ins)])
+            copy.start()
+            ins.append(copy)
+
+    def first_row(i):
+        return pl.ds(pl.multiple_of(low[i] * (edge - BAND), 128), BAND)
+
+    def first_col(flag):
+        return pl.ds(pl.multiple_of(flag * (wide - BAND), 128), BAND)
+
+    plan = []
+    for i in (1, 0):
+        get(spec_hbm.at[:, first_row(i), :], vert_v.at[i, :, :, pl.ds(0, wide)])
         for q in range(2):
             get(pup_hbm.at[:, pl.ds(q * 128, 128), :], vert_v.at[i, :, :, pl.ds(wide + q * 2 * W, 2 * W)])
-    body = wide + 4 * W
+        plan.append((len(ins), vert_v.at[i], (vert_e, vert_o)[i]))
+    for i in (1, 0):
+        get(spec_hbm.at[:, :, first_col(right[i])], side_v.at[i, :, pl.ds(0, edge), :])
+        for q in range(2):
+            half = pl.ds(pl.multiple_of(right[i] * W + q * 128, 128), 128)
+            get(pup_hbm.at[:, :, half], side_v.at[i, :, pl.ds(edge + q * W, W), :])
+        plan.append((len(ins), side_v.at[i], (side_e, side_o)[i]))
+    for j, pair in enumerate(((main_e, main_o), (anti_e, anti_o))):
+        for i in range(2):
+            flag = low[i] if j == 0 else 1 - low[i]
+            get(spec_hbm.at[:, first_row(i), first_col(flag)], diag_v.at[j, i])
+            plan.append((len(ins), diag_v.at[j, i], pair[i]))
     done = 0
-    for ready, src, dst in (
-        (4, ends_v.at[0], ends_e),
-        (4, ends_v.at[1], ends_o),
-        (7, side_v.at[0], side_e),
-        (10, side_v.at[1], side_o),
-        (13, vert_v.at[0], vert_e.at[:, :, pl.ds(0, body)]),
-        (16, vert_v.at[1], vert_o.at[:, :, pl.ds(0, body)]),
-    ):
+    for ready, src, dst in plan:
         while done < ready:
             ins[done].wait()
             done += 1
-        copy = pltpu.make_async_copy(src, dst, sem_out.at[len(outs)])
-        copy.start()
-        outs.append(copy)
+        for c in range(2):
+            copy = pltpu.make_async_copy(src.at[c], dst.at[c], sem_out.at[len(outs)])
+            copy.start()
+            outs.append(copy)
     for copy in outs:
         copy.wait()
 
 
-def pack(parity, spectrum, pupils):
+def pack(spectrum, pupils):
     edge, wide = spectrum.shape[1], spectrum.shape[2]
     hbm = pl.BlockSpec(memory_space=pl.ANY)
-    smem = pl.BlockSpec(memory_space=pltpu.SMEM)
-    ends = (2, 2 * BAND, BAND)
-    side = (2, edge - 2 * BAND + 2 * W, BAND)
-    vert = (2, BAND, wide + 4 * W + 2 * BAND)
+    vert = (2, BAND, wide + 4 * W)
+    side = (2, edge + 2 * W, BAND)
+    diag = (2, BAND, BAND)
     return pl.pallas_call(
         pack_kernel,
-        out_shape=tuple(jax.ShapeDtypeStruct(shape, BF) for shape in (ends, ends, side, side, vert, vert)),
-        in_specs=[smem, hbm, hbm],
-        out_specs=(hbm,) * 6,
+        out_shape=tuple(jax.ShapeDtypeStruct(shape, BF) for shape in (vert, side, side, diag, diag, diag, diag, vert)),
+        in_specs=[hbm, hbm],
+        out_specs=(hbm,) * 8,
         scratch_shapes=[
-            pltpu.VMEM((2,) + ends, BF),
+            pltpu.VMEM((2,) + vert, BF),
             pltpu.VMEM((2,) + side, BF),
-            pltpu.VMEM((2, 2, BAND, wide + 4 * W), BF),
+            pltpu.VMEM((2, 2) + diag, BF),
+            pltpu.SemaphoreType.DMA((32,)),
             pltpu.SemaphoreType.DMA((16,)),
-            pltpu.SemaphoreType.DMA((6,)),
         ],
         compiler_params=pltpu.CompilerParams(vmem_limit_bytes=PACK_VMEM),
         cost_estimate=pl.CostEstimate(flops=1, bytes_accessed=11_000_000, transcendentals=0),
         name="pack",
-    )(parity, spectrum, pupils)
-
-
-def corners_kernel(par, e_in, o_in, ends_e, ends_o, vert_e, vert_o, sem):
-    body = vert_e.shape[2] - 2 * BAND
-    copies = []
-    for i, msg in enumerate((vert_e, vert_o)):
-        low = 1 - par[0] if i == 0 else par[0]
-        rows = pl.ds(pl.multiple_of(low * BAND, 128), BAND)
-        for j, src in enumerate((ends_e, ends_o)):
-            right = 1 - par[1] if j == 0 else par[1]
-            cols = pl.ds(pl.multiple_of(body + right * BAND, 128), BAND)
-            copy = pltpu.make_async_copy(src.at[:, rows, :], msg.at[:, :, cols], sem.at[2 * i + j])
-            copy.start()
-            copies.append(copy)
-    for copy in copies:
-        copy.wait()
-
-
-def add_corners(parity, vert_e, vert_o, ends_e, ends_o):
-    hbm = pl.BlockSpec(memory_space=pl.ANY)
-    smem = pl.BlockSpec(memory_space=pltpu.SMEM)
-    vert = jax.ShapeDtypeStruct(vert_e.shape, BF)
-    return pl.pallas_call(
-        corners_kernel,
-        out_shape=(vert, vert),
-        in_specs=[smem] + [hbm] * 4,
-        out_specs=(hbm, hbm),
-        input_output_aliases={1: 0, 2: 1},
-        scratch_shapes=[pltpu.SemaphoreType.DMA((4,))],
-        compiler_params=pltpu.CompilerParams(vmem_limit_bytes=CORNER_VMEM),
-        cost_estimate=pl.CostEstimate(flops=1, bytes_accessed=1_000_000, transcendentals=0),
-        name="add_corners",
-    )(parity, vert_e, vert_o, ends_e, ends_o)
+    )(spectrum, pupils)
 
 
 def local(spectrum, pupils, amplitudes, crop_starts, led_counts):
     rows = lax.axis_size("sy")
     cols = lax.axis_size("sx")
-    row = lax.axis_index("sy")
-    col = lax.axis_index("sx")
 
     def swap(value, axis, count, first):
         pairs = [(i, i + 1) for i in range(first, count - 1, 2)]
         return lax.ppermute(value, axis, pairs + [(j, i) for i, j in pairs])
 
-    parity = jnp.stack([row % 2, col % 2]).astype(jnp.int32)
-    ends_e, ends_o, side_e, side_o, vert_e, vert_o = pack(parity, spectrum, pupils)
-    ends_e = swap(ends_e, "sx", cols, 0)
-    ends_o = swap(ends_o, "sx", cols, 1)
-    side_e = swap(side_e, "sx", cols, 0)
-    side_o = swap(side_o, "sx", cols, 1)
-    vert_e, vert_o = add_corners(parity, vert_e, vert_o, ends_e, ends_o)
-    vert_o = swap(vert_o, "sy", rows, 1)
-    vert_e = swap(vert_e, "sy", rows, 0)
-    weights = jnp.stack([row > 0, row < rows - 1, col > 0, col < cols - 1]).astype(F32)
-    out, prow, pcol, ppup = compute(
-        spectrum, pupils, amplitudes, crop_starts.reshape(-1), led_counts.reshape(-1), weights
+    def swap_diagonal(value, first, step):
+        pairs = [
+            (y * cols + x, (y + 1) * cols + x + step)
+            for y in range(first, rows - 1, 2)
+            for x in range(cols)
+            if 0 <= x + step < cols
+        ]
+        return lax.ppermute(value, ("sy", "sx"), pairs + [(j, i) for i, j in pairs])
+
+    vert_o, side_e, side_o, main_o, anti_o, main_e, anti_e, vert_e = pack(spectrum, pupils)
+    below = swap(vert_o, "sy", rows, 1)
+    sides = (swap(side_e, "sx", cols, 0), swap(side_o, "sx", cols, 1))
+    diags = (
+        swap_diagonal(main_e, 0, 1),
+        swap_diagonal(main_o, 1, 1),
+        swap_diagonal(anti_e, 0, -1),
+        swap_diagonal(anti_o, 1, -1),
     )
-    return finish(parity, out, prow, pcol, ppup, (vert_e, vert_o), (side_e, side_o), (ends_e, ends_o))
+    verts = (swap(vert_e, "sy", rows, 0), below)
+    out, prow, pcol, ppup = compute(spectrum, pupils, amplitudes, crop_starts.reshape(-1), led_counts.reshape(-1))
+    return finish(out, prow, pcol, ppup, verts, sides, diags)
 
 
 def solution(mesh):

time: 64.6 us -> 100 us (1.55)
  the two profiles are of different devices: /device:TPU:6 before, /device:TPU:98 now
where the time goes in v3:
time: 100 us; the launch traced here: 101 us
  waiting for transfers between devices  47.2 us (47%)
  Pallas kernels  34.1 us (34%)
  starting transfers between devices  17.7 us (18%)
  local copies, waits for them, and re-layouts  1.32 us (1%)
    ppermute x4, waiting for transfers between devices, swap_diagonal(): return lax.ppermute(value, ('sy', 'sx'), pairs + [(j, i) for i, j in pairs])  47.2 us
    pallas_call x1, Pallas kernels, compute(): pl.pallas_call(compute_kernel, out_shape=(jax.ShapeDtypeStruct(spectrum.s...  22.1 us
    ppermute x4, starting transfers between devices, swap(): return lax.ppermute(value, axis, pairs + [(j, i) for i, j in pairs])  9.38 us
    ppermute x4, starting transfers between devices, swap_diagonal(): return lax.ppermute(value, ('sy', 'sx'), pairs + [(j, i) for i, j in pairs])  8.29 us
    pallas_call x1, Pallas kernels, finish(): pl.pallas_call(finish_kernel, out_shape=(jax.ShapeDtypeStruct(out.shape,...  6.75 us
    pallas_call x1, Pallas kernels, pack(): pl.pallas_call(pack_kernel, out_shape=tuple((jax.ShapeDtypeStruct(shape,...  5.25 us
  transfers between devices with their start and end apart: 8, of which 3 were waited for; matrix products, arithmetic and copies ran while one was open for 1% of the time, Pallas kernels for 22%

profile of v3, /device:TPU:98, one launch (start us, length us, event | category | flops | bytes accessed | tf_op | source)
XLA Modules:
  0.0 101.2 jit_solution(7331077808678942672)
XLA Ops:
  0.6 0.0 copy-start.4
  0.6 5.3 %pack.1 = (bf16[2,128,3328]{2,1,0:T(8,128)(2,1)}, bf16[2,1664,128]{2,1,0:T(8,128)(2,1)}, bf16[2,1664,128]{2,1,0:T(8,128)(2,1)}, bf16[2,128,128]{2,1,0:T(8,128)(2...) custom-call(bf16[2,1152,2304]{2,1,0:T(8,128)(2,1)} %spec_hbm.3, ...), custom_call_target="tpu_custom_call" | custom-call | flops 1 | bytes 11000000 | tf_op jit(solution)/shard_map/pack/pallas_call | solution.py:557
  5.9 4.3 %collective-permute-start = (bf16[2,128,3328]{2,1,0:T(8,128)(2,1)}, bf16[2,128,3328]{2,1,0:T(8,128)(2,1)}, u32[]{:S(2)}, u32[]{:S(2)}) collective-permute-start(bf16[2,128,3328]{2,1,0:T(8,128)(2,1)} %get-tuple-element.18), channel_id=1, source_target_pairs={{8,16},{24,32},{40,48},{56,64},{72,80},{88,96},{104,112},{16,8},{3... | collective-permute-start | bytes 5111816 | tf_op jit(solution)/shard_map/ppermute | solution.py:581
  10.2 0.1 collective-permute-start.7
  10.3 0.5 collective-permute-start.1
  10.8 4.5 %collective-permute-start.2 = (bf16[2,1664,128]{2,1,0:T(8,128)(2,1)}, bf16[2,1664,128]{2,1,0:T(8,128)(2,1)}, u32[]{:S(2)}, u32[]{:S(2)}) collective-permute-start(bf16[2,1664,128]{2,1,0:T(8,128)(2,1)} %get-tuple-element.20), channel_id=1, source_target_pairs={{1,2},{3,4},{5,6},{2,1},{4,3},{6,5},{9,10},{11,12},{13,14},{10,9},... | collective-permute-start | bytes 2555912 | tf_op jit(solution)/shard_map/ppermute | solution.py:581
  15.3 1.9 %collective-permute-start.3 = (bf16[2,128,128]{2,1,0:T(8,128)(2,1)}, bf16[2,128,128]{2,1,0:T(8,128)(2,1)S(1)}, u32[]{:S(2)}, u32[]{:S(2)}) collective-permute-start(bf16[2,128,128]{2,1,0:T(8,128)(2,1)} %get-tuple-element.21), channel_id=1, source_target_pairs={{8,17},{9,18},{10,19},{11,20},{12,21},{13,22},{14,23},{24,33},{25,... | collective-permute-start | bytes 196616 | tf_op jit(solution)/shard_map/ppermute | solution.py:590
  17.2 32.3 %collective-permute-done.3.maino_hbm = bf16[2,128,128]{2,1,0:T(8,128)(2,1)S(1)} collective-permute-done((bf16[2,128,128]{2,1,0:T(8,128)(2,1)}, bf16[2,128,128]{2,1,0:T(8,128)(2,1)S(1)}, u32[]{:S(2)}, u32[]{:S(2)}) %collective-permute-start.3) | collective-permute-done | bytes 65568 | tf_op jit(solution)/shard_map/ppermute | solution.py:590
  49.5 2.6 %collective-permute-start.4 = (bf16[2,128,128]{2,1,0:T(8,128)(2,1)}, bf16[2,128,128]{2,1,0:T(8,128)(2,1)S(1)}, u32[]{:S(2)}, u32[]{:S(2)}) collective-permute-start(bf16[2,128,128]{2,1,0:T(8,128)(2,1)} %get-tuple-element.22), channel_id=1, source_target_pairs={{9,16},{10,17},{11,18},{12,19},{13,20},{14,21},{15,22},{25,32},{26... | collective-permute-start | bytes 196616 | tf_op jit(solution)/shard_map/ppermute | solution.py:590
  52.1 7.4 %collective-permute-done.4.antio_hbm = bf16[2,128,128]{2,1,0:T(8,128)(2,1)S(1)} collective-permute-done((bf16[2,128,128]{2,1,0:T(8,128)(2,1)}, bf16[2,128,128]{2,1,0:T(8,128)(2,1)S(1)}, u32[]{:S(2)}, u32[]{:S(2)}) %collective-permute-start.4) | collective-permute-done | bytes 65568 | tf_op jit(solution)/shard_map/ppermute | solution.py:590
  59.6 1.9 %collective-permute-start.5 = (bf16[2,128,128]{2,1,0:T(8,128)(2,1)}, bf16[2,128,128]{2,1,0:T(8,128)(2,1)S(1)}, u32[]{:S(2)}, u32[]{:S(2)}) collective-permute-start(bf16[2,128,128]{2,1,0:T(8,128)(2,1)} %get-tuple-element.23), channel_id=1, source_target_pairs={{0,9},{1,10},{2,11},{3,12},{4,13},{5,14},{6,15},{16,25},{17,26},{1... | collective-permute-start | bytes 196616 | tf_op jit(solution)/shard_map/ppermute | solution.py:590
  61.5 7.5 %collective-permute-done.5.maine_hbm = bf16[2,128,128]{2,1,0:T(8,128)(2,1)S(1)} collective-permute-done((bf16[2,128,128]{2,1,0:T(8,128)(2,1)}, bf16[2,128,128]{2,1,0:T(8,128)(2,1)S(1)}, u32[]{:S(2)}, u32[]{:S(2)}) %collective-permute-start.5) | collective-permute-done | bytes 65568 | tf_op jit(solution)/shard_map/ppermute | solution.py:590
  69.0 1.9 %collective-permute-start.6 = (bf16[2,128,128]{2,1,0:T(8,128)(2,1)}, bf16[2,128,128]{2,1,0:T(8,128)(2,1)S(1)}, u32[]{:S(2)}, u32[]{:S(2)}) collective-permute-start(bf16[2,128,128]{2,1,0:T(8,128)(2,1)} %get-tuple-element.24), channel_id=1, source_target_pairs={{1,8},{2,9},{3,10},{4,11},{5,12},{6,13},{7,14},{17,24},{18,25},{19... | collective-permute-start | bytes 196616 | tf_op jit(solution)/shard_map/ppermute | solution.py:590
  70.9 0.1 copy.11
  71.0 0.6 reshape.10.starts
  71.6 22.1 %data_terms.1 = (bf16[2,1152,2304]{2,1,0:T(8,128)(2,1)}, f32[2,2,18,128,128]{4,3,2,1,0:T(8,128)}, f32[2,2,896,128]{3,2,1,0:T(8,128)}, f32[2,256,512]{2,1,0:T(8,128)}) custom-call(s32[16]{0:T(128)} %reshape.10.starts, s32[2]{0:T(128)} %bitcast.1, bf16[2,1152,2304]{2,1,0:T(8,128)(2,1)} %spec_hbm.3, bf16[2,256,512]{2,1,0:T(8,128)(2,1)} %pup_hbm.3, ...), custom_call_target="tpu_custom_call" | custom-call | flops 1000 | bytes 1000 | tf_op jit(solution)/shard_map/data_terms/pallas_call | solution.py:330
  93.7 0.0 copy-done
  93.8 0.0 collective-permute-done.6.antie_hbm
  93.8 0.0 collective-permute-done.1.sidee_hbm
  93.8 0.0 collective-permute-done.2.sideo_hbm
  93.8 0.0 collective-permute-done.verto_hbm
  93.8 0.0 collective-permute-done.7.verte_hbm
  93.8 0.6 copy-done.3
  94.4 6.7 %shared_bands.1 = (bf16[2,1152,2304]{2,1,0:T(8,128)(2,1)}, f32[2,256,512]{2,1,0:T(8,128)}) custom-call(bf16[2,1152,2304]{2,1,0:T(8,128)(2,1)} %get-tuple-element.14.out_in, f32[2,2,18,128,128]{4,3,2,1,0:T(8,128)} %get-tuple-element.15.prow_hbm, f32[2,2,896,128]{3,2,1,0:T(8,128)} %get-tuple-element.16.pcol_hbm, ...), custom_call_target="tpu_custom_call", output_to_operand_aliasing={{0}: (0, {})} | custom-call | flops 10000000 | bytes 17000000 | tf_op jit(solution)/shard_map/shared_bands/pallas_call | solution.py:466
  (7 shorter events, 0.0 us)
Async XLA Ops:
  0.6 70.2 %copy-start.4 = (s32[1,2,4,2]{2,3,1,0:T(2,128)S(1)}, s32[1,2,4,2]{2,3,1,0:T(2,128)}, u32[]{:S(2)}) copy-start(s32[1,2,4,2]{2,3,1,0:T(2,128)} %param.10) | copy-start | bytes 196
  5.9 87.9 %collective-permute-start = (bf16[2,128,3328]{2,1,0:T(8,128)(2,1)}, bf16[2,128,3328]{2,1,0:T(8,128)(2,1)}, u32[]{:S(2)}, u32[]{:S(2)}) collective-permute-start(bf16[2,128,3328]{2,1,0:T(8,128)(2,1)} %get-tuple-element.18), channel_id=1, source_target_pairs={{8,16},{24,32},{40,48},{56,64},{72,80},{88,96},{104,112},{16,8},{3... | collective-permute-start | bytes 5111816 | tf_op jit(solution)/shard_map/ppermute | solution.py:581
  10.2 83.6 %collective-permute-start.7 = (bf16[2,128,3328]{2,1,0:T(8,128)(2,1)}, bf16[2,128,3328]{2,1,0:T(8,128)(2,1)}, u32[]{:S(2)}, u32[]{:S(2)}) collective-permute-start(bf16[2,128,3328]{2,1,0:T(8,128)(2,1)} %get-tuple-element.25), channel_id=1, source_target_pairs={{0,8},{16,24},{32,40},{48,56},{64,72},{80,88},{96,104},{112,120},{... | collective-permute-start | bytes 5111816 | tf_op jit(solution)/shard_map/ppermute | solution.py:581
  10.3 83.4 %collective-permute-start.1 = (bf16[2,1664,128]{2,1,0:T(8,128)(2,1)}, bf16[2,1664,128]{2,1,0:T(8,128)(2,1)}, u32[]{:S(2)}, u32[]{:S(2)}) collective-permute-start(bf16[2,1664,128]{2,1,0:T(8,128)(2,1)} %get-tuple-element.19), channel_id=1, source_target_pairs={{0,1},{2,3},{4,5},{6,7},{1,0},{3,2},{5,4},{7,6},{8,9},{10,11},{12,... | collective-permute-start | bytes 2555912 | tf_op jit(solution)/shard_map/ppermute | solution.py:581
  10.8 83.0 %collective-permute-start.2 = (bf16[2,1664,128]{2,1,0:T(8,128)(2,1)}, bf16[2,1664,128]{2,1,0:T(8,128)(2,1)}, u32[]{:S(2)}, u32[]{:S(2)}) collective-permute-start(bf16[2,1664,128]{2,1,0:T(8,128)(2,1)} %get-tuple-element.20), channel_id=1, source_target_pairs={{1,2},{3,4},{5,6},{2,1},{4,3},{6,5},{9,10},{11,12},{13,14},{10,9},... | collective-permute-start | bytes 2555912 | tf_op jit(solution)/shard_map/ppermute | solution.py:581
  15.3 34.2 %collective-permute-start.3 = (bf16[2,128,128]{2,1,0:T(8,128)(2,1)}, bf16[2,128,128]{2,1,0:T(8,128)(2,1)S(1)}, u32[]{:S(2)}, u32[]{:S(2)}) collective-permute-start(bf16[2,128,128]{2,1,0:T(8,128)(2,1)} %get-tuple-element.21), channel_id=1, source_target_pairs={{8,17},{9,18},{10,19},{11,20},{12,21},{13,22},{14,23},{24,33},{25,... | collective-permute-start | bytes 196616 | tf_op jit(solution)/shard_map/ppermute | solution.py:590
  49.5 44.2 %copy-start = (bf16[2,128,128]{2,1,0:T(8,128)(2,1)}, bf16[2,128,128]{2,1,0:T(8,128)(2,1)S(1)}, u32[]{:S(2)}) copy-start(bf16[2,128,128]{2,1,0:T(8,128)(2,1)S(1)} %collective-permute-done.3.maino_hbm) | copy-start | bytes 196612
  49.5 10.0 %collective-permute-start.4 = (bf16[2,128,128]{2,1,0:T(8,128)(2,1)}, bf16[2,128,128]{2,1,0:T(8,128)(2,1)S(1)}, u32[]{:S(2)}, u32[]{:S(2)}) collective-permute-start(bf16[2,128,128]{2,1,0:T(8,128)(2,1)} %get-tuple-element.22), channel_id=1, source_target_pairs={{9,16},{10,17},{11,18},{12,19},{13,20},{14,21},{15,22},{25,32},{26... | collective-permute-start | bytes 196616 | tf_op jit(solution)/shard_map/ppermute | solution.py:590
  59.5 34.2 %copy-start.1 = (bf16[2,128,128]{2,1,0:T(8,128)(2,1)}, bf16[2,128,128]{2,1,0:T(8,128)(2,1)S(1)}, u32[]{:S(2)}) copy-start(bf16[2,128,128]{2,1,0:T(8,128)(2,1)S(1)} %collective-permute-done.4.antio_hbm) | copy-start | bytes 196612
  59.6 9.4 %collective-permute-start.5 = (bf16[2,128,128]{2,1,0:T(8,128)(2,1)}, bf16[2,128,128]{2,1,0:T(8,128)(2,1)S(1)}, u32[]{:S(2)}, u32[]{:S(2)}) collective-permute-start(bf16[2,128,128]{2,1,0:T(8,128)(2,1)} %get-tuple-element.23), channel_id=1, source_target_pairs={{0,9},{1,10},{2,11},{3,12},{4,13},{5,14},{6,15},{16,25},{17,26},{1... | collective-permute-start | bytes 196616 | tf_op jit(solution)/shard_map/ppermute | solution.py:590
  68.9 24.8 %copy-start.2 = (bf16[2,128,128]{2,1,0:T(8,128)(2,1)}, bf16[2,128,128]{2,1,0:T(8,128)(2,1)S(1)}, u32[]{:S(2)}) copy-start(bf16[2,128,128]{2,1,0:T(8,128)(2,1)S(1)} %collective-permute-done.5.maine_hbm) | copy-start | bytes 196612
  69.0 24.8 %collective-permute-start.6 = (bf16[2,128,128]{2,1,0:T(8,128)(2,1)}, bf16[2,128,128]{2,1,0:T(8,128)(2,1)S(1)}, u32[]{:S(2)}, u32[]{:S(2)}) collective-permute-start(bf16[2,128,128]{2,1,0:T(8,128)(2,1)} %get-tuple-element.24), channel_id=1, source_target_pairs={{1,8},{2,9},{3,10},{4,11},{5,12},{6,13},{7,14},{17,24},{18,25},{19... | collective-permute-start | bytes 196616 | tf_op jit(solution)/shard_map/ppermute | solution.py:590
  93.8 0.6 copy-start.3

commit v4 on v3

--- a/solution.py
+++ b/solution.py
@@ -15,10 +15,11 @@
 W = 256
 HALF = 128
 FLOOR_SQUARE = 0.0625
-COST_FLOPS = 1000
-COST_BYTES = 1000
-PACK_VMEM = 60 * 1024 * 1024
-FINISH_VMEM = 66500000
+COST_FLOPS = 20_000_000_000
+COST_BYTES = 30_000_000
+FULL_VMEM = 60 * 1024 * 1024
+DATA_VMEM = 53 * 1024 * 1024
+FINISH_VMEM = 24 * 1024 * 1024
 BAND = 2 * H
 BF = jnp.bfloat16
 F32 = jnp.float32
@@ -76,8 +77,8 @@
 
 def compute_kernel(
     starts, counts, spec_hbm, pup_hbm, amp_hbm, tab_hbm, spread_hbm,
-    out_hbm, prow_hbm, pcol_hbm, ppup_hbm,
-    spec, pupb, pup, amp, tab_l, tab_r, spread, acc, pacc, inner,
+    out_hbm, prow, pcol, ppup,
+    spec, pupb, pup, amp, tab_l, tab_r, spread, acc, pacc,
     win, prs, xr, xc, xa, ya, yb, ampq, sem_in, sem_out,
 ):
     edge = spec.shape[2]
@@ -263,13 +264,34 @@
     lax.fori_loop(0, both, run((0, 1)), 0)
     for g in range(2):
         lax.fori_loop(both, counts[g], run((g,)), 0)
+    for c in range(2):
+
+        def finish(i, carry, c=c):
+            rows = pl.ds(pl.multiple_of(low_row + i * 64, 64), 64)
+            for k in range(1, tiles - 1):
+                for g in range(2):
+                    spec[g, c, rows, pl.ds(k * 128, 128)] = acc[g, c, k, rows, :].astype(BF)
+            end = pl.ds((tiles - 1) * 128, 128)
+            start = pl.ds(0, 128)
+            gap = 0.5 * (spec[0, c, rows, end].astype(F32) - spec[1, c, rows, start].astype(F32))
+            spec[0, c, rows, end] = (acc[0, c, tiles - 1, rows, :] + gap).astype(BF)
+            spec[1, c, rows, start] = (acc[1, c, 0, rows, :] - gap).astype(BF)
+            return carry
+
+        lax.fori_loop(0, mid // 64, finish, 0)
+        for g in range(2):
+            first_tile = 1 - g
+            cols = (tiles - 1) * 128
+            put(
+                spec.at[g, c, pl.ds(low_row, mid), pl.ds(first_tile * 128, cols)],
+                out_hbm.at[c, pl.ds(low_row, mid), pl.ds((g * tiles + first_tile) * 128, cols)],
+            )
     for g in range(2):
         left = left_out if g == 0 else F32(1.0)
         right = right_out if g == 1 else F32(1.0)
         neighbours = up + down + left + right
         for c in range(2):
-            pacc[g, c] = pacc[g, c] + 0.5 * (neighbours * pup[g, c] - pup[1 - g, c])
-            put(pacc.at[g, c], ppup_hbm.at[c, :, pl.ds(g * W, W)])
+            ppup[c, :, pl.ds(g * W, W)] = pacc[g, c] + 0.5 * (neighbours * pup[g, c] - pup[1 - g, c])
         for c in range(2):
             for k in range(tiles):
                 side = left if k == 0 else right if k == tiles - 1 else None
@@ -281,41 +303,18 @@
                     if local:
                         other = spec[1 - g, c, pl.ds(first, BAND), pl.ds((tiles - 1 - k) * 128, 128)].astype(F32)
                         add = add - 0.5 * other
-                    acc[g, c, k, pl.ds(first, BAND), :] += add
-            for t, first in enumerate((0, high_row)):
-                put(acc.at[g, c, :, pl.ds(first, BAND), :], prow_hbm.at[t, c, pl.ds(g * tiles, tiles)])
+                    prow[t, c, g * tiles + k] = acc[g, c, k, pl.ds(first, BAND), :] + add
         k_out = 0 if g == 0 else tiles - 1
         w_out = left_out if g == 0 else right_out
         for c in range(2):
 
             def outer(i, carry, c=c):
                 rows = pl.ds(pl.multiple_of(low_row + i * 128, 128), 128)
-                acc[g, c, k_out, rows, :] += (0.5 * w_out) * spec[g, c, rows, pl.ds(k_out * 128, 128)].astype(F32)
+                add = (0.5 * w_out) * spec[g, c, rows, pl.ds(k_out * 128, 128)].astype(F32)
+                pcol[g, c, pl.ds(pl.multiple_of(i * 128, 128), 128), :] = acc[g, c, k_out, rows, :] + add
                 return carry
 
             lax.fori_loop(0, mid // 128, outer, 0)
-            put(acc.at[g, c, k_out, pl.ds(low_row, mid), :], pcol_hbm.at[g, c])
-        k_in = tiles - 1 if g == 0 else 0
-        first_tile = 1 if g == 0 else 0
-        for c in range(2):
-
-            def finish(i, carry, c=c):
-                rows = pl.ds(pl.multiple_of(low_row + i * 64, 64), 64)
-                dst = pl.ds(pl.multiple_of(i * 64, 64), 64)
-                for k in range(first_tile, first_tile + tiles - 1):
-                    v = acc[g, c, k, rows, :]
-                    if k == k_in:
-                        own = spec[g, c, rows, pl.ds(k * 128, 128)].astype(F32)
-                        other = spec[1 - g, c, rows, pl.ds((tiles - 1 - k) * 128, 128)].astype(F32)
-                        v = v + 0.5 * (own - other)
-                    inner[g, c, dst, pl.ds((k - first_tile) * 128, 128)] = v.astype(BF)
-                return carry
-
-            lax.fori_loop(0, mid // 64, finish, 0)
-            put(
-                inner.at[g, c],
-                out_hbm.at[c, pl.ds(low_row, mid), pl.ds((g * tiles + first_tile) * 128, (tiles - 1) * 128)],
-            )
     for copy in pending:
         copy.wait()
 
@@ -327,16 +326,17 @@
     packed, spread = tables()
     hbm = pl.BlockSpec(memory_space=pl.ANY)
     smem = pl.BlockSpec(memory_space=pltpu.SMEM)
+    vmem = pl.BlockSpec(memory_space=pltpu.VMEM)
     return pl.pallas_call(
         compute_kernel,
         out_shape=(
             jax.ShapeDtypeStruct(spectrum.shape, BF),
-            jax.ShapeDtypeStruct((2, 2, 2 * tiles, BAND, 128), F32),
-            jax.ShapeDtypeStruct((2, 2, mid, 128), F32),
-            jax.ShapeDtypeStruct(pupils.shape, F32),
+            pltpu.VMEM((2, 2, 2 * tiles, BAND, 128), F32),
+            pltpu.VMEM((2, 2, mid, 128), F32),
+            pltpu.VMEM(pupils.shape, F32),
         ),
         in_specs=[smem, smem] + [hbm] * 5,
-        out_specs=(hbm, hbm, hbm, hbm),
+        out_specs=(hbm, vmem, vmem, vmem),
         scratch_shapes=[
             pltpu.VMEM((2, 2, edge, edge), BF),
             pltpu.VMEM((2, W, 2 * W), BF),
@@ -347,7 +347,6 @@
             pltpu.VMEM((2 * W, W), BF),
             pltpu.VMEM((2, 2, tiles, edge, 128), F32),
             pltpu.VMEM((2, 2, W, W), F32),
-            pltpu.VMEM((2, 2, mid, (tiles - 1) * 128), BF),
             pltpu.VMEM((2, 2, 3, W + 16, 128), F32),
             pltpu.VMEM((2, 2, 2, W, 128), F32),
             pltpu.VMEM((2, 2, 3 * W, W), BF),
@@ -357,19 +356,18 @@
             pltpu.VMEM((2, 2, W, W), F32),
             pltpu.VMEM((2, W, W), F32),
             pltpu.SemaphoreType.DMA((12,)),
-            pltpu.SemaphoreType.DMA((20,)),
+            pltpu.SemaphoreType.DMA((4,)),
         ],
-        compiler_params=pltpu.CompilerParams(vmem_limit_bytes=66500000),
+        compiler_params=pltpu.CompilerParams(vmem_limit_bytes=DATA_VMEM),
         cost_estimate=pl.CostEstimate(flops=COST_FLOPS, bytes_accessed=COST_BYTES, transcendentals=0),
         name="data_terms",
     )(starts, counts, spectrum, pupils, amplitudes, jnp.asarray(packed), jnp.asarray(spread))
 
 
 def finish_kernel(
-    out_in, prow_hbm, pcol_hbm, ppup_hbm, verto_hbm, sidee_hbm, sideo_hbm,
-    maino_hbm, antio_hbm, maine_hbm, antie_hbm, verte_hbm,
+    out_in, prow, pcol, ppup, verte_hbm, verto_hbm, sidee_hbm, sideo_hbm, endse_hbm, endso_hbm,
     out_hbm, pup_hbm,
-    prow, pcol, ppup, vert, side, diag, rows_out, cols_out, pup_out, sem_in, sem_out,
+    vert, side, ends, rows_out, cols_out, pup_out, sem_in, sem_out,
 ):
     edge = out_in.shape[1]
     tiles = edge // 128
@@ -385,24 +383,14 @@
 
     verts = (verte_hbm, verto_hbm)
     sides = (sidee_hbm, sideo_hbm)
-    diags = ((maine_hbm, maino_hbm), (antie_hbm, antio_hbm))
     odd_row, odd_col = parity_of("sy"), parity_of("sx")
     v_at = (1 - odd_row, odd_row)
     s_at = (1 - odd_col, odd_col)
-    for i in range(2):
-        get(("vert", i), verts[i], vert.at[i])
     for c in range(2):
-        get(("prow", 0, c), prow_hbm.at[0, c], prow.at[0, c])
-    for i in range(2):
-        get(("side", i), sides[i], side.at[i])
-    for j in range(2):
         for i in range(2):
-            get(("diag", j, i), diags[j][i], diag.at[j, i])
-    for c in range(2):
-        get(("prow", 1, c), prow_hbm.at[1, c], prow.at[1, c])
-    for d in range(2):
-        get(("pcol", d), pcol_hbm.at[d], pcol.at[d])
-    get("ppup", ppup_hbm, ppup)
+            get(("vert", i, c), verts[i].at[c], vert.at[i, c])
+            get(("side", i, c), sides[i].at[c], side.at[i, c])
+            get(("ends", i, c), (endse_hbm, endso_hbm)[i].at[c], ends.at[i, c])
     outs = []
 
     def put(src, dst):
@@ -416,40 +404,28 @@
             sub = sub + vert[v_at[t], c, :, pl.ds((2 * tiles - 1 - k) * 128, 128)].astype(F32)
         if k == 0 or k == last:
             d = 0 if k == 0 else 1
-            far = diag[0 if t == d else 1, v_at[t], c].astype(F32)
-            sub = sub + (far + side[s_at[d], c, pl.ds(t * high_row, BAND), :].astype(F32))
+            far = vert[v_at[t], c, :, pl.ds(2 * edge + 4 * W + d * BAND, BAND)].astype(F32)
+            sub = sub + (far + ends[s_at[d], c, pl.ds(t * BAND, BAND), :].astype(F32))
         rows_out[t, c, :, pl.ds(k * 128, 128)] = (prow[t, c, k] - 0.5 * sub).astype(BF)
 
-    for i in range(2):
-        ins["vert", i].wait()
-    for t in range(2):
-        for c in range(2):
-            ins["prow", t, c].wait()
-            for k in range(1, last):
+    for c in range(2):
+        for i in range(2):
+            for name in ("vert", "side", "ends"):
+                ins[name, i, c].wait()
+        for t in range(2):
+            for k in range(last + 1):
                 band(t, c, k)
-        if t == 0:
-            for i in range(2):
-                ins["side", i].wait()
-                for j in range(2):
-                    ins["diag", j, i].wait()
-        for c in range(2):
-            band(t, c, 0)
-            band(t, c, last)
             put(rows_out.at[t, c], out_hbm.at[c, pl.ds(t * high_row, BAND), :])
-    for d in range(2):
-        ins["pcol", d].wait()
-        for c in range(2):
-            sub = side[s_at[d], c, pl.ds(BAND, mid), :].astype(F32)
+        for d in range(2):
+            sub = side[s_at[d], c, pl.ds(0, mid), :].astype(F32)
             cols_out[d, c] = (pcol[d, c] - 0.5 * sub).astype(BF)
             put(cols_out.at[d, c], out_hbm.at[c, pl.ds(BAND, mid), pl.ds(d * last * 128, 128)])
-    ins["ppup"].wait()
-    for c in range(2):
         for half in range(2):
             rows = pl.ds(half * 128, 128)
             for q in range(4):
                 cols = pl.ds(q * 128, 128)
                 d = q // 2
-                sub = side[s_at[d], c, pl.ds(edge + (q % 2) * W + half * 128, 128), :].astype(F32)
+                sub = side[s_at[d], c, pl.ds(mid + (q % 2) * W + half * 128, 128), :].astype(F32)
                 for t in range(2):
                     sub = sub + vert[v_at[t], c, :, pl.ds(2 * edge + half * 512 + q * 128, 128)].astype(F32)
                 pup_out[c, rows, cols] = ppup[c, rows, cols] - 0.5 * sub
@@ -458,27 +434,25 @@
         copy.wait()
 
 
-def finish(out, prow, pcol, ppup, verts, sides, diags):
+def finish(out, prow, pcol, ppup, verts, sides, ends):
     edge = out.shape[1]
     tiles = edge // 128
     mid = edge - 2 * BAND
     hbm = pl.BlockSpec(memory_space=pl.ANY)
+    vmem = pl.BlockSpec(memory_space=pltpu.VMEM)
     return pl.pallas_call(
         finish_kernel,
         out_shape=(
             jax.ShapeDtypeStruct(out.shape, BF),
             jax.ShapeDtypeStruct(ppup.shape, F32),
         ),
-        in_specs=[hbm] * 12,
+        in_specs=[hbm] + [vmem] * 3 + [hbm] * 6,
         out_specs=(hbm, hbm),
         input_output_aliases={0: 0},
         scratch_shapes=[
-            pltpu.VMEM(prow.shape, F32),
-            pltpu.VMEM(pcol.shape, F32),
-            pltpu.VMEM(ppup.shape, F32),
             pltpu.VMEM((2,) + verts[0].shape, BF),
             pltpu.VMEM((2,) + sides[0].shape, BF),
-            pltpu.VMEM((2, 2) + diags[0].shape, BF),
+            pltpu.VMEM((2,) + ends[0].shape, BF),
             pltpu.VMEM((2, 2, BAND, 2 * edge), BF),
             pltpu.VMEM((2, 2, mid, 128), BF),
             pltpu.VMEM(ppup.shape, F32),
@@ -488,23 +462,27 @@
         compiler_params=pltpu.CompilerParams(vmem_limit_bytes=FINISH_VMEM),
         cost_estimate=pl.CostEstimate(flops=10_000_000, bytes_accessed=17_000_000, transcendentals=0),
         name="shared_bands",
-    )(out, prow, pcol, ppup, verts[1], *sides, diags[1], diags[3], diags[0], diags[2], verts[0])
+    )(out, prow, pcol, ppup, *verts, *sides, *ends)
 
 
 def parity_of(axis):
     return lax.rem(lax.axis_index(axis), 2)
 
 
-def pack_kernel(
-    spec_hbm, pup_hbm,
-    vert_o, side_e, side_o, main_o, anti_o, main_e, anti_e, vert_e,
-    vert_v, side_v, diag_v, sem_in, sem_out,
-):
+def row_start(flag, edge):
+    return pl.ds(pl.multiple_of(flag * (edge - BAND), 128), BAND)
+
+
+def both_ways(axis):
+    odd = parity_of(axis)
+    return 1 - odd, odd
+
+
+def sides_kernel(spec_hbm, pup_hbm, ends_e, ends_o, side_e, side_o, ends_v, side_v, sem_in, sem_out):
     edge, wide = spec_hbm.shape[1], spec_hbm.shape[2]
-    odd_row, odd_col = parity_of("sy"), parity_of("sx")
-    low = (1 - odd_row, odd_row)
-    right = (1 - odd_col, odd_col)
-    ins, outs = [], []
+    mid = edge - 2 * BAND
+    right = both_ways("sx")
+    ins, outs, plan = [], [], []
 
     def get(src, dst):
         for c in range(2):
@@ -512,29 +490,21 @@
             copy.start()
             ins.append(copy)
 
-    def first_row(i):
-        return pl.ds(pl.multiple_of(low[i] * (edge - BAND), 128), BAND)
-
-    def first_col(flag):
-        return pl.ds(pl.multiple_of(flag * (wide - BAND), 128), BAND)
-
-    plan = []
-    for i in (1, 0):
-        get(spec_hbm.at[:, first_row(i), :], vert_v.at[i, :, :, pl.ds(0, wide)])
-        for q in range(2):
-            get(pup_hbm.at[:, pl.ds(q * 128, 128), :], vert_v.at[i, :, :, pl.ds(wide + q * 2 * W, 2 * W)])
-        plan.append((len(ins), vert_v.at[i], (vert_e, vert_o)[i]))
-    for i in (1, 0):
-        get(spec_hbm.at[:, :, first_col(right[i])], side_v.at[i, :, pl.ds(0, edge), :])
+    for i in range(2):
+        cols = row_start(right[i], wide)
+        for t in range(2):
+            get(spec_hbm.at[:, pl.ds(t * (edge - BAND), BAND), cols], ends_v.at[i, :, pl.ds(t * BAND, BAND), :])
+        plan.append((len(ins), ends_v.at[i], (ends_e, ends_o)[i]))
+    for i in range(2):
+        get(spec_hbm.at[:, pl.ds(BAND, mid), row_start(right[i], wide)], side_v.at[i, :, pl.ds(0, mid), :])
         for q in range(2):
             half = pl.ds(pl.multiple_of(right[i] * W + q * 128, 128), 128)
-            get(pup_hbm.at[:, :, half], side_v.at[i, :, pl.ds(edge + q * W, W), :])
+            get(pup_hbm.at[:, :, half], side_v.at[i, :, pl.ds(mid + q * W, W), :])
         plan.append((len(ins), side_v.at[i], (side_e, side_o)[i]))
-    for j, pair in enumerate(((main_e, main_o), (anti_e, anti_o))):
-        for i in range(2):
-            flag = low[i] if j == 0 else 1 - low[i]
-            get(spec_hbm.at[:, first_row(i), first_col(flag)], diag_v.at[j, i])
-            plan.append((len(ins), diag_v.at[j, i], pair[i]))
+    send(plan, ins, outs, sem_out)
+
+
+def send(plan, ins, outs, sem_out):
     done = 0
     for ready, src, dst in plan:
         while done < ready:
@@ -548,28 +518,69 @@
         copy.wait()
 
 
-def pack(spectrum, pupils):
-    edge, wide = spectrum.shape[1], spectrum.shape[2]
+def pack_sides(spectrum, pupils):
+    edge = spectrum.shape[1]
     hbm = pl.BlockSpec(memory_space=pl.ANY)
-    vert = (2, BAND, wide + 4 * W)
-    side = (2, edge + 2 * W, BAND)
-    diag = (2, BAND, BAND)
+    ends = (2, 2 * BAND, BAND)
+    side = (2, edge - 2 * BAND + 2 * W, BAND)
     return pl.pallas_call(
-        pack_kernel,
-        out_shape=tuple(jax.ShapeDtypeStruct(shape, BF) for shape in (vert, side, side, diag, diag, diag, diag, vert)),
+        sides_kernel,
+        out_shape=tuple(jax.ShapeDtypeStruct(shape, BF) for shape in (ends, ends, side, side)),
         in_specs=[hbm, hbm],
-        out_specs=(hbm,) * 8,
+        out_specs=(hbm,) * 4,
+        scratch_shapes=[
+            pltpu.VMEM((2,) + ends, BF),
+            pltpu.VMEM((2,) + side, BF),
+            pltpu.SemaphoreType.DMA((20,)),
+            pltpu.SemaphoreType.DMA((8,)),
+        ],
+        compiler_params=pltpu.CompilerParams(vmem_limit_bytes=FULL_VMEM),
+        cost_estimate=pl.CostEstimate(flops=1, bytes_accessed=4_000_000, transcendentals=0),
+        name="pack_sides",
+    )(spectrum, pupils)
+
+
+def verts_kernel(spec_hbm, pup_hbm, ends_e, ends_o, vert_e, vert_o, vert_v, sem_in, sem_out):
+    edge, wide = spec_hbm.shape[1], spec_hbm.shape[2]
+    low, right = both_ways("sy"), both_ways("sx")
+    ins, outs, plan = [], [], []
+
+    def get(src, dst):
+        for c in range(2):
+            copy = pltpu.make_async_copy(src.at[c], dst.at[c], sem_in.at[len(ins)])
+            copy.start()
+            ins.append(copy)
+
+    for i in (1, 0):
+        get(spec_hbm.at[:, row_start(low[i], edge), :], vert_v.at[i, :, :, pl.ds(0, wide)])
+        for q in range(2):
+            get(pup_hbm.at[:, pl.ds(q * 128, 128), :], vert_v.at[i, :, :, pl.ds(wide + q * 2 * W, 2 * W)])
+        rows = pl.ds(pl.multiple_of(low[i] * BAND, 128), BAND)
+        for j, src in enumerate((ends_e, ends_o)):
+            cols = pl.ds(pl.multiple_of(wide + 4 * W + right[j] * BAND, 128), BAND)
+            get(src.at[:, rows, :], vert_v.at[i, :, :, cols])
+        plan.append((len(ins), vert_v.at[i], (vert_e, vert_o)[i]))
+    send(plan, ins, outs, sem_out)
+
+
+def pack_verts(spectrum, pupils, ends_e, ends_o):
+    wide = spectrum.shape[2]
+    hbm = pl.BlockSpec(memory_space=pl.ANY)
+    vert = (2, BAND, wide + 4 * W + 2 * BAND)
+    return pl.pallas_call(
+        verts_kernel,
+        out_shape=tuple(jax.ShapeDtypeStruct(vert, BF) for _ in range(2)),
+        in_specs=[hbm] * 4,
+        out_specs=(hbm, hbm),
         scratch_shapes=[
             pltpu.VMEM((2,) + vert, BF),
-            pltpu.VMEM((2,) + side, BF),
-            pltpu.VMEM((2, 2) + diag, BF),
-            pltpu.SemaphoreType.DMA((32,)),
-            pltpu.SemaphoreType.DMA((16,)),
+            pltpu.SemaphoreType.DMA((20,)),
+            pltpu.SemaphoreType.DMA((4,)),
         ],
-        compiler_params=pltpu.CompilerParams(vmem_limit_bytes=PACK_VMEM),
-        cost_estimate=pl.CostEstimate(flops=1, bytes_accessed=11_000_000, transcendentals=0),
-        name="pack",
-    )(spectrum, pupils)
+        compiler_params=pltpu.CompilerParams(vmem_limit_bytes=FULL_VMEM),
+        cost_estimate=pl.CostEstimate(flops=1, bytes_accessed=8_000_000, transcendentals=0),
+        name="pack_verts",
+    )(spectrum, pupils, ends_e, ends_o)
 
 
 def local(spectrum, pupils, amplitudes, crop_starts, led_counts):
@@ -580,27 +591,14 @@
         pairs = [(i, i + 1) for i in range(first, count - 1, 2)]
         return lax.ppermute(value, axis, pairs + [(j, i) for i, j in pairs])
 
-    def swap_diagonal(value, first, step):
-        pairs = [
-            (y * cols + x, (y + 1) * cols + x + step)
-            for y in range(first, rows - 1, 2)
-            for x in range(cols)
-            if 0 <= x + step < cols
-        ]
-        return lax.ppermute(value, ("sy", "sx"), pairs + [(j, i) for i, j in pairs])
-
-    vert_o, side_e, side_o, main_o, anti_o, main_e, anti_e, vert_e = pack(spectrum, pupils)
+    ends_e, ends_o, side_e, side_o = pack_sides(spectrum, pupils)
+    ends = (swap(ends_e, "sx", cols, 0), swap(ends_o, "sx", cols, 1))
+    sides = (swap(side_e, "sx", cols, 0), swap(side_o, "sx", cols, 1))
+    vert_e, vert_o = pack_verts(spectrum, pupils, *ends)
     below = swap(vert_o, "sy", rows, 1)
-    sides = (swap(side_e, "sx", cols, 0), swap(side_o, "sx", cols, 1))
-    diags = (
-        swap_diagonal(main_e, 0, 1),
-        swap_diagonal(main_o, 1, 1),
-        swap_diagonal(anti_e, 0, -1),
-        swap_diagonal(anti_o, 1, -1),
-    )
     verts = (swap(vert_e, "sy", rows, 0), below)
     out, prow, pcol, ppup = compute(spectrum, pupils, amplitudes, crop_starts.reshape(-1), led_counts.reshape(-1))
-    return finish(out, prow, pcol, ppup, verts, sides, diags)
+    return finish(out, prow, pcol, ppup, verts, sides, ends)
 
 
 def solution(mesh):

time: 100 us -> 58.4 us (0.58)
  the two profiles are of different devices: /device:TPU:98 before, /device:TPU:6 now
where the time goes in v4:
time: 58.4 us; the launch traced here: 58.2 us
  Pallas kernels  26.4 us (45%)
  starting transfers between devices  16.9 us (29%)
  waiting for transfers between devices  11.5 us (20%)
  local copies, waits for them, and re-layouts  2.64 us (5%)
  between operations  0.74 us (1%)
    ppermute x6, starting transfers between devices, swap(): return lax.ppermute(value, axis, pairs + [(j, i) for i, j in pairs])  16.9 us
    pallas_call x1, Pallas kernels, compute(): pl.pallas_call(compute_kernel, out_shape=(jax.ShapeDtypeStruct(spectrum.s...  15.8 us
    ppermute x6, waiting for transfers between devices, swap(): return lax.ppermute(value, axis, pairs + [(j, i) for i, j in pairs])  11.5 us
    pallas_call x1, Pallas kernels, finish(): pl.pallas_call(finish_kernel, out_shape=(jax.ShapeDtypeStruct(out.shape,...  3.98 us
    pallas_call x1, Pallas kernels, pack_verts(): pl.pallas_call(verts_kernel, out_shape=tuple((jax.ShapeDtypeStruct(vert,...  3.97 us
    pallas_call x1, Pallas kernels, pack_sides(): pl.pallas_call(sides_kernel, out_shape=tuple((jax.ShapeDtypeStruct(shape,...  2.66 us
    unnamed x11, local copies, waits for them, and re-layouts  1.98 us
  transfers between devices with their start and end apart: 6, of which 2 were waited for; matrix products, arithmetic and copies ran while one was open for 1% of the time, Pallas kernels for 34%

profile of v4, /device:TPU:6, one launch (start us, length us, event | category | flops | bytes accessed | tf_op | source)
XLA Modules:
  0.0 58.2 jit_solution(6562396992555819642)
XLA Ops:
  0.6 0.0 copy-start.4
  0.6 2.7 %pack_sides.1 = (bf16[2,256,128]{2,1,0:T(8,128)(2,1)}, bf16[2,256,128]{2,1,0:T(8,128)(2,1)}, bf16[2,1408,128]{2,1,0:T(8,128)(2,1)}, bf16[2,1408,128]{2,1,0:T(8,128)(2,1)}) custom-call(bf16[2,1152,2304]{2,1,0:T(8,128)(2,1)} %spec_hbm.5, bf16[2,256,512]{2,1,0:T(8,128)(2,1)} %pup_hbm.5), custom_call_target="tpu_custom_call" | custom-call | flops 1 | bytes 4000000 | tf_op jit(solution)/shard_map/pack_sides/pallas_call | solution.py:526
  3.3 2.0 %collective-permute-start = (bf16[2,256,128]{2,1,0:T(8,128)(2,1)}, bf16[2,256,128]{2,1,0:T(8,128)(2,1)S(1)}, u32[]{:S(2)}, u32[]{:S(2)}) collective-permute-start(bf16[2,256,128]{2,1,0:T(8,128)(2,1)} %get-tuple-element.16), channel_id=1, source_target_pairs={{0,1},{2,3},{4,5},{6,7},{1,0},{3,2},{5,4},{7,6},{8,9},{10,11},{12,... | collective-permute-start | bytes 393224 | tf_op jit(solution)/shard_map/ppermute | solution.py:592
  5.3 5.3 %collective-permute-start.1 = (bf16[2,256,128]{2,1,0:T(8,128)(2,1)}, bf16[2,256,128]{2,1,0:T(8,128)(2,1)S(1)}, u32[]{:S(2)}, u32[]{:S(2)}) collective-permute-start(bf16[2,256,128]{2,1,0:T(8,128)(2,1)} %get-tuple-element.17), channel_id=1, source_target_pairs={{1,2},{3,4},{5,6},{2,1},{4,3},{6,5},{9,10},{11,12},{13,14},{10,9},... | collective-permute-start | bytes 393224 | tf_op jit(solution)/shard_map/ppermute | solution.py:592
  10.6 0.3 collective-permute-start.4
  10.8 4.0 %collective-permute-start.5 = (bf16[2,1408,128]{2,1,0:T(8,128)(2,1)}, bf16[2,1408,128]{2,1,0:T(8,128)(2,1)}, u32[]{:S(2)}, u32[]{:S(2)}) collective-permute-start(bf16[2,1408,128]{2,1,0:T(8,128)(2,1)} %get-tuple-element.21), channel_id=1, source_target_pairs={{1,2},{3,4},{5,6},{2,1},{4,3},{6,5},{9,10},{11,12},{13,14},{10,9},... | collective-permute-start | bytes 2162696 | tf_op jit(solution)/shard_map/ppermute | solution.py:592
  14.9 0.0 copy-done.4
  14.9 0.1 copy.11
  15.0 0.7 %reshape.10.starts = s32[16]{0:T(128)} reshape(s32[1,2,4,2]{3,2,1,0:T(4,128)S(1)} %copy.11) | data formatting | bytes 128 | tf_op jit(solution)/shard_map/reshape | solution.py:600
  15.6 0.0 collective-permute-done.ends_e.endse_hbm
  15.6 0.3 collective-permute-done.1.ends_o.endso_hbm
  16.0 0.3 copy-done
  16.3 0.6 %copy-done.2 = bf16[2,256,128]{2,1,0:T(8,128)(2,1)} copy-done((bf16[2,256,128]{2,1,0:T(8,128)(2,1)}, bf16[2,256,128]{2,1,0:T(8,128)(2,1)S(1)}, u32[]{:S(2)}) %copy-start.2) | copy-done | bytes 131096
  16.9 4.0 %pack_verts.1 = (bf16[2,128,3584]{2,1,0:T(8,128)(2,1)}, bf16[2,128,3584]{2,1,0:T(8,128)(2,1)}) custom-call(bf16[2,1152,2304]{2,1,0:T(8,128)(2,1)} %spec_hbm.5, bf16[2,256,512]{2,1,0:T(8,128)(2,1)} %pup_hbm.5, bf16[2,256,128]{2,1,0:T(8,128)(2,1)} %copy-done, bf16[2,256,128]{2,1,0:T(8,128)(2,1)} %copy-done.2), custom_call_target="tpu_custom_call" | custom-call | flops 1 | bytes 8000000 | tf_op jit(solution)/shard_map/pack_verts/pallas_call | solution.py:570
  20.9 0.1 collective-permute-start.2
  21.0 5.3 %collective-permute-start.3 = (bf16[2,128,3584]{2,1,0:T(8,128)(2,1)}, bf16[2,128,3584]{2,1,0:T(8,128)(2,1)S(1)}, u32[]{:S(2)}, u32[]{:S(2)}) collective-permute-start(bf16[2,128,3584]{2,1,0:T(8,128)(2,1)} %get-tuple-element.19), channel_id=1, source_target_pairs={{8,16},{24,32},{40,48},{56,64},{72,80},{88,96},{104,112},{16,8},{3... | collective-permute-start | bytes 5505032 | tf_op jit(solution)/shard_map/ppermute | solution.py:592
  26.3 0.0 copy-start.1
  26.3 15.8 %data_terms.1 = (bf16[2,1152,2304]{2,1,0:T(8,128)(2,1)}, f32[2,2,18,128,128]{4,3,2,1,0:T(8,128)S(1)}, f32[2,2,896,128]{3,2,1,0:T(8,128)S(1)}, f32[2,256,512]{2,1,0:T(8,128)S(1)}) custom-call(s32[16]{0:T(128)} %reshape.10.starts, s32[2]{0:T(128)} %bitcast.1, bf16[2,1152,2304]{2,1,0:T(8,128)(2,1)} %spec_hbm.5, bf16[2,256,512]{2,1,0:T(8,128)(2,1)} %pup_hbm.5, ...), custom_call_target="tpu_custom_call" | custom-call | flops 20000000000 | bytes 30000000 | tf_op jit(solution)/shard_map/data_terms/pallas_call | solution.py:330
  42.1 0.0 collective-permute-done.4.sidee_hbm
  42.1 0.0 collective-permute-done.5.sideo_hbm
  42.2 0.0 collective-permute-done.2.verte_hbm
  42.2 11.1 %collective-permute-done.3.verto_hbm = bf16[2,128,3584]{2,1,0:T(8,128)(2,1)S(1)} collective-permute-done((bf16[2,128,3584]{2,1,0:T(8,128)(2,1)}, bf16[2,128,3584]{2,1,0:T(8,128)(2,1)S(1)}, u32[]{:S(2)}, u32[]{:S(2)}) %collective-permute-start.3) | collective-permute-done | bytes 1835040 | tf_op jit(solution)/shard_map/ppermute | solution.py:592
  53.3 0.9 %copy-done.3 = bf16[2,256,128]{2,1,0:T(8,128)(2,1)S(1)} copy-done((bf16[2,256,128]{2,1,0:T(8,128)(2,1)S(1)}, bf16[2,256,128]{2,1,0:T(8,128)(2,1)}, u32[]{:S(2)}) %copy-start.3) | copy-done | bytes 131096
  54.2 4.0 %shared_bands.1 = (bf16[2,1152,2304]{2,1,0:T(8,128)(2,1)}, f32[2,256,512]{2,1,0:T(8,128)}) custom-call(bf16[2,1152,2304]{2,1,0:T(8,128)(2,1)} %get-tuple-element.12.out_in, f32[2,2,18,128,128]{4,3,2,1,0:T(8,128)S(1)} %get-tuple-element.13.prow, f32[2,2,896,128]{3,2,1,0:T(8,128)S(1)} %get-tuple-element.14.pcol, ...), custom_call_target="tpu_custom_call", output_to_operand_aliasing={{0}: (0, {})} | custom-call | flops 10000000 | bytes 17000000 | tf_op jit(solution)/shard_map/shared_bands/pallas_call | solution.py:443
  (4 shorter events, 0.0 us)
Async XLA Ops:
  0.6 14.2 %copy-start.4 = (s32[1,2,4,2]{2,3,1,0:T(2,128)S(1)}, s32[1,2,4,2]{2,3,1,0:T(2,128)}, u32[]{:S(2)}) copy-start(s32[1,2,4,2]{2,3,1,0:T(2,128)} %param.10) | copy-start | bytes 196
  3.3 12.3 %collective-permute-start = (bf16[2,256,128]{2,1,0:T(8,128)(2,1)}, bf16[2,256,128]{2,1,0:T(8,128)(2,1)S(1)}, u32[]{:S(2)}, u32[]{:S(2)}) collective-permute-start(bf16[2,256,128]{2,1,0:T(8,128)(2,1)} %get-tuple-element.16), channel_id=1, source_target_pairs={{0,1},{2,3},{4,5},{6,7},{1,0},{3,2},{5,4},{7,6},{8,9},{10,11},{12,... | collective-permute-start | bytes 393224 | tf_op jit(solution)/shard_map/ppermute | solution.py:592
  5.3 10.7 %collective-permute-start.1 = (bf16[2,256,128]{2,1,0:T(8,128)(2,1)}, bf16[2,256,128]{2,1,0:T(8,128)(2,1)S(1)}, u32[]{:S(2)}, u32[]{:S(2)}) collective-permute-start(bf16[2,256,128]{2,1,0:T(8,128)(2,1)} %get-tuple-element.17), channel_id=1, source_target_pairs={{1,2},{3,4},{5,6},{2,1},{4,3},{6,5},{9,10},{11,12},{13,14},{10,9},... | collective-permute-start | bytes 393224 | tf_op jit(solution)/shard_map/ppermute | solution.py:592
  10.6 31.6 %collective-permute-start.4 = (bf16[2,1408,128]{2,1,0:T(8,128)(2,1)}, bf16[2,1408,128]{2,1,0:T(8,128)(2,1)}, u32[]{:S(2)}, u32[]{:S(2)}) collective-permute-start(bf16[2,1408,128]{2,1,0:T(8,128)(2,1)} %get-tuple-element.20), channel_id=1, source_target_pairs={{0,1},{2,3},{4,5},{6,7},{1,0},{3,2},{5,4},{7,6},{8,9},{10,11},{12,... | collective-permute-start | bytes 2162696 | tf_op jit(solution)/shard_map/ppermute | solution.py:592
  10.8 31.3 %collective-permute-start.5 = (bf16[2,1408,128]{2,1,0:T(8,128)(2,1)}, bf16[2,1408,128]{2,1,0:T(8,128)(2,1)}, u32[]{:S(2)}, u32[]{:S(2)}) collective-permute-start(bf16[2,1408,128]{2,1,0:T(8,128)(2,1)} %get-tuple-element.21), channel_id=1, source_target_pairs={{1,2},{3,4},{5,6},{2,1},{4,3},{6,5},{9,10},{11,12},{13,14},{10,9},... | collective-permute-start | bytes 2162696 | tf_op jit(solution)/shard_map/ppermute | solution.py:592
  15.6 0.7 %copy-start = (bf16[2,256,128]{2,1,0:T(8,128)(2,1)}, bf16[2,256,128]{2,1,0:T(8,128)(2,1)S(1)}, u32[]{:S(2)}) copy-start(bf16[2,256,128]{2,1,0:T(8,128)(2,1)S(1)} %collective-permute-done.ends_e.endse_hbm) | copy-start | bytes 393220
  16.3 0.6 %copy-start.2 = (bf16[2,256,128]{2,1,0:T(8,128)(2,1)}, bf16[2,256,128]{2,1,0:T(8,128)(2,1)S(1)}, u32[]{:S(2)}) copy-start(bf16[2,256,128]{2,1,0:T(8,128)(2,1)S(1)} %collective-permute-done.1.ends_o.endso_hbm) | copy-start | bytes 393220
  20.9 21.2 %collective-permute-start.2 = (bf16[2,128,3584]{2,1,0:T(8,128)(2,1)}, bf16[2,128,3584]{2,1,0:T(8,128)(2,1)S(1)}, u32[]{:S(2)}, u32[]{:S(2)}) collective-permute-start(bf16[2,128,3584]{2,1,0:T(8,128)(2,1)} %get-tuple-element.18), channel_id=1, source_target_pairs={{0,8},{16,24},{32,40},{48,56},{64,72},{80,88},{96,104},{112,120},{... | collective-permute-start | bytes 5505032 | tf_op jit(solution)/shard_map/ppermute | solution.py:592
  21.0 32.3 %collective-permute-start.3 = (bf16[2,128,3584]{2,1,0:T(8,128)(2,1)}, bf16[2,128,3584]{2,1,0:T(8,128)(2,1)S(1)}, u32[]{:S(2)}, u32[]{:S(2)}) collective-permute-start(bf16[2,128,3584]{2,1,0:T(8,128)(2,1)} %get-tuple-element.19), channel_id=1, source_target_pairs={{8,16},{24,32},{40,48},{56,64},{72,80},{88,96},{104,112},{16,8},{3... | collective-permute-start | bytes 5505032 | tf_op jit(solution)/shard_map/ppermute | solution.py:592
  26.3 27.0 %copy-start.1 = (bf16[2,256,128]{2,1,0:T(8,128)(2,1)S(1)}, bf16[2,256,128]{2,1,0:T(8,128)(2,1)}, u32[]{:S(2)}) copy-start(bf16[2,256,128]{2,1,0:T(8,128)(2,1)} %copy-done) | copy-start | bytes 393220
  53.3 0.9 %copy-start.3 = (bf16[2,256,128]{2,1,0:T(8,128)(2,1)S(1)}, bf16[2,256,128]{2,1,0:T(8,128)(2,1)}, u32[]{:S(2)}) copy-start(bf16[2,256,128]{2,1,0:T(8,128)(2,1)} %copy-done.2) | copy-start | bytes 393220

commit v5 on v4

--- a/solution.py
+++ b/solution.py
@@ -18,7 +18,8 @@
 COST_FLOPS = 20_000_000_000
 COST_BYTES = 30_000_000
 FULL_VMEM = 60 * 1024 * 1024
-DATA_VMEM = 53 * 1024 * 1024
+VERT_VMEM = 48 * 1024 * 1024
+DATA_VMEM = 50 * 1024 * 1024
 FINISH_VMEM = 24 * 1024 * 1024
 BAND = 2 * H
 BF = jnp.bfloat16
@@ -123,8 +124,8 @@
     lane = lax.broadcasted_iota(jnp.int32, (16, 128), 1)
 
     def slot_stages(g, slot):
-        a = starts[(g * MAXL + slot) * 2]
-        b = starts[(g * MAXL + slot) * 2 + 1]
+        a = starts[0, g, slot, 0]
+        b = starts[0, g, slot, 1]
         a0 = pl.multiple_of(jnp.minimum(a // 16 * 16, edge - W - 16), 16)
         off = a - a0
         k0 = jnp.minimum(b // 128, tiles - 3)
@@ -260,10 +261,10 @@
 
         return step
 
-    both = jnp.minimum(counts[0], counts[1])
+    both = jnp.minimum(counts[0, 0], counts[0, 1])
     lax.fori_loop(0, both, run((0, 1)), 0)
     for g in range(2):
-        lax.fori_loop(both, counts[g], run((g,)), 0)
+        lax.fori_loop(both, counts[0, g], run((g,)), 0)
     for c in range(2):
 
         def finish(i, carry, c=c):
@@ -365,7 +366,7 @@
 
 
 def finish_kernel(
-    out_in, prow, pcol, ppup, verte_hbm, verto_hbm, sidee_hbm, sideo_hbm, endse_hbm, endso_hbm,
+    out_in, prow, pcol, ppup, verto_hbm, verte_hbm, sidee_hbm, sideo_hbm, endse_hbm, endso_hbm,
     out_hbm, pup_hbm,
     vert, side, ends, rows_out, cols_out, pup_out, sem_in, sem_out,
 ):
@@ -462,7 +463,7 @@
         compiler_params=pltpu.CompilerParams(vmem_limit_bytes=FINISH_VMEM),
         cost_estimate=pl.CostEstimate(flops=10_000_000, bytes_accessed=17_000_000, transcendentals=0),
         name="shared_bands",
-    )(out, prow, pcol, ppup, *verts, *sides, *ends)
+    )(out, prow, pcol, ppup, verts[1], verts[0], *sides, *ends)
 
 
 def parity_of(axis):
@@ -540,10 +541,10 @@
     )(spectrum, pupils)
 
 
-def verts_kernel(spec_hbm, pup_hbm, ends_e, ends_o, vert_e, vert_o, vert_v, sem_in, sem_out):
+def vert_kernel(odd_pairs, spec_hbm, pup_hbm, ends_e, ends_o, vert, vert_v, sem_in, sem_out):
     edge, wide = spec_hbm.shape[1], spec_hbm.shape[2]
-    low, right = both_ways("sy"), both_ways("sx")
-    ins, outs, plan = [], [], []
+    low, right = both_ways("sy")[odd_pairs], both_ways("sx")
+    ins, outs = [], []
 
     def get(src, dst):
         for c in range(2):
@@ -551,35 +552,33 @@
             copy.start()
             ins.append(copy)
 
-    for i in (1, 0):
-        get(spec_hbm.at[:, row_start(low[i], edge), :], vert_v.at[i, :, :, pl.ds(0, wide)])
-        for q in range(2):
-            get(pup_hbm.at[:, pl.ds(q * 128, 128), :], vert_v.at[i, :, :, pl.ds(wide + q * 2 * W, 2 * W)])
-        rows = pl.ds(pl.multiple_of(low[i] * BAND, 128), BAND)
-        for j, src in enumerate((ends_e, ends_o)):
-            cols = pl.ds(pl.multiple_of(wide + 4 * W + right[j] * BAND, 128), BAND)
-            get(src.at[:, rows, :], vert_v.at[i, :, :, cols])
-        plan.append((len(ins), vert_v.at[i], (vert_e, vert_o)[i]))
-    send(plan, ins, outs, sem_out)
-
-
-def pack_verts(spectrum, pupils, ends_e, ends_o):
+    get(spec_hbm.at[:, row_start(low, edge), :], vert_v.at[:, :, pl.ds(0, wide)])
+    for q in range(2):
+        get(pup_hbm.at[:, pl.ds(q * 128, 128), :], vert_v.at[:, :, pl.ds(wide + q * 2 * W, 2 * W)])
+    rows = pl.ds(pl.multiple_of(low * BAND, 128), BAND)
+    for j, src in enumerate((ends_e, ends_o)):
+        cols = pl.ds(pl.multiple_of(wide + 4 * W + right[j] * BAND, 128), BAND)
+        get(src.at[:, rows, :], vert_v.at[:, :, cols])
+    send([(len(ins), vert_v, vert)], ins, outs, sem_out)
+
+
+def pack_vert(odd_pairs, spectrum, pupils, ends_e, ends_o):
     wide = spectrum.shape[2]
     hbm = pl.BlockSpec(memory_space=pl.ANY)
     vert = (2, BAND, wide + 4 * W + 2 * BAND)
     return pl.pallas_call(
-        verts_kernel,
-        out_shape=tuple(jax.ShapeDtypeStruct(vert, BF) for _ in range(2)),
+        functools.partial(vert_kernel, odd_pairs),
+        out_shape=jax.ShapeDtypeStruct(vert, BF),
         in_specs=[hbm] * 4,
-        out_specs=(hbm, hbm),
+        out_specs=hbm,
         scratch_shapes=[
-            pltpu.VMEM((2,) + vert, BF),
-            pltpu.SemaphoreType.DMA((20,)),
-            pltpu.SemaphoreType.DMA((4,)),
+            pltpu.VMEM(vert, BF),
+            pltpu.SemaphoreType.DMA((10,)),
+            pltpu.SemaphoreType.DMA((2,)),
         ],
-        compiler_params=pltpu.CompilerParams(vmem_limit_bytes=FULL_VMEM),
-        cost_estimate=pl.CostEstimate(flops=1, bytes_accessed=8_000_000, transcendentals=0),
-        name="pack_verts",
+        compiler_params=pltpu.CompilerParams(vmem_limit_bytes=VERT_VMEM),
+        cost_estimate=pl.CostEstimate(flops=1, bytes_accessed=4_000_000, transcendentals=0),
+        name="pack_odd" if odd_pairs else "pack_even",
     )(spectrum, pupils, ends_e, ends_o)
 
 
@@ -594,10 +593,9 @@
     ends_e, ends_o, side_e, side_o = pack_sides(spectrum, pupils)
     ends = (swap(ends_e, "sx", cols, 0), swap(ends_o, "sx", cols, 1))
     sides = (swap(side_e, "sx", cols, 0), swap(side_o, "sx", cols, 1))
-    vert_e, vert_o = pack_verts(spectrum, pupils, *ends)
-    below = swap(vert_o, "sy", rows, 1)
-    verts = (swap(vert_e, "sy", rows, 0), below)
-    out, prow, pcol, ppup = compute(spectrum, pupils, amplitudes, crop_starts.reshape(-1), led_counts.reshape(-1))
+    odd = swap(pack_vert(1, spectrum, pupils, *ends), "sy", rows, 1)
+    verts = (swap(pack_vert(0, spectrum, pupils, *ends), "sy", rows, 0), odd)
+    out, prow, pcol, ppup = compute(spectrum, pupils, amplitudes, crop_starts, led_counts)
     return finish(out, prow, pcol, ppup, verts, sides, ends)
 
 

time: 58.4 us -> 57.8 us (0.990)
  waiting for transfers between devices: 11.5 us -> 15.9 us
  local copies, waits for them, and re-layouts: 2.64 us -> 0.7 us
  starting transfers between devices: 16.9 us -> 15.2 us
  Pallas kernels: 26.4 us -> 25 us
    ppermute x6, waiting for transfers between devices: 11.5 us -> 15.9 us  [swap(): return lax.ppermute(value, axis, pairs + [(j, i) for i, j in pairs])]
    pallas_call x1, Pallas kernels: 15.8 us -> 13.7 us  [compute(): pl.pallas_call(compute_kernel, out_shape=(jax.ShapeDtypeStruct(spectrum.s...]
    ppermute x6, starting transfers between devices: 16.9 us -> 15.2 us  [swap(): return lax.ppermute(value, axis, pairs + [(j, i) for i, j in pairs])]
    unnamed x11 -> x5, local copies, waits for them, and re-layouts: 1.98 us -> 0.7 us
    reshape x1 -> x0, local copies, waits for them, and re-layouts: 0.66 us -> none  [local(): crop_starts.reshape(-1)]
    pallas_call x1 -> x2, Pallas kernels: 3.97 us -> 4.43 us  [pack_vert(): pl.pallas_call(functools.partial(vert_kernel, odd_pairs), out_shape=jax.S...]
  transfers between devices with their start and end apart: 6 -> 6, of which waited for: 2 -> 2; matrix products, arithmetic and copies ran while one was open for 1% -> 1% of each run, Pallas kernels for 34% -> 32%
where the time goes in v5:
time: 57.8 us; the launch traced here: 57.5 us
  Pallas kernels  25 us (43%)
  waiting for transfers between devices  15.9 us (28%)
  starting transfers between devices  15.2 us (26%)
  between operations  0.73 us (1%)
  local copies, waits for them, and re-layouts  0.7 us (1%)
    ppermute x6, waiting for transfers between devices, swap(): return lax.ppermute(value, axis, pairs + [(j, i) for i, j in pairs])  15.9 us
    ppermute x6, starting transfers between devices, swap(): return lax.ppermute(value, axis, pairs + [(j, i) for i, j in pairs])  15.2 us
    pallas_call x1, Pallas kernels, compute(): pl.pallas_call(compute_kernel, out_shape=(jax.ShapeDtypeStruct(spectrum.s...  13.7 us
    pallas_call x2, Pallas kernels, pack_vert(): pl.pallas_call(functools.partial(vert_kernel, odd_pairs), out_shape=jax.S...  4.43 us
    pallas_call x1, Pallas kernels, finish(): pl.pallas_call(finish_kernel, out_shape=(jax.ShapeDtypeStruct(out.shape,...  4.17 us
    pallas_call x1, Pallas kernels, pack_sides(): pl.pallas_call(sides_kernel, out_shape=tuple((jax.ShapeDtypeStruct(shape,...  2.71 us
  transfers between devices with their start and end apart: 6, of which 2 were waited for; matrix products, arithmetic and copies ran while one was open for 1% of the time, Pallas kernels for 32%

profile of v5, /device:TPU:6, one launch (start us, length us, event | category | flops | bytes accessed | tf_op | source)
XLA Modules:
  0.0 57.5 jit_solution(15389085415969678893)
XLA Ops:
  0.6 0.0 copy-start
  0.6 0.0 copy-start.1
  0.7 2.7 %pack_sides.1 = (bf16[2,256,128]{2,1,0:T(8,128)(2,1)}, bf16[2,256,128]{2,1,0:T(8,128)(2,1)}, bf16[2,1408,128]{2,1,0:T(8,128)(2,1)}, bf16[2,1408,128]{2,1,0:T(8,128)(2,1)}) custom-call(bf16[2,1152,2304]{2,1,0:T(8,128)(2,1)} %spec_hbm.7, bf16[2,256,512]{2,1,0:T(8,128)(2,1)} %pup_hbm.7), custom_call_target="tpu_custom_call" | custom-call | flops 1 | bytes 4000000 | tf_op jit(solution)/shard_map/pack_sides/pallas_call | solution.py:527
  3.4 2.0 %collective-permute-start = (bf16[2,256,128]{2,1,0:T(8,128)(2,1)}, bf16[2,256,128]{2,1,0:T(8,128)(2,1)S(1)}, u32[]{:S(2)}, u32[]{:S(2)}) collective-permute-start(bf16[2,256,128]{2,1,0:T(8,128)(2,1)} %get-tuple-element.14), channel_id=1, source_target_pairs={{0,1},{2,3},{4,5},{6,7},{1,0},{3,2},{5,4},{7,6},{8,9},{10,11},{12,... | collective-permute-start | bytes 393224 | tf_op jit(solution)/shard_map/ppermute | solution.py:591
  5.4 5.3 %collective-permute-start.1 = (bf16[2,256,128]{2,1,0:T(8,128)(2,1)}, bf16[2,256,128]{2,1,0:T(8,128)(2,1)S(1)}, u32[]{:S(2)}, u32[]{:S(2)}) collective-permute-start(bf16[2,256,128]{2,1,0:T(8,128)(2,1)} %get-tuple-element.15), channel_id=1, source_target_pairs={{1,2},{3,4},{5,6},{2,1},{4,3},{6,5},{9,10},{11,12},{13,14},{10,9},... | collective-permute-start | bytes 393224 | tf_op jit(solution)/shard_map/ppermute | solution.py:591
  10.6 0.3 collective-permute-start.4
  10.9 4.0 %collective-permute-start.5 = (bf16[2,1408,128]{2,1,0:T(8,128)(2,1)}, bf16[2,1408,128]{2,1,0:T(8,128)(2,1)}, u32[]{:S(2)}, u32[]{:S(2)}) collective-permute-start(bf16[2,1408,128]{2,1,0:T(8,128)(2,1)} %get-tuple-element.17), channel_id=1, source_target_pairs={{1,2},{3,4},{5,6},{2,1},{4,3},{6,5},{9,10},{11,12},{13,14},{10,9},... | collective-permute-start | bytes 2162696 | tf_op jit(solution)/shard_map/ppermute | solution.py:591
  14.9 0.0 copy-done.1
  14.9 0.7 %copy.10.starts = s32[1,2,4,2]{3,2,1,0:T(4,128)} copy(s32[1,2,4,2]{2,3,1,0:T(2,128)S(1)} %copy-done.1) | data formatting | bytes 128 | tf_op args[3]
  15.6 0.0 collective-permute-done.ends_e.endse_hbm
  15.6 0.4 collective-permute-done.1.ends_o.endso_hbm
  16.0 0.0 copy-done
  16.0 1.8 %pack_odd.1 = bf16[2,128,3584]{2,1,0:T(8,128)(2,1)S(1)} custom-call(bf16[2,1152,2304]{2,1,0:T(8,128)(2,1)} %spec_hbm.7, bf16[2,256,512]{2,1,0:T(8,128)(2,1)S(1)} %copy-done, bf16[2,256,128]{2,1,0:T(8,128)(2,1)S(1)} %collective-permute-done.ends_e.endse_hbm, bf16[2,256,128]{2,1,0:T(8,128)(2,1)S(1)} %collective-permute-done.1.ends_o.endso_hbm), custom_call_target="tpu_custom_call" | custom-call | flops 1 | bytes 4000000 | tf_op jit(solution)/shard_map/pack_odd/pallas_call | solution.py:569
  17.9 3.4 %collective-permute-start.2 = (bf16[2,128,3584]{2,1,0:T(8,128)(2,1)S(1)}, bf16[2,128,3584]{2,1,0:T(8,128)(2,1)S(1)}, u32[]{:S(2)}, u32[]{:S(2)}) collective-permute-start(bf16[2,128,3584]{2,1,0:T(8,128)(2,1)S(1)} %pack_odd.1), channel_id=1, source_target_pairs={{8,16},{24,32},{40,48},{56,64},{72,80},{88,96},{104,112},{16,8},{3... | collective-permute-start | bytes 5505032 | tf_op jit(solution)/shard_map/ppermute | solution.py:591
  21.2 2.6 %pack_even.1 = bf16[2,128,3584]{2,1,0:T(8,128)(2,1)} custom-call(bf16[2,1152,2304]{2,1,0:T(8,128)(2,1)} %spec_hbm.7, bf16[2,256,512]{2,1,0:T(8,128)(2,1)S(1)} %copy-done, bf16[2,256,128]{2,1,0:T(8,128)(2,1)S(1)} %collective-permute-done.ends_e.endse_hbm, bf16[2,256,128]{2,1,0:T(8,128)(2,1)S(1)} %collective-permute-done.1.ends_o.endso_hbm), custom_call_target="tpu_custom_call" | custom-call | flops 1 | bytes 4000000 | tf_op jit(solution)/shard_map/pack_even/pallas_call | solution.py:569
  23.9 0.3 collective-permute-start.3
  24.2 13.7 %data_terms.1 = (bf16[2,1152,2304]{2,1,0:T(8,128)(2,1)}, f32[2,2,18,128,128]{4,3,2,1,0:T(8,128)S(1)}, f32[2,2,896,128]{3,2,1,0:T(8,128)S(1)}, f32[2,256,512]{2,1,0:T(8,128)S(1)}) custom-call(s32[1,2,4,2]{3,2,1,0:T(4,128)} %copy.10.starts, s32[1,2]{1,0:T(1,128)} %counts.1, bf16[2,1152,2304]{2,1,0:T(8,128)(2,1)} %spec_hbm.7, bf16[2,256,512]{2,1,0:T(8,128)(2,1)} %pup_hbm.7, ...), custom_call_target="tpu_custom_call" | custom-call | flops 20000000000 | bytes 30000000 | tf_op jit(solution)/shard_map/data_terms/pallas_call | solution.py:331
  37.9 0.0 collective-permute-done.4.sidee_hbm
  37.9 0.0 collective-permute-done.5.sideo_hbm
  37.9 15.4 %collective-permute-done.2.verto_hbm = bf16[2,128,3584]{2,1,0:T(8,128)(2,1)S(1)} collective-permute-done((bf16[2,128,3584]{2,1,0:T(8,128)(2,1)S(1)}, bf16[2,128,3584]{2,1,0:T(8,128)(2,1)S(1)}, u32[]{:S(2)}, u32[]{:S(2)}) %collective-permute-start.2) | collective-permute-done | bytes 1835040 | tf_op jit(solution)/shard_map/ppermute | solution.py:591
  53.3 0.0 collective-permute-done.3.verte_hbm
  53.3 4.2 %shared_bands.1 = (bf16[2,1152,2304]{2,1,0:T(8,128)(2,1)}, f32[2,256,512]{2,1,0:T(8,128)}) custom-call(bf16[2,1152,2304]{2,1,0:T(8,128)(2,1)} %get-tuple-element.10.out_in, f32[2,2,18,128,128]{4,3,2,1,0:T(8,128)S(1)} %get-tuple-element.11.prow, f32[2,2,896,128]{3,2,1,0:T(8,128)S(1)} %get-tuple-element.12.pcol, ...), custom_call_target="tpu_custom_call", output_to_operand_aliasing={{0}: (0, {})} | custom-call | flops 10000000 | bytes 17000000 | tf_op jit(solution)/shard_map/shared_bands/pallas_call | solution.py:444
Async XLA Ops:
  0.6 15.4 %copy-start = (bf16[2,256,512]{2,1,0:T(8,128)(2,1)S(1)}, bf16[2,256,512]{2,1,0:T(8,128)(2,1)}, u32[]{:S(2)}) copy-start(bf16[2,256,512]{2,1,0:T(8,128)(2,1)} %pup_hbm.7) | copy-start | bytes 1572868
  0.6 14.3 %copy-start.1 = (s32[1,2,4,2]{2,3,1,0:T(2,128)S(1)}, s32[1,2,4,2]{2,3,1,0:T(2,128)}, u32[]{:S(2)}) copy-start(s32[1,2,4,2]{2,3,1,0:T(2,128)} %param.10) | copy-start | bytes 196
  3.4 12.2 %collective-permute-start = (bf16[2,256,128]{2,1,0:T(8,128)(2,1)}, bf16[2,256,128]{2,1,0:T(8,128)(2,1)S(1)}, u32[]{:S(2)}, u32[]{:S(2)}) collective-permute-start(bf16[2,256,128]{2,1,0:T(8,128)(2,1)} %get-tuple-element.14), channel_id=1, source_target_pairs={{0,1},{2,3},{4,5},{6,7},{1,0},{3,2},{5,4},{7,6},{8,9},{10,11},{12,... | collective-permute-start | bytes 393224 | tf_op jit(solution)/shard_map/ppermute | solution.py:591
  5.4 10.7 %collective-permute-start.1 = (bf16[2,256,128]{2,1,0:T(8,128)(2,1)}, bf16[2,256,128]{2,1,0:T(8,128)(2,1)S(1)}, u32[]{:S(2)}, u32[]{:S(2)}) collective-permute-start(bf16[2,256,128]{2,1,0:T(8,128)(2,1)} %get-tuple-element.15), channel_id=1, source_target_pairs={{1,2},{3,4},{5,6},{2,1},{4,3},{6,5},{9,10},{11,12},{13,14},{10,9},... | collective-permute-start | bytes 393224 | tf_op jit(solution)/shard_map/ppermute | solution.py:591
  10.6 27.3 %collective-permute-start.4 = (bf16[2,1408,128]{2,1,0:T(8,128)(2,1)}, bf16[2,1408,128]{2,1,0:T(8,128)(2,1)S(1)}, u32[]{:S(2)}, u32[]{:S(2)}) collective-permute-start(bf16[2,1408,128]{2,1,0:T(8,128)(2,1)} %get-tuple-element.16), channel_id=1, source_target_pairs={{0,1},{2,3},{4,5},{6,7},{1,0},{3,2},{5,4},{7,6},{8,9},{10,11},{12,... | collective-permute-start | bytes 2162696 | tf_op jit(solution)/shard_map/ppermute | solution.py:591
  10.9 27.0 %collective-permute-start.5 = (bf16[2,1408,128]{2,1,0:T(8,128)(2,1)}, bf16[2,1408,128]{2,1,0:T(8,128)(2,1)}, u32[]{:S(2)}, u32[]{:S(2)}) collective-permute-start(bf16[2,1408,128]{2,1,0:T(8,128)(2,1)} %get-tuple-element.17), channel_id=1, source_target_pairs={{1,2},{3,4},{5,6},{2,1},{4,3},{6,5},{9,10},{11,12},{13,14},{10,9},... | collective-permute-start | bytes 2162696 | tf_op jit(solution)/shard_map/ppermute | solution.py:591
  17.9 35.5 %collective-permute-start.2 = (bf16[2,128,3584]{2,1,0:T(8,128)(2,1)S(1)}, bf16[2,128,3584]{2,1,0:T(8,128)(2,1)S(1)}, u32[]{:S(2)}, u32[]{:S(2)}) collective-permute-start(bf16[2,128,3584]{2,1,0:T(8,128)(2,1)S(1)} %pack_odd.1), channel_id=1, source_target_pairs={{8,16},{24,32},{40,48},{56,64},{72,80},{88,96},{104,112},{16,8},{3... | collective-permute-start | bytes 5505032 | tf_op jit(solution)/shard_map/ppermute | solution.py:591
  23.9 29.5 %collective-permute-start.3 = (bf16[2,128,3584]{2,1,0:T(8,128)(2,1)}, bf16[2,128,3584]{2,1,0:T(8,128)(2,1)S(1)}, u32[]{:S(2)}, u32[]{:S(2)}) collective-permute-start(bf16[2,128,3584]{2,1,0:T(8,128)(2,1)} %pack_even.1), channel_id=1, source_target_pairs={{0,8},{16,24},{32,40},{48,56},{64,72},{80,88},{96,104},{112,120},{... | collective-permute-start | bytes 5505032 | tf_op jit(solution)/shard_map/ppermute | solution.py:591
